TPU v7x, 256 devices: a whole 4x4x8 slice. The times are simulated.
256 devices in a mesh: seq: 32 (over z, y), head: 8 (over x, core).
Axes of the slice: x: 4, y: 4, z: 8, core: 2. Of those that a mesh axis runs over, the one named last changes fastest.
Arguments:
- queries: bfloat16 [16384, 32, 128], P('seq', 'head'), may hold values from -6 to 6
- key_matrix: bfloat16 [16384, 32, 128], P('seq', 'head'), may hold values from -6 to 6
- value_matrix: bfloat16 [16384, 32, 128], P('seq', 'head'), may hold values from -6 to 6
- level_weight: float32 [15, 32, 16384], P(None, 'head', 'seq'), may hold values from 0.25 to 4
- out_weight: bfloat16 [32, 128, 4096], P('head'), may hold values from -0.09375 to 0.09375
- grad_out: bfloat16 [16384, 4096], P('seq', 'head'), may hold values from -4 to 4
Outputs:
- mixed_out: bfloat16 [16384, 4096], P('seq', 'head')
- grad_queries: bfloat16 [16384, 32, 128], P('seq', 'head')
- grad_keys: bfloat16 [16384, 32, 128], P('seq', 'head')
- grad_values: bfloat16 [16384, 32, 128], P('seq', 'head')
- grad_levels: float32 [15, 32, 16384], P(None, 'head', 'seq')
All inputs are finite; a program needn't handle non-finite values.
Results may differ from a plain program's by a relative error of at most 0.017.
Values may be sent and summed in bfloat16 or wider, within the bound.
No kernel may reach another device: no remote copies, remote signals or barrier semaphores. Data moves between devices by JAX's collectives and lax.ppermute only.
A program may use at most 128 MiB of HBM per device.

v0:
```python
import jax
import jax.numpy as jnp
from jax import lax
from jax.sharding import PartitionSpec as P


def partner_2(block, axis, distance):
    count = lax.axis_size(axis)
    route = []
    for low in range(count):
        high = low | 1 << distance
        if high != low and high < count:
            route += [(low, high), (high, low)]
    return lax.ppermute(block, axis, route)


def in_blocks(array, dim, devices):
    before, after = (array.shape[:dim], array.shape[dim + 1 :])
    return jnp.moveaxis(array.reshape(*before, devices, -1, *after), dim, 0)


def summed_on_arrival(array, axis, dim):
    parts = in_blocks(array, dim, lax.axis_size(axis))
    arrived = lax.all_to_all(parts, axis, split_axis=0, concat_axis=0, tiled=True)
    return arrived.astype(jnp.float32).sum(axis=0)


def top_bit(differ, bit_total):
    count_bits = jnp.zeros(differ.shape, jnp.int32)
    for exponent in range(bit_total):
        count_bits = count_bits + (differ >= 2**exponent).astype(jnp.int32)
    return count_bits


def level_scales(level_total, head_width):
    raised = jnp.maximum(jnp.arange(level_total, dtype=jnp.int32) - 1, 0).astype(jnp.float32)
    return jnp.exp2(-0.5 * raised) / jnp.sqrt(jnp.float32(head_width))


def two_parts(exact_state):
    upper = exact_state.astype(jnp.bfloat16)
    lower = (exact_state - upper.astype(jnp.float32)).astype(jnp.bfloat16)
    return (upper, lower)


def state_first(form, exact_state, plain):
    upper, lower = two_parts(exact_state)
    return jnp.einsum(form, upper, plain, preferred_element_type=jnp.float32) + jnp.einsum(
        form, lower, plain, preferred_element_type=jnp.float32
    )


def state_second(form, plain, exact_state):
    upper, lower = two_parts(exact_state)
    return jnp.einsum(form, plain, upper, preferred_element_type=jnp.float32) + jnp.einsum(
        form, plain, lower, preferred_element_type=jnp.float32
    )


def on_device(queries, key_matrix, value_matrix, level_weight, out_weight, grad_out):
    rows_dev, head_count, head_width = queries.shape
    level_total = level_weight.shape[0]
    near_levels = rows_dev.bit_length()
    far_levels = lax.axis_size("seq").bit_length() - 1
    my_block = lax.axis_index("seq")
    scales = level_scales(level_total, head_width)
    weighted_levels = level_weight * scales[:, None, None]
    flat_out = out_weight.reshape(head_count * head_width, out_weight.shape[2])
    columns = flat_out
    mix_sum = lax.dot_general(
        lax.all_gather(grad_out, "head", axis=1, tiled=True),
        columns,
        (((1,), (1,)), ((), ())),
        preferred_element_type=jnp.float32,
    )
    grad_mix = mix_sum.astype(jnp.bfloat16).reshape(rows_dev, head_count, head_width)
    mix_f = grad_mix.astype(jnp.float32)
    key_weighted = jnp.einsum(
        "gpl,gpq->plq", key_matrix, value_matrix, preferred_element_type=jnp.float32
    )
    far_weights = weighted_levels[near_levels:]
    weighted = (
        far_weights[:, :, :, None] * jnp.transpose(queries.astype(jnp.float32), (1, 0, 2))[None]
    )
    back_states = state_first("jhik,ihv->jhkv", weighted, grad_mix)
    every = lax.all_gather(
        key_weighted[None].astype(jnp.bfloat16), "seq", axis=0, tiled=True
    ).astype(jnp.float32)
    block_ids = jnp.arange(every.shape[0], dtype=jnp.int32)
    block_gap = top_bit(jnp.bitwise_xor(block_ids, my_block), far_levels)
    level_ladder = jnp.arange(1, far_levels + 1, dtype=jnp.int32)
    masks = ((block_gap[None] == level_ladder[:, None]) & (block_ids < my_block)[None]).astype(
        jnp.float32
    )
    left_states = jnp.einsum("je,ehkv->jhkv", masks, every)
    pending = back_states
    right_list = []
    for bit_index in range(far_levels):
        partner = partner_2(pending.astype(jnp.bfloat16), "seq", bit_index).astype(pending.dtype)
        bit_off = 1.0 - (my_block // 2**bit_index % 2).astype(jnp.float32)
        right_list.append(bit_off * partner[0])
        pending = pending[1:] + partner[1:]
    right_states = jnp.stack(right_list)
    rows_index = lax.broadcasted_iota(jnp.int32, (rows_dev, near_levels, rows_dev), 0)
    tier_index = lax.broadcasted_iota(jnp.int32, (rows_dev, near_levels, rows_dev), 1)
    cols_index = lax.broadcasted_iota(jnp.int32, (rows_dev, near_levels, rows_dev), 2)
    near_gap = top_bit(jnp.bitwise_xor(rows_index, cols_index), near_levels - 1)
    onehot = ((near_gap == tier_index) & (cols_index <= rows_index)).astype(jnp.float32)
    mixing = jnp.einsum("ilj,lhi->hij", onehot, weighted_levels[:near_levels])
    scores = jnp.einsum("ihk,jhk->hij", queries, key_matrix, preferred_element_type=jnp.float32)
    attention = (scores * mixing).astype(jnp.bfloat16)
    local_out = jnp.einsum(
        "hij,jhv->ihv", attention, value_matrix, preferred_element_type=jnp.float32
    )
    far_rows = jnp.transpose(far_weights, (0, 2, 1))[..., None]
    reads = state_second("ihk,jhkv->jihv", queries, left_states)
    attended = (local_out + jnp.sum(far_rows * reads, axis=0)).astype(jnp.bfloat16)
    flat_att = attended.reshape(rows_dev, head_count * head_width)
    columns = flat_out
    mixed_cols = summed_on_arrival(
        lax.dot_general(
            columns, flat_att, (((0,), (1,)), ((), ())), preferred_element_type=jnp.float32
        ).astype(jnp.bfloat16),
        "head",
        0,
    )
    mixed_out = jnp.transpose(mixed_cols).astype(jnp.bfloat16)
    back = jnp.einsum("ihv,jhv->hij", grad_mix, value_matrix, preferred_element_type=jnp.float32)
    near_grad = jnp.einsum("ilj,hij->lhi", onehot, scores * back) * scales[:near_levels, None, None]
    far_grad = (
        jnp.transpose(jnp.sum(reads * mix_f[None], axis=3), (0, 2, 1))
        * scales[near_levels:, None, None]
    )
    grad_score = (back * mixing).astype(jnp.bfloat16)
    grad_queries = jnp.einsum(
        "hij,jhk->ihk", grad_score, key_matrix, preferred_element_type=jnp.float32
    )
    grad_queries = grad_queries + jnp.sum(
        far_rows * state_first("jhkv,ihv->jihk", left_states, grad_mix), axis=0
    )
    grad_keys = jnp.einsum("hij,ihk->jhk", grad_score, queries, preferred_element_type=jnp.float32)
    grad_keys = grad_keys + state_first("jhkv,ihv->ihk", right_states, value_matrix)
    grad_values = jnp.einsum(
        "hij,ihv->jhv", attention, grad_mix, preferred_element_type=jnp.float32
    )
    grad_values = grad_values + state_first("jhkv,ihk->ihv", right_states, key_matrix)
    grad_levels = jnp.concatenate([near_grad, far_grad], 0)
    return (
        mixed_out,
        grad_queries.astype(jnp.bfloat16),
        grad_keys.astype(jnp.bfloat16),
        grad_values.astype(jnp.bfloat16),
        grad_levels,
    )


def solution(mesh):
    in_specs = (
        P("seq", "head", None),
        P("seq", "head", None),
        P("seq", "head", None),
        P(None, "head", "seq"),
        P("head", None, None),
        P("seq", "head"),
    )
    out_specs = (
        P("seq", "head"),
        P("seq", "head", None),
        P("seq", "head", None),
        P("seq", "head", None),
        P(None, "head", "seq"),
    )
    return jax.shard_map(
        on_device, mesh=mesh, in_specs=in_specs, out_specs=out_specs, check_vma=False
    )
```

profile of v0, /device:TPU:1, one launch (start us, length us, event | category | flops | bytes accessed | tf_op | source)
XLA Modules:
  0.0 221.7 jit_solution(6458625137675124422)
XLA Ops:
  8.2 2.0 convolution_convert_fusion.1
  10.3 1.2 convert_bitcast_fusion
  11.5 3.9 %fusion.66 = f32[4,512,512]{2,1,0:T(8,128)} fusion(bf16[512,4,128]{2,1,0:T(4,128)(2,1)} %param.6, bf16[512,4,128]{2,1,0:T(4,128)(2,1)} %param.7), kind=kOutput, calls=%fused_computation.80 | convolution fusion | flops 268435456 | bytes 5242880 | tf_op jit(solution)/shard_map/ihk,jhk->hij/dot_general | solution.py:110
  16.8 12.6 %fusion.12 = f32[512,4,512]{2,1,0:T(4,128)} fusion(bf16[10,4,512]{0,1,2:T(4,128)(2,1)S(1)} %copy.141), kind=kOutput, calls=%fused_computation.15 | convolution fusion | flops 99614720 | bytes 4235264 | tf_op jit(solution)/shard_map/ilj,lhi->hij/dot_general | solution.py:109
  29.4 19.3 %all-gather.4.cloned.1.call-done = bf16[512,4096]{1,0:T(8,128)(2,1)} async-done(((bf16[512,512]{1,0:T(8,128)(2,1)}), bf16[512,4096]{1,0:T(8,128)(2,1)}) %all-gather.4.cloned.1.call-update) | async-done | bytes 4194320 | tf_op jit(solution)/shard_map/all_gather | solution.py:71
  48.7 7.0 %bitcast_convert_fusion.1 = (f32[512,4,128]{0,2,1:T(8,128)}, bf16[512,512]{0,1:T(8,128)(2,1)S(1)}) fusion(bf16[512,4096]{1,0:T(8,128)(2,1)} %all-gather.4.cloned.1.call-done, bf16[512,4096]{1,0:T(8,128)(2,1)} %bitcast.112), kind=kOutput, calls=%fused_computation.127 | convolution fusion | flops 2148007936 | bytes 9961472 | tf_op jit(solution)/shard_map/dot_general | solution.py:70
  55.6 2.4 %fusion.23 = f32[4,128,5,128]{3,1,2,0:T(8,128)S(1)} fusion(bf16[512,4,128,1]{0,2,3,1:T(8,128)(2,1)S(1)} %bitcast.102, f32[4,512,128]{2,1,0:T(8,128)S(1)} %copy.169, f32[5,4,512]{2,0,1:T(8,128)S(1)} %copy.168), kind=kOutput, calls=%fused_computation.33 | convolution fusion | flops 338165760 | bytes 2924544 | tf_op jit(solution)/shard_map/jhik,ihv->jhkv/dot_general | solution.py:48
  58.0 3.4 %fusion.119 = (bf16[5,4,128,128]{2,3,0,1:T(8,128)(2,1)}, f32[5,4,128,128]{2,3,0,1:T(8,128)}) fusion(f32[4,128,5,128]{3,1,2,0:T(8,128)S(1)} %fusion.23, bf16[512,4,128,1]{0,2,3,1:T(8,128)(2,1)S(1)} %bitcast.103, f32[4,512,128]{2,1,0:T(8,128)S(1)} %copy.169, f32[5,4,512]{2,0,1:T(8,128)S(1)} %copy.168), kind=kOutput, calls=%fused_computation.151 | convolution fusion | flops 342753280 | bytes 4890624 | tf_op jit(solution)/shard_map/jhik,ihv->jhkv/dot_general | solution.py:48
  61.4 1.2 collective-permute-start
  62.7 3.5 %fusion.19 = (bf16[4,512,512]{2,1,0:T(8,128)(2,1)S(1)}, bf16[4,512,512]{2,1,0:T(8,128)(2,1)}, f32[4,512,512]{2,1,0:T(8,128)S(1)}) fusion(f32[512,4,512]{2,1,0:T(4,128)S(1)} %copy-done.10, f32[4,512,512]{2,1,0:T(8,128)S(1)} %copy-done.1, bf16[512,4,128]{0,2,1:T(8,128)(2,1)S(1)} %bitcast.104, bf16[512,4,128]{2,1,0:T(4,128)(2,1)S(1)} %copy-done), kind=kOutput, calls=%fused_computation.29 | convolution fusion | flops 272629760 | bytes 17825792 | tf_op jit(solution)/shard_map/ihv,jhv->hij/dot_general | solution.py:128
  66.2 1.2 mul.130
  67.4 13.1 %fusion.47 = f32[10,4,512]{0,1,2:T(4,128)} fusion(bf16[4,512,512]{2,1,0:T(8,128)(2,1)S(1)} %mul.130, f32[10]{0:T(128)S(1)} %bitcast.111), kind=kOutput, calls=%fused_computation.58 | convolution fusion | flops 99635200 | bytes 2179112 | tf_op jit(solution)/shard_map/ilj,hij->lhi/dot_general | solution.py:129
  80.5 1.5 copy.179
  82.0 1.9 convolution_bitcast_fusion
  83.9 2.5 %fusion.120 = f32[4,128,512]{2,1,0:T(8,128)} fusion(bf16[512,4,128]{0,2,1:T(8,128)(2,1)} %bitcast.105, bf16[4,512,512]{2,1,0:T(8,128)(2,1)S(1)} %copy-done.5), kind=kOutput, calls=%fused_computation.152 | convolution fusion | flops 268435456 | bytes 3670016 | tf_op jit(solution)/shard_map/hij,ihv->jhv/dot_general | solution.py:143
  86.4 1.2 convert_element_type.260
  87.7 1.3 fusion.117
  89.0 2.5 %collective-permute-start.1 = (bf16[4,4,128,128]{2,3,0,1:T(8,128)(2,1)}, bf16[4,4,128,128]{2,3,0,1:T(8,128)(2,1)}, u32[]{:S(2)}, u32[]{:S(2)}) collective-permute-start(bf16[4,4,128,128]{2,3,0,1:T(8,128)(2,1)} %get-tuple-element.33), channel_id=1, source_target_pairs={{0,16},{16,0},{8,24},{24,8},{32,48},{48,32},{40,56},{56,40},{64,80... | collective-permute-start | bytes 1572872 | tf_op jit(solution)/shard_map/ppermute | solution.py:14
  91.4 0.7 fusion.86
  92.2 38.1 %all-gather.6.cloned.1.call-done = bf16[128,128,128]{2,1,0:T(8,128)(2,1)} async-done(((bf16[4,128,128]{2,1,0:T(8,128)(2,1)}), bf16[128,128,128]{2,1,0:T(8,128)(2,1)}) %all-gather.6.cloned.1.call-update) | async-done | bytes 4194320 | tf_op jit(solution)/shard_map/all_gather | solution.py:86
  130.3 4.5 %fusion.21 = f32[5,4,128,128]{3,0,2,1:T(8,128)S(1)} fusion(bf16[32,4,128,128]{3,2,1,0:T(8,128)(2,1)} %bitcast.108, s32[32]{0:T(128)S(1)} %fusion.96, s32[5]{0:T(128)S(1)} %iota_add_fusion, pred[32]{0:T(512)(128)(4,1)S(1)} %iota_compare_fusion.2), kind=kOutput, calls=%fused_computation.31 | convolution fusion | flops 20971840 | bytes 5505204 | tf_op jit(solution)/shard_map/je,ehkv->jhkv/dot_general | solution.py:95
  135.4 0.9 copy-done.9
  136.3 0.9 fusion.61
  137.2 2.6 %fusion.17 = (f32[5,512,4]{1,0,2:T(8,128)S(1)}, f32[512,4,128]{0,2,1:T(8,128)}) fusion(f32[512,4,128]{0,2,1:T(8,128)S(1)} %copy-done.17, f32[5,512,4]{1,0,2:T(8,128)S(1)} %copy.144, f32[4,5,128,512]{3,2,1,0:T(8,128)S(1)} %fusion.61, bf16[512,4,128,1]{2,1,0,3:T(4,128)(2,1)S(1)} %bitcast.101, bf16[5,4,128,128]{3,2,1,0:T(8,128)(2,1)S(1)} %subtract_convert_fusion), kind=kOutput, calls=%fused_computation.24 | convolution fusion | flops 341825536 | bytes 8601600 | tf_op jit(solution)/shard_map/ihk,jhkv->jihv/dot_general | solution.py:55
  139.8 2.5 %copy.154 = f32[512,4,128]{2,0,1:T(8,128)} copy(f32[512,4,128]{0,2,1:T(8,128)} %get-tuple-element.26) | data formatting | bytes 2097152 | tf_op jit(solution)/shard_map/reduce_sum | solution.py:117
  142.3 7.1 %bitcast_convert_fusion = bf16[512,4096]{1,0:T(8,128)(2,1)} fusion(bf16[4,128,4096]{2,1,0:T(8,128)(2,1)} %param.10, f32[512,4,128]{2,0,1:T(8,128)} %copy.154, bf16[4,512,512]{2,1,0:T(8,128)(2,1)} %get-tuple-element.36, bf16[512,4,128]{2,1,0:T(4,128)(2,1)S(1)} %copy-done), kind=kOutput, calls=%fused_computation.13 | convolution fusion | flops 2418540544 | bytes 12058624 | tf_op jit(solution)/shard_map/dot_general | solution.py:121
  149.5 4.5 %copy.270 = bf16[64,8,8,512]{3,2,0,1:T(8,128)(2,1)} copy(bf16[64,8,8,512]{3,2,1,0:T(8,128)(2,1)} %bitcast.109) | data formatting | bytes 8388608 | tf_op jit(solution)/shard_map/reshape | solution.py:19
  154.0 8.3 %all-to-all-start = ((bf16[8,512,512]{1,2,0:T(8,128)(2,1)}), bf16[8,512,512]{1,2,0:T(8,128)(2,1)}, u32[]{:S(2)}, u32[]{:S(2)}) async-start(bf16[8,512,512]{1,2,0:T(8,128)(2,1)} %bitcast.99), calls=%async_computation | async-start | bytes 8388608 | tf_op jit(solution)/shard_map/all_to_all | solution.py:24
  162.3 2.0 fusion.59
  164.3 1.1 convert_element_type.263
  165.5 1.0 copy-done.13
  166.5 1.2 fusion.116
  167.6 1.2 collective-permute-start.2
  168.8 1.9 fusion.15
  170.7 2.7 %copy.165 = f32[512,4,128]{2,0,1:T(8,128)} copy(f32[512,4,128]{0,2,1:T(8,128)} %fusion.15) | data formatting | bytes 2097152 | tf_op jit(solution)/shard_map/reduce_sum | solution.py:138
  173.4 2.2 fusion.54
  175.6 2.9 %collective-permute-done.2 = bf16[3,4,128,128]{2,3,0,1:T(8,128)(2,1)} collective-permute-done((bf16[3,4,128,128]{2,3,0,1:T(8,128)(2,1)}, bf16[3,4,128,128]{2,3,0,1:T(8,128)(2,1)}, u32[]{:S(2)}, u32[]{:S(2)}) %collective-permute-start.2) | collective-permute-done | bytes 393248 | tf_op jit(solution)/shard_map/ppermute | solution.py:14
  178.5 1.1 convert_element_type.266
  179.6 1.9 collective-permute-start.3
  181.6 1.0 fusion.85
  182.6 11.1 %collective-permute-done.3 = bf16[2,4,128,128]{2,3,0,1:T(8,128)(2,1)S(1)} collective-permute-done((bf16[2,4,128,128]{2,3,0,1:T(8,128)(2,1)S(1)}, bf16[2,4,128,128]{2,3,0,1:T(8,128)(2,1)S(1)}, u32[]{:S(2)}, u32[]{:S(2)}) %collective-permute-start.3) | collective-permute-done | bytes 262176 | tf_op jit(solution)/shard_map/ppermute | solution.py:14
  193.8 2.6 %collective-permute-start.4 = (bf16[1,4,128,128]{2,3,0,1:T(8,128)(2,1)S(1)}, bf16[1,4,128,128]{2,3,0,1:T(8,128)(2,1)S(1)}, u32[]{:S(2)}, u32[]{:S(2)}) collective-permute-start(bf16[1,4,128,128]{2,3,0,1:T(8,128)(2,1)S(1)} %get-tuple-element.37), channel_id=1, source_target_pairs={{0,128},{128,0},{8,136},{136,8},{16,144},{144,16},{24,152},{152,24... | collective-permute-start | bytes 393224 | tf_op jit(solution)/shard_map/ppermute | solution.py:14
  196.4 1.2 copy.181
  198.3 6.2 %collective-permute-done.4 = bf16[1,4,128,128]{2,3,0,1:T(8,128)(2,1)S(1)} collective-permute-done((bf16[1,4,128,128]{2,3,0,1:T(8,128)(2,1)S(1)}, bf16[1,4,128,128]{2,3,0,1:T(8,128)(2,1)S(1)}, u32[]{:S(2)}, u32[]{:S(2)}) %collective-permute-start.4) | collective-permute-done | bytes 131104 | tf_op jit(solution)/shard_map/ppermute | solution.py:14
  205.4 1.2 copy.182
  207.2 1.1 copy.183
  208.3 2.8 %all-to-all-done = bf16[8,512,512]{1,2,0:T(8,128)(2,1)} async-done(((bf16[8,512,512]{1,2,0:T(8,128)(2,1)}), bf16[8,512,512]{1,2,0:T(8,128)(2,1)}, u32[]{:S(2)}, u32[]{:S(2)}) %all-to-all-start) | async-done | bytes 4194336 | tf_op jit(solution)/shard_map/all_to_all | solution.py:24
  211.1 3.7 %reduce_sum.66 = bf16[512,512]{0,1:T(8,128)(2,1)} reduce(bf16[8,512,512]{1,2,0:T(8,128)(2,1)} %all-to-all-done, bf16[]{:T(256)} %constant.118.clone.1), dimensions={0}, to_apply=%region_1.2 | reduce | flops 1835008 | bytes 4718594 | tf_op jit(solution)/shard_map/reduce_sum | solution.py:25
  (73 shorter events, 5.1 us)
Async XLA Ops:
  7.2 1.0 copy-start
  7.2 41.5 %all-gather.4.cloned.1.call-start = ((), (), s32[]{:S(2)}) async-start(), calls=%async_computation.1 | async-start | bytes 4718592 | tf_op jit(solution)/shard_map/all_gather | solution.py:71
  7.9 7.5 %copy-start.19 = (f32[15,4,512]{2,1,0:T(4,128)S(1)}, f32[15,4,512]{2,1,0:T(4,128)}, u32[]{:S(2)}) copy-start(f32[15,4,512]{2,1,0:T(4,128)} %param.9) | copy-start | bytes 368644
  7.9 122.4 %all-gather.6.cloned.1.call-start = ((), (), s32[]{:S(2)}) async-start(), calls=%async_computation.2 | async-start | bytes 4325376 | tf_op jit(solution)/shard_map/all_gather | solution.py:86
  48.7 14.0 %copy-start.10 = (f32[512,4,512]{2,1,0:T(4,128)S(1)}, f32[512,4,512]{2,1,0:T(4,128)}, u32[]{:S(2)}) copy-start(f32[512,4,512]{2,1,0:T(4,128)} %fusion.12) | copy-start | bytes 12582916
  55.6 10.5 %copy-start.3 = (bf16[512,512]{0,1:T(8,128)(2,1)}, bf16[512,512]{0,1:T(8,128)(2,1)S(1)}, u32[]{:S(2)}) copy-start(bf16[512,512]{0,1:T(8,128)(2,1)S(1)} %get-tuple-element.42) | copy-start | bytes 1572868
  55.6 7.0 %copy-start.1 = (f32[4,512,512]{2,1,0:T(8,128)S(1)}, f32[4,512,512]{2,1,0:T(8,128)}, u32[]{:S(2)}) copy-start(f32[4,512,512]{2,1,0:T(8,128)} %fusion.66) | copy-start | bytes 12582916
  61.4 25.0 %collective-permute-start = (bf16[5,4,128,128]{2,3,0,1:T(8,128)(2,1)}, bf16[5,4,128,128]{2,3,0,1:T(8,128)(2,1)}, u32[]{:S(2)}, u32[]{:S(2)}) collective-permute-start(bf16[5,4,128,128]{2,3,0,1:T(8,128)(2,1)} %get-tuple-element.44), channel_id=1, source_target_pairs={{0,8},{8,0},{16,24},{24,16},{32,40},{40,32},{48,56},{56,48},{64,72... | collective-permute-start | bytes 1966088 | tf_op jit(solution)/shard_map/ppermute | solution.py:14
  67.3 14.7 %copy-start.2 = (bf16[512,4,128]{2,1,0:T(4,128)(2,1)S(1)}, bf16[512,4,128]{2,1,0:T(4,128)(2,1)}, u32[]{:S(2)}) copy-start(bf16[512,4,128]{2,1,0:T(4,128)(2,1)} %param.6) | copy-start | bytes 1572868
  82.0 1.9 copy-start.5
  82.0 5.6 %copy-start.18 = (f32[5,4,128,128]{2,3,0,1:T(8,128)S(1)}, f32[5,4,128,128]{2,3,0,1:T(8,128)}, u32[]{:S(2)}) copy-start(f32[5,4,128,128]{2,3,0,1:T(8,128)} %get-tuple-element.45) | copy-start | bytes 3932164
  89.0 75.4 %collective-permute-start.1 = (bf16[4,4,128,128]{2,3,0,1:T(8,128)(2,1)}, bf16[4,4,128,128]{2,3,0,1:T(8,128)(2,1)}, u32[]{:S(2)}, u32[]{:S(2)}) collective-permute-start(bf16[4,4,128,128]{2,3,0,1:T(8,128)(2,1)} %get-tuple-element.33), channel_id=1, source_target_pairs={{0,16},{16,0},{8,24},{24,8},{32,48},{48,32},{40,56},{56,40},{64,80... | collective-permute-start | bytes 1572872 | tf_op jit(solution)/shard_map/ppermute | solution.py:14
  135.1 2.0 copy-start.7
  135.1 2.0 copy-start.17
  135.4 0.9 copy-start.9
  154.0 8.3 %copy-start.4 = (bf16[512,512]{0,1:T(8,128)(2,1)S(1)}, bf16[512,512]{0,1:T(8,128)(2,1)}, u32[]{:S(2)}) copy-start(bf16[512,512]{0,1:T(8,128)(2,1)} %copy-done.3) | copy-start | bytes 1572868
  154.0 57.1 %all-to-all-start = ((bf16[8,512,512]{1,2,0:T(8,128)(2,1)}), bf16[8,512,512]{1,2,0:T(8,128)(2,1)}, u32[]{:S(2)}, u32[]{:S(2)}) async-start(bf16[8,512,512]{1,2,0:T(8,128)(2,1)} %bitcast.99), calls=%async_computation | async-start | bytes 8388608 | tf_op jit(solution)/shard_map/all_to_all | solution.py:24
  162.3 4.2 %copy-start.14 = (f32[4,4,128,128]{2,3,0,1:T(8,128)S(1)}, f32[4,4,128,128]{2,3,0,1:T(8,128)}, u32[]{:S(2)}) copy-start(f32[4,4,128,128]{2,3,0,1:T(8,128)} %get-tuple-element.34) | copy-start | bytes 3145732
  162.3 6.5 %copy-start.8 = (bf16[5,4,128,128]{3,2,1,0:T(8,128)(2,1)S(1)}, bf16[5,4,128,128]{3,2,1,0:T(8,128)(2,1)}, u32[]{:S(2)}) copy-start(bf16[5,4,128,128]{3,2,1,0:T(8,128)(2,1)} %copy-done.7) | copy-start | bytes 1966084
  165.5 1.0 copy-start.13
  167.6 10.8 %collective-permute-start.2 = (bf16[3,4,128,128]{2,3,0,1:T(8,128)(2,1)}, bf16[3,4,128,128]{2,3,0,1:T(8,128)(2,1)}, u32[]{:S(2)}, u32[]{:S(2)}) collective-permute-start(bf16[3,4,128,128]{2,3,0,1:T(8,128)(2,1)} %get-tuple-element.31), channel_id=1, source_target_pairs={{0,32},{32,0},{8,40},{40,8},{16,48},{48,16},{24,56},{56,24},{64,96... | collective-permute-start | bytes 1179656 | tf_op jit(solution)/shard_map/ppermute | solution.py:14
  170.7 8.9 %copy-start.15 = (f32[3,4,128,128]{2,3,0,1:T(8,128)S(1)}, f32[3,4,128,128]{2,3,0,1:T(8,128)}, u32[]{:S(2)}) copy-start(f32[3,4,128,128]{2,3,0,1:T(8,128)} %get-tuple-element.32) | copy-start | bytes 2359300
  173.4 8.2 %copy-start.16 = (f32[5,4,128,128]{2,3,0,1:T(8,128)S(1)}, f32[5,4,128,128]{2,3,0,1:T(8,128)}, u32[]{:S(2)}) copy-start(f32[5,4,128,128]{2,3,0,1:T(8,128)} %fusion.86) | copy-start | bytes 3932164
  173.4 23.0 %copy-start.20 = (f32[5]{0:T(128)S(1)}, f32[5]{0:T(128)}, u32[]{:S(2)}) copy-start(f32[5]{0:T(128)} %slice.63) | copy-start | bytes 64
  179.6 25.4 %copy-start.12 = (f32[512,4,128]{2,0,1:T(8,128)S(1)}, f32[512,4,128]{2,0,1:T(8,128)}, u32[]{:S(2)}) copy-start(f32[512,4,128]{2,0,1:T(8,128)} %convolution_bitcast_fusion) | copy-start | bytes 3145732
  179.6 14.0 %collective-permute-start.3 = (bf16[2,4,128,128]{2,3,0,1:T(8,128)(2,1)S(1)}, bf16[2,4,128,128]{2,3,0,1:T(8,128)(2,1)S(1)}, u32[]{:S(2)}, u32[]{:S(2)}) collective-permute-start(bf16[2,4,128,128]{2,3,0,1:T(8,128)(2,1)S(1)} %get-tuple-element.29), channel_id=1, source_target_pairs={{0,64},{64,0},{8,72},{72,8},{16,80},{80,16},{24,88},{88,24},{32,96... | collective-permute-start | bytes 786440 | tf_op jit(solution)/shard_map/ppermute | solution.py:14
  193.8 10.8 %collective-permute-start.4 = (bf16[1,4,128,128]{2,3,0,1:T(8,128)(2,1)S(1)}, bf16[1,4,128,128]{2,3,0,1:T(8,128)(2,1)S(1)}, u32[]{:S(2)}, u32[]{:S(2)}) collective-permute-start(bf16[1,4,128,128]{2,3,0,1:T(8,128)(2,1)S(1)} %get-tuple-element.37), channel_id=1, source_target_pairs={{0,128},{128,0},{8,136},{136,8},{16,144},{144,16},{24,152},{152,24... | collective-permute-start | bytes 393224 | tf_op jit(solution)/shard_map/ppermute | solution.py:14
  197.6 8.9 %copy-start.6 = (bf16[512,4,128]{2,1,0:T(4,128)(2,1)S(1)}, bf16[512,4,128]{2,1,0:T(4,128)(2,1)}, u32[]{:S(2)}) copy-start(bf16[512,4,128]{2,1,0:T(4,128)(2,1)} %param.7) | copy-start | bytes 1572868
  204.7 2.1 copy-start.11
Sparse Core Ops, SparseCore 0:
  9.8 38.7 all-gather.3
  51.8 78.4 all-gather.5
where the time goes:
time: 222 us
  waiting for transfers between devices  81.1 us (37%)
  matrix products  74.8 us (34%)
  local copies, waits for them, and re-layouts  18.3 us (8%)
  starting transfers between devices  17.7 us (8%)
  other arithmetic  15.1 us (7%)
  between operations  14.6 us (7%)
    all_gather x1, waiting for transfers between devices, on_device(): lax.all_gather(key_weighted[None].astype(jnp.bfloat16), 'seq', axis=0, ti...  38.1 us
    ppermute x5, waiting for transfers between devices, partner_2(): return lax.ppermute(block, axis, route)  20.2 us
    all_gather x1, waiting for transfers between devices, on_device(): lax.all_gather(grad_out, 'head', axis=1, tiled=True)  19.3 us
    dot_general x1, matrix products, on_device(): jnp.einsum('ilj,hij->lhi', onehot, scores * back)  13.1 us
    dot_general x1, matrix products, on_device(): mixing = jnp.einsum('ilj,lhi->hij', onehot, weighted_levels[:near_levels])  12.6 us
    ppermute x5, starting transfers between devices, partner_2(): return lax.ppermute(block, axis, route)  9.37 us
    all_to_all x1, starting transfers between devices, summed_on_arrival(): lax.all_to_all(parts, axis, split_axis=0, concat_axis=0, tiled=True)  8.28 us
    dot_general x1, matrix products, on_device(): lax.dot_general(columns, flat_att, (((0,), (1,)), ((), ())), preferred_el...  7.13 us
  transfers between devices with their start and end apart: 8, of which 6 were waited for; matrix products, arithmetic and copies ran while one was open for 46% of the time, Pallas kernels for 0%

commit v1 on v0

v1 whole, which is shorter than its diff:
```python
import math

import jax
import jax.numpy as jnp
from jax import lax
from jax.experimental import pallas as pl
from jax.experimental.pallas import tpu as pltpu
from jax.sharding import Mesh, PartitionSpec as P


F32 = jnp.float32
BF16 = jnp.bfloat16
BLK = 128
NEAR = 10
FAR = 5
HD = 128
C = [2.0 ** (-max(l - 1, 0) / 2) / math.sqrt(HD) for l in range(NEAR + FAR)]

NN = (((1,), (0,)), ((), ()))
NT = (((1,), (1,)), ((), ()))
TN = (((0,), (0,)), ((), ()))


def dot(a, b, dims):
    return lax.dot_general(a, b, dims, preferred_element_type=F32)


def diag_level():
    s = lax.broadcasted_iota(jnp.int32, (BLK, BLK), 0)
    t = lax.broadcasted_iota(jnp.int32, (BLK, BLK), 1)
    differ = s ^ t
    level = jnp.zeros((BLK, BLK), jnp.int32)
    for e in range(7):
        level = level + (differ >= 2**e).astype(jnp.int32)
    return jnp.where(s <= t, level, -1)


def w_row(lw_ref, l, h, i):
    return lw_ref[l, pl.ds(h, 1), pl.ds(i * BLK, BLK)] * C[l]


def mix_parts(lw_ref, level, h, i):
    diag = jnp.zeros((BLK, BLK), F32)
    for l in range(8):
        diag = jnp.where(level == l, w_row(lw_ref, l, h, i), diag)
    parts = []
    for j in range(i):
        parts.append(w_row(lw_ref, 8 if (i ^ j) == 1 else 9, h, i))
    return parts + [diag]


def flat(ref):
    rows, heads, hd = ref.shape
    return ref[...].reshape(rows, heads * hd)


def fwd_kernel(q_ref, k_ref, v_ref, lw_ref, lo_ref, wq_ref):
    level = diag_level()
    rows, heads, _ = q_ref.shape
    q_all, k_all, v_all = flat(q_ref), flat(k_ref), flat(v_ref)
    for h in range(heads):
        lanes = slice(h * HD, (h + 1) * HD)
        q, k, v = q_all[:, lanes], k_all[:, lanes], v_all[:, lanes]
        for i in range(rows // BLK):
            n = (i + 1) * BLK
            st = dot(k[:n], q[i * BLK : n], NT)
            mix = mix_parts(lw_ref, level, h, i)
            at = jnp.concatenate(
                [(st[j * BLK : (j + 1) * BLK] * mix[j]).astype(BF16) for j in range(i + 1)],
                axis=0,
            )
            lo_ref[pl.ds(i * BLK, BLK), lanes] = dot(at, v[:n], TN)
        qt = q.astype(F32).T
        for j in range(FAR):
            row = lw_ref[NEAR + j, pl.ds(h, 1), :] * C[NEAR + j]
            wq_ref[h, pl.ds(j * HD, HD), :] = (qt * row).astype(BF16)


def bwd_kernel(q_ref, k_ref, v_ref, g_ref, lw_ref, dq_ref, dk_ref, dv_ref, ng_ref):
    level = diag_level()
    rows, heads, _ = q_ref.shape
    blocks = rows // BLK
    q_all, k_all, v_all = flat(q_ref), flat(k_ref), flat(v_ref)
    for h in range(heads):
        lanes = slice(h * HD, (h + 1) * HD)
        q, k, v, g = q_all[:, lanes], k_all[:, lanes], v_all[:, lanes], g_ref[:, lanes]
        for i in reversed(range(blocks)):
            n = (i + 1) * BLK
            q_i, g_i = q[i * BLK : n], g[i * BLK : n]
            st = dot(k[:n], q_i, NT)
            bt = dot(v[:n], g_i, NT)
            mix = mix_parts(lw_ref, level, h, i)
            ats, gts, sums = [], [], [None] * NEAR
            for j in range(i + 1):
                s_j = st[j * BLK : (j + 1) * BLK]
                b_j = bt[j * BLK : (j + 1) * BLK]
                ats.append((s_j * mix[j]).astype(BF16))
                gts.append((b_j * mix[j]).astype(BF16))
                prod = s_j * b_j
                if j == i:
                    for l in range(8):
                        sums[l] = jnp.sum(
                            jnp.where(level == l, prod, 0.0), axis=0, keepdims=True
                        )
                else:
                    l = 8 if (i ^ j) == 1 else 9
                    total = jnp.sum(prod, axis=0, keepdims=True)
                    sums[l] = total if sums[l] is None else sums[l] + total
            at = jnp.concatenate(ats, axis=0)
            gt = jnp.concatenate(gts, axis=0)
            for l in range(NEAR):
                value = jnp.zeros((1, BLK), F32) if sums[l] is None else sums[l] * C[l]
                ng_ref[l, pl.ds(h, 1), pl.ds(i * BLK, BLK)] = value
            dq_ref[pl.ds(i * BLK, BLK), lanes] = dot(gt, k[:n], TN)
            if i == blocks - 1:
                dk_ref[:, lanes] = dot(gt, q_i, NN)
                dv_ref[:, lanes] = dot(at, g_i, NN)
            else:
                dk_ref[pl.ds(0, n), lanes] += dot(gt, q_i, NN)
                dv_ref[pl.ds(0, n), lanes] += dot(at, g_i, NN)


def left_stack(m_ref, r_refs, h):
    return jnp.concatenate(
        [(r[h].astype(F32) * m_ref[j]).astype(BF16) for j, r in enumerate(r_refs)], axis=0
    )


def attend_kernel(m_ref, lo_ref, wq_ref, r0, r1, r2, r3, r4, att_ref):
    for h in range(wq_ref.shape[0]):
        lanes = slice(h * HD, (h + 1) * HD)
        states = left_stack(m_ref, (r0, r1, r2, r3, r4), h)
        att_ref[:, lanes] = (lo_ref[:, lanes] + dot(wq_ref[h], states, TN)).astype(BF16)


def dq_kernel(m_ref, q_ref, g_ref, lw_ref, dql_ref, ng_ref, r0, r1, r2, r3, r4, dq_ref, gl_ref):
    _, heads, _ = q_ref.shape
    q_all = flat(q_ref)
    outs = []
    gl_ref[pl.ds(0, NEAR)] = ng_ref[...]
    for h in range(heads):
        lanes = slice(h * HD, (h + 1) * HD)
        states = left_stack(m_ref, (r0, r1, r2, r3, r4), h)
        read = dot(states, g_ref[:, lanes], NT)
        qt = q_all[:, lanes].astype(F32).T
        total = jnp.zeros(qt.shape, F32)
        for j in range(FAR):
            part = read[j * HD : (j + 1) * HD]
            row = lw_ref[NEAR + j, pl.ds(h, 1), :] * C[NEAR + j]
            total = total + part * row
            gl_ref[NEAR + j, pl.ds(h, 1), :] = (
                jnp.sum(part * qt, axis=0, keepdims=True) * C[NEAR + j]
            )
        outs.append((dql_ref[:, lanes] + total.T).astype(BF16))
    dq_ref[...] = jnp.concatenate(outs, axis=1).reshape(q_ref.shape)


def state_kernel(own_ref, rec_ref, wq_ref, g_ref, ws_ref):
    for h in range(wq_ref.shape[0]):
        lanes = slice(h * HD, (h + 1) * HD)
        g = (own_ref[:, lanes] + rec_ref[:, lanes].astype(F32)).astype(BF16)
        g_ref[:, lanes] = g
        ws_ref[h] = dot(wq_ref[h], g, NN).astype(BF16)


def final_kernel(dkl_ref, dvl_ref, k_ref, v_ref, r_ref, dk_ref, dv_ref):
    k_all, v_all = flat(k_ref), flat(v_ref)
    dks, dvs = [], []
    for h in range(r_ref.shape[0]):
        lanes = slice(h * HD, (h + 1) * HD)
        r = r_ref[h]
        dks.append((dkl_ref[:, lanes] + dot(v_all[:, lanes], r, NT)).astype(BF16))
        dvs.append((dvl_ref[:, lanes] + dot(k_all[:, lanes], r, NN)).astype(BF16))
    dk_ref[...] = jnp.concatenate(dks, axis=1).reshape(k_ref.shape)
    dv_ref[...] = jnp.concatenate(dvs, axis=1).reshape(k_ref.shape)


def wcol(ref, idx_ref, n, seg):
    return ref[:, pl.ds(pl.multiple_of(idx_ref[n] * seg, seg), seg)]


def mix12_kernel(idx_ref, go, gl, gr, w_ref, p_ref, own_ref, par_ref):
    seg = go.shape[1]
    for ref, out in ((p_ref, par_ref), (w_ref, own_ref)):
        out[...] = (
            dot(go[...], wcol(ref, idx_ref, 0, seg), NT)
            + dot(gl[...], wcol(ref, idx_ref, 1, seg), NT)
            + dot(gr[...], wcol(ref, idx_ref, 2, seg), NT)
        )


def mix3_kernel(idx_ref, top, bot, acc, w_ref, out_ref):
    half, seg = top.shape
    w = wcol(w_ref, idx_ref, 3, seg)
    for base, part in ((0, top), (half, bot)):
        rows = pl.ds(base, half)
        out_ref[rows, :] = (acc[rows, :] + dot(part[...], w, NT)).astype(out_ref.dtype)


def out_rows(idx_ref, a, ap, w_ref, p_ref, n, rows, seg):
    return dot(a[rows, :], wcol(w_ref, idx_ref, n, seg), NN) + dot(
        ap[rows, :], wcol(p_ref, idx_ref, n, seg), NN
    )


def out_far_kernel(idx_ref, a, ap, w_ref, p_ref, top_ref, bot_ref):
    half, seg = top_ref.shape
    for ref, base in ((top_ref, 0), (bot_ref, half)):
        ref[...] = out_rows(idx_ref, a, ap, w_ref, p_ref, 3, pl.ds(base, half), seg).astype(BF16)


def out_first_kernel(idx_ref, a, ap, w_ref, p_ref, r_bot, l_top):
    half, seg = r_bot.shape
    r_bot[...] = out_rows(idx_ref, a, ap, w_ref, p_ref, 2, pl.ds(half, half), seg).astype(BF16)
    l_top[...] = out_rows(idx_ref, a, ap, w_ref, p_ref, 1, pl.ds(0, half), seg).astype(BF16)


def out_rest_kernel(idx_ref, a, ap, w_ref, p_ref, r_top, l_bot, own):
    half, seg = r_top.shape
    r_top[...] = out_rows(idx_ref, a, ap, w_ref, p_ref, 2, pl.ds(0, half), seg)
    l_bot[...] = out_rows(idx_ref, a, ap, w_ref, p_ref, 1, pl.ds(half, half), seg)
    own[...] = out_rows(idx_ref, a, ap, w_ref, p_ref, 0, pl.ds(0, 2 * half), seg)


def sum_kernel(own, lt, lb, rt, rb, out_ref):
    half = lt.shape[0]
    for base, a, b in ((0, lt, rt), (half, lb, rb)):
        rows = pl.ds(base, half)
        out_ref[rows, :] = (own[rows, :] + a[...].astype(F32) + b[...].astype(F32)).astype(BF16)


SMEM = pl.BlockSpec(memory_space=pltpu.SMEM)
VMEM = pl.BlockSpec(memory_space=pltpu.VMEM)


def kernel_call(body, outs, operands, flops, scalars=0, vmem=16):
    out_shape = [jax.ShapeDtypeStruct(s, d) for s, d in outs]
    nbytes = sum(math.prod(s) * jnp.dtype(d).itemsize for s, d in outs)
    nbytes += sum(o.size * o.dtype.itemsize for o in operands)
    return pl.pallas_call(
        body,
        in_specs=[SMEM] * scalars + [VMEM] * (len(operands) - scalars),
        out_specs=[VMEM] * len(outs),
        out_shape=out_shape,
        cost_estimate=pl.CostEstimate(
            flops=int(flops), transcendentals=0, bytes_accessed=int(nbytes)
        ),
        compiler_params=pltpu.CompilerParams(vmem_limit_bytes=vmem << 20),
    )(*operands)


def body(queries, key_matrix, value_matrix, level_weight, out_weight, grad_out):
    rows, heads, hd = queries.shape
    width = heads * hd
    feat = out_weight.shape[2]
    levels = level_weight.shape[0]
    half = rows // 2
    z, y, x, c = (lax.axis_index(n) for n in ("z", "y", "x", "c"))
    nx, ny, nz = (lax.axis_size(n) for n in ("x", "y", "z"))
    right = [(i, (i + 1) % nx) for i in range(nx)]
    left = [(i, (i - 1) % nx) for i in range(nx)]
    swap = [(0, 1), (1, 0)]
    seg = feat // (2 * nx)
    w2 = out_weight.reshape(width, feat)

    from_l = lax.ppermute(grad_out, "x", right)
    from_r = lax.ppermute(grad_out, "x", left)
    w_par = lax.ppermute(w2, "c", swap)

    run = jnp.einsum("gpl,gpq->plq", key_matrix, value_matrix, preferred_element_type=F32)
    lefts = []
    for step, (axis, bit) in enumerate((("y", 0), ("y", 1), ("z", 0), ("z", 1), ("z", 2))):
        n = lax.axis_size(axis)
        last = step == 4
        route = [(i, i ^ (1 << bit)) for i in range(n) if not (last and i >> bit & 1)]
        got = lax.ppermute(run.astype(BF16), axis, route)
        lefts.append(got)
        if not last:
            run = run + got.astype(F32)
    bits = [y & 1, y >> 1 & 1, z & 1, z >> 1 & 1, z >> 2 & 1]
    mask = jnp.stack(bits).astype(F32)

    block = 2 * rows * rows * width
    local_out, wq = kernel_call(
        fwd_kernel,
        [((rows, width), F32), ((heads, FAR * hd, rows), BF16)],
        (queries, key_matrix, value_matrix, level_weight),
        2 * block,
    )

    xs = jnp.stack([x, (x + nx - 1) % nx, (x + 1) % nx, (x + 2) % nx])
    idx = (xs * 2 + c).astype(jnp.int32)

    far_top = lax.ppermute(from_l[:half], "x", right)
    far_bot = lax.ppermute(from_r[half:], "x", left)
    mm = 2 * rows * seg * width
    own12, par12 = kernel_call(
        mix12_kernel,
        [((rows, width), F32)] * 2,
        (idx, grad_out, from_l, from_r, w2, w_par),
        6 * mm,
        scalars=1,
    )
    (mix_send,) = kernel_call(
        mix3_kernel, [((rows, width), BF16)], (idx, far_top, far_bot, par12, w_par), mm, scalars=1
    )
    mix_got = lax.ppermute(mix_send, "c", swap)
    (mix_own,) = kernel_call(
        mix3_kernel, [((rows, width), F32)], (idx, far_top, far_bot, own12, w2), mm, scalars=1
    )
    g2, ws = kernel_call(
        state_kernel,
        [((rows, width), BF16), ((heads, FAR * hd, hd), BF16)],
        (mix_own, mix_got, wq),
        2 * rows * hd * hd * FAR * heads,
    )

    got = lax.all_to_all(ws, "y", split_axis=0, concat_axis=0, tiled=True)
    got = got.reshape(ny, FAR, hd, hd).astype(F32)
    pairs = got[2, 1] + got[3, 1]
    near = [got[1, 0] + pairs, pairs, got[3, 0], jnp.zeros_like(pairs)]
    held = got[:, 2:].sum(axis=0)
    acc = jnp.zeros_like(pairs)
    for bit in range(3):
        route = [(i, i ^ (1 << bit)) for i in range(nz)]
        other = lax.ppermute(held.astype(BF16), "z", route).astype(F32)
        acc = acc + jnp.where(z >> bit & 1, 0.0, other[0])
        held = held[1:] + other[1:]
    back = jnp.stack([part + acc for part in near]).astype(BF16)
    right_states = lax.all_to_all(back, "y", split_axis=0, concat_axis=0, tiled=True)

    (attended,) = kernel_call(
        attend_kernel,
        [((rows, width), BF16)],
        (mask, local_out, wq, *lefts),
        2 * rows * hd * hd * FAR * heads,
        scalars=1,
    )
    att_par = lax.ppermute(attended, "c", swap)

    piece = ((half, seg), BF16)
    piece32 = ((half, seg), F32)
    operands = (idx, attended, att_par, w2, w_par)
    opp_top, opp_bot = kernel_call(out_far_kernel, [piece] * 2, operands, 2 * mm, scalars=1)
    via_l = lax.ppermute(opp_top, "x", right)
    via_r = lax.ppermute(opp_bot, "x", left)
    r_bot, l_top = kernel_call(out_first_kernel, [piece] * 2, operands, 2 * mm, scalars=1)
    in_l_bot = lax.ppermute(r_bot, "x", right)
    in_r_top = lax.ppermute(l_top, "x", left)
    r_top, l_bot, out_own = kernel_call(
        out_rest_kernel, [piece32, piece32, ((rows, seg), F32)], operands, 4 * mm, scalars=1
    )
    r_top = (r_top + via_l.astype(F32)).astype(BF16)
    l_bot = (l_bot + via_r.astype(F32)).astype(BF16)
    in_l_top = lax.ppermute(r_top, "x", right)
    in_r_bot = lax.ppermute(l_bot, "x", left)
    (mixed_out,) = kernel_call(
        sum_kernel,
        [((rows, seg), BF16)],
        (out_own, in_l_top, in_l_bot, in_r_top, in_r_bot),
        rows * seg * 4,
    )

    dq_local, dk_local, dv_local, near_grad = kernel_call(
        bwd_kernel,
        [((rows, width), F32)] * 3 + [((NEAR, heads, rows), F32)],
        (queries, key_matrix, value_matrix, g2, level_weight),
        5 * block,
    )
    grad_queries, grad_levels = kernel_call(
        dq_kernel,
        [((rows, heads, hd), BF16), ((levels, heads, rows), F32)],
        (mask, queries, g2, level_weight, dq_local, near_grad, *lefts),
        2 * rows * hd * hd * FAR * heads,
        scalars=1,
    )
    grad_keys, grad_values = kernel_call(
        final_kernel,
        [((rows, heads, hd), BF16)] * 2,
        (dk_local, dv_local, key_matrix, value_matrix, right_states),
        4 * rows * hd * hd * heads,
    )
    return mixed_out, grad_queries, grad_keys, grad_values, grad_levels


def solution(mesh):
    grid = Mesh(mesh.devices.reshape(8, 4, 4, 2), ("z", "y", "x", "c"))
    seq, head = ("z", "y"), ("x", "c")
    by_row = P(seq, head, None)
    in_specs = (by_row, by_row, by_row, P(None, head, seq), P(head, None, None), P(seq, head))
    out_specs = (P(seq, head), by_row, by_row, by_row, P(None, head, seq))
    return jax.shard_map(body, mesh=grid, in_specs=in_specs, out_specs=out_specs, check_vma=False)
```

time: 222 us -> 123 us (0.55)
  the two profiles are of different devices: /device:TPU:1 before, /device:TPU:10 now
where the time goes in v1:
time: 123 us; the launch traced here: 122 us
  starting transfers between devices  49.6 us (40%)
  Pallas kernels  37.9 us (31%)
  local copies, waits for them, and re-layouts  14.6 us (12%)
  waiting for transfers between devices  11.8 us (10%)
  other arithmetic  5.83 us (5%)
  matrix products  1.59 us (1%)
    pallas_call x13, Pallas kernels, kernel_call(): pl.pallas_call(body, in_specs=[SMEM] * scalars + [VMEM] * (len(operands)...  37.9 us
    ppermute x5, starting transfers between devices, body(): got = lax.ppermute(run.astype(BF16), axis, route)  15 us
    unnamed x46, local copies, waits for them, and re-layouts  14.4 us
    ppermute x3, starting transfers between devices, body(): other = lax.ppermute(held.astype(BF16), 'z', route).astype(F32)  10.9 us
    ppermute x5, waiting for transfers between devices, body(): got = lax.ppermute(run.astype(BF16), axis, route)  8.34 us
    all_to_all x1, starting transfers between devices, body(): got = lax.all_to_all(ws, 'y', split_axis=0, concat_axis=0, tiled=True)  4.91 us
    all_to_all x1, starting transfers between devices, body(): lax.all_to_all(back, 'y', split_axis=0, concat_axis=0, tiled=True)  4.81 us
    ppermute x3, waiting for transfers between devices, body(): other = lax.ppermute(held.astype(BF16), 'z', route).astype(F32)  3.12 us
  transfers between devices with their start and end apart: 23, of which 5 were waited for; matrix products, arithmetic and copies ran while one was open for 6% of the time, Pallas kernels for 29%

profile of v1, /device:TPU:10, one launch (start us, length us, event | category | flops | bytes accessed | tf_op | source)
XLA Modules:
  0.0 122.3 jit_solution(7612117955394071960)
XLA Ops:
  0.7 1.6 %fusion.18 = (bf16[4,128,128]{2,1,0:T(8,128)(2,1)S(1)}, f32[4,128,128]{2,1,0:T(8,128)S(1)}) fusion(bf16[512,4,128]{2,1,0:T(4,128)(2,1)} %v_ref.5, bf16[512,4,128]{2,1,0:T(4,128)(2,1)} %k_ref.5), kind=kOutput, calls=%fused_computation.34 | convolution fusion | flops 67174400 | bytes 1441792 | tf_op jit(solution)/shard_map/gpl,gpq->plq/dot_general | solution.py:270
  2.9 1.5 %collective-permute-start.13 = (bf16[512,512]{1,0:T(8,128)(2,1)S(1)}, bf16[512,512]{1,0:T(8,128)(2,1)S(1)}, u32[]{:S(2)}, u32[]{:S(2)}) collective-permute-start(bf16[512,512]{1,0:T(8,128)(2,1)S(1)} %copy-done.12), channel_id=1, source_target_pairs={{0,2},{2,4},{4,6},{6,0},{1,3},{3,5},{5,7},{7,1},{8,10},{10,12},{12... | collective-permute-start | bytes 1572872 | tf_op jit(solution)/shard_map/ppermute | solution.py:266
  4.4 0.8 collective-permute-start.15
  5.1 3.1 %collective-permute-done.r0 = bf16[4,128,128]{2,1,0:T(8,128)(2,1)S(1)} collective-permute-done((bf16[4,128,128]{2,1,0:T(8,128)(2,1)S(1)}, bf16[4,128,128]{2,1,0:T(8,128)(2,1)S(1)}, u32[]{:S(2)}, u32[]{:S(2)}) %collective-permute-start) | collective-permute-done | bytes 131104 | tf_op jit(solution)/shard_map/ppermute | solution.py:276
  8.3 2.4 %collective-permute-start.1 = (bf16[4,128,128]{2,1,0:T(8,128)(2,1)S(1)}, bf16[4,128,128]{2,1,0:T(8,128)(2,1)S(1)}, u32[]{:S(2)}, u32[]{:S(2)}) collective-permute-start(bf16[4,128,128]{2,1,0:T(8,128)(2,1)S(1)} %fusion.3), channel_id=1, source_target_pairs={{0,16},{8,24},{16,0},{24,8},{1,17},{9,25},{17,1},{25,9},{2,18},{10... | collective-permute-start | bytes 393224 | tf_op jit(solution)/shard_map/ppermute | solution.py:276
  10.7 4.2 %collective-permute-done.1.r1 = bf16[4,128,128]{2,1,0:T(8,128)(2,1)S(1)} collective-permute-done((bf16[4,128,128]{2,1,0:T(8,128)(2,1)S(1)}, bf16[4,128,128]{2,1,0:T(8,128)(2,1)S(1)}, u32[]{:S(2)}, u32[]{:S(2)}) %collective-permute-start.1) | collective-permute-done | bytes 131104 | tf_op jit(solution)/shard_map/ppermute | solution.py:276
  15.0 2.0 %collective-permute-start.2 = (bf16[4,128,128]{2,1,0:T(8,128)(2,1)S(1)}, bf16[4,128,128]{2,1,0:T(8,128)(2,1)S(1)}, u32[]{:S(2)}, u32[]{:S(2)}) collective-permute-start(bf16[4,128,128]{2,1,0:T(8,128)(2,1)S(1)} %fusion.15), channel_id=1, source_target_pairs={{0,32},{32,0},{64,96},{96,64},{128,160},{160,128},{192,224},{224,1... | collective-permute-start | bytes 393224 | tf_op jit(solution)/shard_map/ppermute | solution.py:276
  17.4 1.2 %collective-permute-start.14 = (bf16[256,512]{1,0:T(8,128)(2,1)S(1)}, bf16[256,512]{1,0:T(8,128)(2,1)S(1)}, u32[]{:S(2)}, u32[]{:S(2)}) collective-permute-start(bf16[256,512]{1,0:T(8,128)(2,1)S(1)} %slice.52), channel_id=1, source_target_pairs={{0,2},{2,4},{4,6},{6,0},{1,3},{3,5},{5,7},{7,1},{8,10},{10,12},{12... | collective-permute-start | bytes 786440 | tf_op jit(solution)/shard_map/ppermute | solution.py:294
  18.7 1.9 %collective-permute-start.16 = (bf16[256,512]{1,0:T(8,128)(2,1)S(1)}, bf16[256,512]{1,0:T(8,128)(2,1)S(1)}, u32[]{:S(2)}, u32[]{:S(2)}) collective-permute-start(bf16[256,512]{1,0:T(8,128)(2,1)S(1)} %slice.53), channel_id=1, source_target_pairs={{0,6},{2,0},{4,2},{6,4},{1,7},{3,1},{5,3},{7,5},{8,14},{10,8},{12,... | collective-permute-start | bytes 786440 | tf_op jit(solution)/shard_map/ppermute | solution.py:295
  20.6 2.8 %collective-permute-start.3 = (bf16[4,128,128]{2,1,0:T(8,128)(2,1)S(1)}, bf16[4,128,128]{2,1,0:T(8,128)(2,1)S(1)}, u32[]{:S(2)}, u32[]{:S(2)}) collective-permute-start(bf16[4,128,128]{2,1,0:T(8,128)(2,1)S(1)} %fusion.4), channel_id=1, source_target_pairs={{0,64},{32,96},{64,0},{96,32},{128,192},{160,224},{192,128},{224,1... | collective-permute-start | bytes 393224 | tf_op jit(solution)/shard_map/ppermute | solution.py:276
  23.4 2.2 %copy-done = bf16[4,128,4096]{2,1,0:T(8,128)(2,1)S(1)} copy-done((bf16[4,128,4096]{2,1,0:T(8,128)(2,1)S(1)}, bf16[4,128,4096]{2,1,0:T(8,128)(2,1)}, u32[]{:S(2)}) %copy-start) | copy-done | bytes 4194328
  25.6 1.0 copy-done.13
  26.7 4.0 %shard_map.107 = (f32[512,512]{1,0:T(8,128)S(1)}, f32[512,512]{1,0:T(8,128)S(1)}) custom-call(s32[4]{0:T(128)S(1)} %fusion.14.idx_ref, bf16[512,512]{1,0:T(8,128)(2,1)S(1)} %copy-done.13, bf16[512,512]{1,0:T(8,128)(2,1)S(1)} %collective-permute-done.13.gl, bf16[512,512]{1,0:T(8,128)(2,1)S(1)} %collective-permute-done.15.gr, bf16[512,4096]{1,0:T(8,128)(2,1)S(1)} %bitcast.33, ...), custom_call_target="tpu_custom_call" | custom-call | flops 1610612736 | bytes 12058640 | tf_op jit(solution)/shard_map/pallas_call | solution.py:240
  30.7 1.0 copy-done.10
  31.7 3.6 %shard_map.109 = bf16[512,512]{1,0:T(8,128)(2,1)} custom-call(s32[4]{0:T(128)S(1)} %fusion.14.idx_ref, bf16[256,512]{1,0:T(8,128)(2,1)S(1)} %collective-permute-done.14.top, bf16[256,512]{1,0:T(8,128)(2,1)S(1)} %collective-permute-done.16.bot, f32[512,512]{1,0:T(8,128)S(1)} %get-tuple-element.36.acc, bf16[512,4096]{1,0:T(8,128)(2,1)} %collective-permute-done.6.p_ref.w_ref), custom_call_target="tpu_custom_call" | custom-call | flops 268435456 | bytes 6291472 | tf_op jit(solution)/shard_map/pallas_call | solution.py:240
  35.4 7.3 %collective-permute-start.4 = (bf16[4,128,128]{2,1,0:T(8,128)(2,1)S(1)}, bf16[4,128,128]{2,1,0:T(8,128)(2,1)S(1)}, u32[]{:S(2)}, u32[]{:S(2)}) collective-permute-start(bf16[4,128,128]{2,1,0:T(8,128)(2,1)S(1)} %add_convert_fusion.2), channel_id=1, source_target_pairs={{0,128},{32,160},{64,192},{96,224},{1,129},{33,161},{65,193},{97,2... | collective-permute-start | bytes 393224 | tf_op jit(solution)/shard_map/ppermute | solution.py:276
  42.9 2.3 %shard_map.101 = (f32[512,512]{1,0:T(8,128)S(1)}, bf16[4,640,512]{2,1,0:T(8,128)(2,1)S(1)}) custom-call(bf16[512,4,128]{2,1,0:T(4,128)(2,1)S(1)} %copy-done.14, bf16[512,4,128]{2,1,0:T(4,128)(2,1)S(1)} %copy-done.4, bf16[512,4,128]{2,1,0:T(4,128)(2,1)S(1)} %copy-done.5, f32[15,4,512]{2,1,0:T(4,128)S(1)} %copy-done.20), custom_call_target="tpu_custom_call" | custom-call | flops 536870912 | bytes 5365760 | tf_op jit(solution)/shard_map/pallas_call | solution.py:240
  45.2 1.0 collective-permute-done.4.r4
  46.2 1.4 %shard_map.102.a = bf16[512,512]{1,0:T(8,128)(2,1)S(1)} custom-call(f32[5]{0:T(128)S(1)} %convert_element_type.67.m_ref, f32[512,512]{1,0:T(8,128)S(1)} %get-tuple-element.26.lo_ref, bf16[4,640,512]{2,1,0:T(8,128)(2,1)S(1)} %get-tuple-element.27.wq_ref, bf16[4,128,128]{2,1,0:T(8,128)(2,1)S(1)} %collective-permute-done.r0, ...), custom_call_target="tpu_custom_call" | custom-call | flops 335544320 | bytes 4849684 | tf_op jit(solution)/shard_map/pallas_call | solution.py:240
  48.3 1.0 shard_map.108.own_ref
  49.4 2.8 %shard_map.110 = (bf16[512,512]{1,0:T(8,128)(2,1)S(1)}, bf16[4,640,128]{2,1,0:T(8,128)(2,1)}) custom-call(f32[512,512]{1,0:T(8,128)S(1)} %shard_map.108.own_ref, bf16[512,512]{1,0:T(8,128)(2,1)} %collective-permute-done.17.rec_ref, bf16[4,640,512]{2,1,0:T(8,128)(2,1)S(1)} %get-tuple-element.27.wq_ref), custom_call_target="tpu_custom_call" | custom-call | flops 335544320 | bytes 5373952 | tf_op jit(solution)/shard_map/pallas_call | solution.py:240
  52.2 0.8 copy-done.16
  53.0 4.9 %all-to-all-start = ((bf16[4,640,128]{2,1,0:T(8,128)(2,1)}), bf16[4,640,128]{2,1,0:T(8,128)(2,1)}, u32[]{:S(2)}, u32[]{:S(2)}) async-start(bf16[4,640,128]{2,1,0:T(8,128)(2,1)} %get-tuple-element.43), calls=%async_computation | async-start | bytes 1310720 | tf_op jit(solution)/shard_map/all_to_all | solution.py:318
  57.9 2.2 %copy-done.2 = bf16[4,128,4096]{2,1,0:T(8,128)(2,1)S(1)} copy-done((bf16[4,128,4096]{2,1,0:T(8,128)(2,1)S(1)}, bf16[4,128,4096]{2,1,0:T(8,128)(2,1)}, u32[]{:S(2)}) %copy-start.2) | copy-done | bytes 4194328
  60.1 3.6 %shard_map.104 = (bf16[256,512]{1,0:T(8,128)(2,1)S(1)}, bf16[256,512]{1,0:T(8,128)(2,1)}) custom-call(s32[4]{0:T(128)S(1)} %fusion.14.idx_ref, bf16[512,512]{1,0:T(8,128)(2,1)S(1)} %shard_map.102.a, bf16[512,512]{1,0:T(8,128)(2,1)S(1)} %collective-permute-done.5.ap, bf16[512,4096]{1,0:T(8,128)(2,1)S(1)} %bitcast.35, ...), custom_call_target="tpu_custom_call" | custom-call | flops 536870912 | bytes 9961488 | tf_op jit(solution)/shard_map/pallas_call | solution.py:240
  63.7 1.5 %collective-permute-start.7 = (bf16[256,512]{1,0:T(8,128)(2,1)S(1)}, bf16[256,512]{1,0:T(8,128)(2,1)}, u32[]{:S(2)}, u32[]{:S(2)}) collective-permute-start(bf16[256,512]{1,0:T(8,128)(2,1)S(1)} %get-tuple-element.30), channel_id=1, source_target_pairs={{0,2},{2,4},{4,6},{6,0},{1,3},{3,5},{5,7},{7,1},{8,10},{10,12},{12... | collective-permute-start | bytes 786440 | tf_op jit(solution)/shard_map/ppermute | solution.py:345
  65.2 3.6 %shard_map.105 = (bf16[256,512]{1,0:T(8,128)(2,1)}, bf16[256,512]{1,0:T(8,128)(2,1)}) custom-call(s32[4]{0:T(128)S(1)} %fusion.14.idx_ref, bf16[512,512]{1,0:T(8,128)(2,1)S(1)} %shard_map.102.a, bf16[512,512]{1,0:T(8,128)(2,1)S(1)} %collective-permute-done.5.ap, bf16[512,4096]{1,0:T(8,128)(2,1)S(1)} %bitcast.36, ...), custom_call_target="tpu_custom_call" | custom-call | flops 536870912 | bytes 9961488 | tf_op jit(solution)/shard_map/pallas_call | solution.py:240
  68.8 1.2 collective-permute-start.9
  70.0 0.8 collective-permute-start.10
  70.8 2.6 %collective-permute-start.11 = (bf16[256,512]{1,0:T(8,128)(2,1)}, bf16[256,512]{1,0:T(8,128)(2,1)}, u32[]{:S(2)}, u32[]{:S(2)}) collective-permute-start(bf16[256,512]{1,0:T(8,128)(2,1)} %get-tuple-element.34), channel_id=1, source_target_pairs={{0,6},{2,0},{4,2},{6,4},{1,7},{3,1},{5,3},{7,5},{8,14},{10,8},{12,... | collective-permute-start | bytes 786440 | tf_op jit(solution)/shard_map/ppermute | solution.py:346
  73.4 1.2 convert.17
  74.7 3.9 %collective-permute-start.18 = (bf16[3,128,128]{2,1,0:T(8,128)(2,1)S(1)}, bf16[3,128,128]{2,1,0:T(8,128)(2,1)S(1)}, u32[]{:S(2)}, u32[]{:S(2)}) collective-permute-start(bf16[3,128,128]{2,1,0:T(8,128)(2,1)S(1)} %convert_element_type.83), channel_id=1, source_target_pairs={{0,32},{32,0},{64,96},{96,64},{128,160},{160,128},{192,224},{224,1... | collective-permute-start | bytes 294920 | tf_op jit(solution)/shard_map/ppermute | solution.py:326
  78.7 2.2 %copy-done.3 = bf16[4,128,4096]{2,1,0:T(8,128)(2,1)S(1)} copy-done((bf16[4,128,4096]{2,1,0:T(8,128)(2,1)S(1)}, bf16[4,128,4096]{2,1,0:T(8,128)(2,1)}, u32[]{:S(2)}) %copy-start.3) | copy-done | bytes 4194328
  80.8 3.5 %shard_map.103 = (f32[256,512]{1,0:T(8,128)S(1)}, f32[256,512]{1,0:T(8,128)S(1)}, f32[512,512]{1,0:T(8,128)S(1)}) custom-call(s32[4]{0:T(128)S(1)} %fusion.14.idx_ref, bf16[512,512]{1,0:T(8,128)(2,1)S(1)} %shard_map.102.a, bf16[512,512]{1,0:T(8,128)(2,1)S(1)} %collective-permute-done.5.ap, bf16[512,4096]{1,0:T(8,128)(2,1)S(1)} %bitcast.37, ...), custom_call_target="tpu_custom_call" | custom-call | flops 1073741824 | bytes 11534352 | tf_op jit(solution)/shard_map/pallas_call | solution.py:240
  84.9 1.7 %add_convert_fusion.1 = bf16[256,512]{1,0:T(8,128)(2,1)} fusion(f32[256,512]{1,0:T(8,128)S(1)} %get-tuple-element.29, bf16[256,512]{1,0:T(8,128)(2,1)} %collective-permute-done.7), kind=kLoop, calls=%fused_computation.5 | loop fusion | flops 393216 | bytes 1048576 | tf_op jit(solution)/shard_map/convert_element_type | solution.py:353
  86.7 3.1 %collective-permute-done.19 = bf16[2,128,128]{2,1,0:T(8,128)(2,1)S(1)} collective-permute-done((bf16[2,128,128]{2,1,0:T(8,128)(2,1)S(1)}, bf16[2,128,128]{2,1,0:T(8,128)(2,1)S(1)}, u32[]{:S(2)}, u32[]{:S(2)}) %collective-permute-start.19) | collective-permute-done | bytes 65568 | tf_op jit(solution)/shard_map/ppermute | solution.py:326
  89.8 6.5 %collective-permute-start.20 = (bf16[1,128,128]{2,1,0:T(8,128)(2,1)S(1)}, bf16[1,128,128]{2,1,0:T(8,128)(2,1)S(1)}, u32[]{:S(2)}, u32[]{:S(2)}) collective-permute-start(bf16[1,128,128]{2,1,0:T(8,128)(2,1)S(1)} %fusion.7), channel_id=1, source_target_pairs={{0,128},{32,160},{64,192},{96,224},{128,0},{160,32},{192,64},{224,... | collective-permute-start | bytes 98312 | tf_op jit(solution)/shard_map/ppermute | solution.py:326
  96.3 1.7 %add_convert_fusion = bf16[256,512]{1,0:T(8,128)(2,1)} fusion(f32[256,512]{1,0:T(8,128)S(1)} %get-tuple-element.33, bf16[256,512]{1,0:T(8,128)(2,1)} %collective-permute-done.11), kind=kLoop, calls=%fused_computation.4 | loop fusion | flops 393216 | bytes 1048576 | tf_op jit(solution)/shard_map/convert_element_type | solution.py:354
  98.1 2.0 %collective-permute-start.12 = (bf16[256,512]{1,0:T(8,128)(2,1)}, bf16[256,512]{1,0:T(8,128)(2,1)}, u32[]{:S(2)}, u32[]{:S(2)}) collective-permute-start(bf16[256,512]{1,0:T(8,128)(2,1)} %add_convert_fusion), channel_id=1, source_target_pairs={{0,6},{2,0},{4,2},{6,4},{1,7},{3,1},{5,3},{7,5},{8,14},{10,8},{12,... | collective-permute-start | bytes 786440 | tf_op jit(solution)/shard_map/ppermute | solution.py:356
  100.8 4.8 %all-to-all-start.1 = ((bf16[4,128,128]{2,1,0:T(8,128)(2,1)}), bf16[4,128,128]{2,1,0:T(8,128)(2,1)}, u32[]{:S(2)}, u32[]{:S(2)}) async-start(bf16[4,128,128]{2,1,0:T(8,128)(2,1)} %pad_maximum_fusion), calls=%async_computation.1 | async-start | bytes 262144 | tf_op jit(solution)/shard_map/all_to_all | solution.py:330
  105.6 1.0 copy-done.17
  106.7 0.9 copy-done.21
  107.6 4.8 %shard_map.111 = (f32[512,512]{1,0:T(8,128)S(1)}, f32[512,512]{1,0:T(8,128)S(1)}, f32[512,512]{1,0:T(8,128)S(1)}, f32[10,4,512]{2,1,0:T(4,128)S(1)}) custom-call(bf16[512,4,128]{2,1,0:T(4,128)(2,1)S(1)} %copy-done.15, bf16[512,4,128]{2,1,0:T(4,128)(2,1)S(1)} %copy-done.4, bf16[512,4,128]{2,1,0:T(4,128)(2,1)S(1)} %copy-done.5, ...), custom_call_target="tpu_custom_call" | custom-call | flops 1342177280 | bytes 5447680 | tf_op jit(solution)/shard_map/pallas_call | solution.py:240
  112.4 1.0 copy-done.6
  113.4 2.7 %shard_map.112 = (bf16[512,4,128]{2,1,0:T(4,128)(2,1)}, f32[15,4,512]{2,1,0:T(4,128)}) custom-call(f32[5]{0:T(128)S(1)} %convert_element_type.67.m_ref, bf16[512,4,128]{2,1,0:T(4,128)(2,1)S(1)} %copy-done.15, bf16[512,512]{1,0:T(8,128)(2,1)S(1)} %copy-done.17, f32[15,4,512]{2,1,0:T(4,128)S(1)} %copy-done.22, f32[512,512]{1,0:T(8,128)S(1)} %get-tuple-element.38.dql_ref, ...), custom_call_target="tpu_custom_call" | custom-call | flops 335544320 | bytes 3604500 | tf_op jit(solution)/shard_map/pallas_call | solution.py:240
  116.8 0.9 copy-done.19
  117.7 2.2 %shard_map.106 = bf16[512,512]{1,0:T(8,128)(2,1)} custom-call(f32[512,512]{1,0:T(8,128)S(1)} %copy-done.9, bf16[256,512]{1,0:T(8,128)(2,1)} %collective-permute-done.8.lt, bf16[256,512]{1,0:T(8,128)(2,1)S(1)} %copy-done.19, bf16[256,512]{1,0:T(8,128)(2,1)} %collective-permute-done.10.rt, bf16[256,512]{1,0:T(8,128)(2,1)} %collective-permute-done.12.rb), custom_call_target="tpu_custom_call" | custom-call | flops 1048576 | bytes 2621440 | tf_op jit(solution)/shard_map/pallas_call | solution.py:240
  119.9 2.4 %shard_map.113 = (bf16[512,4,128]{2,1,0:T(4,128)(2,1)}, bf16[512,4,128]{2,1,0:T(4,128)(2,1)}) custom-call(f32[512,512]{1,0:T(8,128)S(1)} %get-tuple-element.41.dkl_ref, f32[512,512]{1,0:T(8,128)S(1)} %copy-done.7, bf16[512,4,128]{2,1,0:T(4,128)(2,1)S(1)} %copy-done.4, bf16[512,4,128]{2,1,0:T(4,128)(2,1)S(1)} %copy-done.5, ...), custom_call_target="tpu_custom_call" | custom-call | flops 134217728 | bytes 4325376 | tf_op jit(solution)/shard_map/pallas_call | solution.py:240
  (79 shorter events, 4.3 us)
Async XLA Ops:
  0.6 2.2 %copy-start.12 = (bf16[512,512]{1,0:T(8,128)(2,1)S(1)}, bf16[512,512]{1,0:T(8,128)(2,1)}, u32[]{:S(2)}) copy-start(bf16[512,512]{1,0:T(8,128)(2,1)} %go.1) | copy-start | bytes 1572868
  0.6 22.8 %collective-permute-start.6 = (bf16[512,4096]{1,0:T(8,128)(2,1)}, bf16[512,4096]{1,0:T(8,128)(2,1)}, u32[]{:S(2)}, u32[]{:S(2)}) collective-permute-start(bf16[512,4096]{1,0:T(8,128)(2,1)} %bitcast.32), channel_id=1, source_target_pairs={{0,1},{1,0},{2,3},{3,2},{4,5},{5,4},{6,7},{7,6},{8,9},{9,8},{10,11... | collective-permute-start | bytes 12582920 | tf_op jit(solution)/shard_map/ppermute | solution.py:268
  2.3 5.9 %collective-permute-start = (bf16[4,128,128]{2,1,0:T(8,128)(2,1)S(1)}, bf16[4,128,128]{2,1,0:T(8,128)(2,1)S(1)}, u32[]{:S(2)}, u32[]{:S(2)}) collective-permute-start(bf16[4,128,128]{2,1,0:T(8,128)(2,1)S(1)} %get-tuple-element.54), channel_id=1, source_target_pairs={{0,8},{8,0},{16,24},{24,16},{1,9},{9,1},{17,25},{25,17},{2,10},{10... | collective-permute-start | bytes 393224 | tf_op jit(solution)/shard_map/ppermute | solution.py:276
  2.9 14.5 %collective-permute-start.13 = (bf16[512,512]{1,0:T(8,128)(2,1)S(1)}, bf16[512,512]{1,0:T(8,128)(2,1)S(1)}, u32[]{:S(2)}, u32[]{:S(2)}) collective-permute-start(bf16[512,512]{1,0:T(8,128)(2,1)S(1)} %copy-done.12), channel_id=1, source_target_pairs={{0,2},{2,4},{4,6},{6,0},{1,3},{3,5},{5,7},{7,1},{8,10},{10,12},{12... | collective-permute-start | bytes 1572872 | tf_op jit(solution)/shard_map/ppermute | solution.py:266
  4.4 14.3 %collective-permute-start.15 = (bf16[512,512]{1,0:T(8,128)(2,1)S(1)}, bf16[512,512]{1,0:T(8,128)(2,1)S(1)}, u32[]{:S(2)}, u32[]{:S(2)}) collective-permute-start(bf16[512,512]{1,0:T(8,128)(2,1)S(1)} %copy-done.12), channel_id=1, source_target_pairs={{0,6},{2,0},{4,2},{6,4},{1,7},{3,1},{5,3},{7,5},{8,14},{10,8},{12,... | collective-permute-start | bytes 1572872 | tf_op jit(solution)/shard_map/ppermute | solution.py:267
  8.3 6.6 %collective-permute-start.1 = (bf16[4,128,128]{2,1,0:T(8,128)(2,1)S(1)}, bf16[4,128,128]{2,1,0:T(8,128)(2,1)S(1)}, u32[]{:S(2)}, u32[]{:S(2)}) collective-permute-start(bf16[4,128,128]{2,1,0:T(8,128)(2,1)S(1)} %fusion.3), channel_id=1, source_target_pairs={{0,16},{8,24},{16,0},{24,8},{1,17},{9,25},{17,1},{25,9},{2,18},{10... | collective-permute-start | bytes 393224 | tf_op jit(solution)/shard_map/ppermute | solution.py:276
  15.0 5.6 %collective-permute-start.2 = (bf16[4,128,128]{2,1,0:T(8,128)(2,1)S(1)}, bf16[4,128,128]{2,1,0:T(8,128)(2,1)S(1)}, u32[]{:S(2)}, u32[]{:S(2)}) collective-permute-start(bf16[4,128,128]{2,1,0:T(8,128)(2,1)S(1)} %fusion.15), channel_id=1, source_target_pairs={{0,32},{32,0},{64,96},{96,64},{128,160},{160,128},{192,224},{224,1... | collective-permute-start | bytes 393224 | tf_op jit(solution)/shard_map/ppermute | solution.py:276
  17.4 14.3 %collective-permute-start.14 = (bf16[256,512]{1,0:T(8,128)(2,1)S(1)}, bf16[256,512]{1,0:T(8,128)(2,1)S(1)}, u32[]{:S(2)}, u32[]{:S(2)}) collective-permute-start(bf16[256,512]{1,0:T(8,128)(2,1)S(1)} %slice.52), channel_id=1, source_target_pairs={{0,2},{2,4},{4,6},{6,0},{1,3},{3,5},{5,7},{7,1},{8,10},{10,12},{12... | collective-permute-start | bytes 786440 | tf_op jit(solution)/shard_map/ppermute | solution.py:294
  18.7 13.0 %collective-permute-start.16 = (bf16[256,512]{1,0:T(8,128)(2,1)S(1)}, bf16[256,512]{1,0:T(8,128)(2,1)S(1)}, u32[]{:S(2)}, u32[]{:S(2)}) collective-permute-start(bf16[256,512]{1,0:T(8,128)(2,1)S(1)} %slice.53), channel_id=1, source_target_pairs={{0,6},{2,0},{4,2},{6,4},{1,7},{3,1},{5,3},{7,5},{8,14},{10,8},{12,... | collective-permute-start | bytes 786440 | tf_op jit(solution)/shard_map/ppermute | solution.py:295
  20.6 14.7 %collective-permute-start.3 = (bf16[4,128,128]{2,1,0:T(8,128)(2,1)S(1)}, bf16[4,128,128]{2,1,0:T(8,128)(2,1)S(1)}, u32[]{:S(2)}, u32[]{:S(2)}) collective-permute-start(bf16[4,128,128]{2,1,0:T(8,128)(2,1)S(1)} %fusion.4), channel_id=1, source_target_pairs={{0,64},{32,96},{64,0},{96,32},{128,192},{160,224},{192,128},{224,1... | collective-permute-start | bytes 393224 | tf_op jit(solution)/shard_map/ppermute | solution.py:276
  23.4 2.2 %copy-start = (bf16[4,128,4096]{2,1,0:T(8,128)(2,1)S(1)}, bf16[4,128,4096]{2,1,0:T(8,128)(2,1)}, u32[]{:S(2)}) copy-start(bf16[4,128,4096]{2,1,0:T(8,128)(2,1)} %param.10) | copy-start | bytes 12582916
  25.6 1.0 copy-start.13
  30.7 1.0 copy-start.10
  31.7 11.1 %copy-start.4 = (bf16[512,4,128]{2,1,0:T(4,128)(2,1)S(1)}, bf16[512,4,128]{2,1,0:T(4,128)(2,1)}, u32[]{:S(2)}) copy-start(bf16[512,4,128]{2,1,0:T(4,128)(2,1)} %k_ref.5) | copy-start | bytes 1572868
  31.7 11.1 %copy-start.5 = (bf16[512,4,128]{2,1,0:T(4,128)(2,1)S(1)}, bf16[512,4,128]{2,1,0:T(4,128)(2,1)}, u32[]{:S(2)}) copy-start(bf16[512,4,128]{2,1,0:T(4,128)(2,1)} %v_ref.5) | copy-start | bytes 1572868
  31.7 11.1 %copy-start.14 = (bf16[512,4,128]{2,1,0:T(4,128)(2,1)S(1)}, bf16[512,4,128]{2,1,0:T(4,128)(2,1)}, u32[]{:S(2)}) copy-start(bf16[512,4,128]{2,1,0:T(4,128)(2,1)} %q_ref.5) | copy-start | bytes 1572868
  31.7 11.1 %copy-start.20 = (f32[15,4,512]{2,1,0:T(4,128)S(1)}, f32[15,4,512]{2,1,0:T(4,128)}, u32[]{:S(2)}) copy-start(f32[15,4,512]{2,1,0:T(4,128)} %lw_ref.5) | copy-start | bytes 368644
  35.3 14.0 %collective-permute-start.17 = (bf16[512,512]{1,0:T(8,128)(2,1)}, bf16[512,512]{1,0:T(8,128)(2,1)}, u32[]{:S(2)}, u32[]{:S(2)}) collective-permute-start(bf16[512,512]{1,0:T(8,128)(2,1)} %shard_map.109), channel_id=1, source_target_pairs={{0,1},{1,0},{2,3},{3,2},{4,5},{5,4},{6,7},{7,6},{8,9},{9,8},{10,11... | collective-permute-start | bytes 1572872 | tf_op jit(solution)/shard_map/ppermute | solution.py:307
  35.4 10.7 %collective-permute-start.4 = (bf16[4,128,128]{2,1,0:T(8,128)(2,1)S(1)}, bf16[4,128,128]{2,1,0:T(8,128)(2,1)S(1)}, u32[]{:S(2)}, u32[]{:S(2)}) collective-permute-start(bf16[4,128,128]{2,1,0:T(8,128)(2,1)S(1)} %add_convert_fusion.2), channel_id=1, source_target_pairs={{0,128},{32,160},{64,192},{96,224},{1,129},{33,161},{65,193},{97,2... | collective-permute-start | bytes 393224 | tf_op jit(solution)/shard_map/ppermute | solution.py:276
  42.9 5.0 %copy-start.11 = (f32[512,512]{1,0:T(8,128)S(1)}, f32[512,512]{1,0:T(8,128)}, u32[]{:S(2)}) copy-start(f32[512,512]{1,0:T(8,128)} %copy-done.10) | copy-start | bytes 3145732
  46.1 2.2 %copy-start.1 = (bf16[4,128,4096]{2,1,0:T(8,128)(2,1)S(1)}, bf16[4,128,4096]{2,1,0:T(8,128)(2,1)}, u32[]{:S(2)}) copy-start(bf16[4,128,4096]{2,1,0:T(8,128)(2,1)} %param.10) | copy-start | bytes 12582916
  47.6 10.3 %collective-permute-start.5 = (bf16[512,512]{1,0:T(8,128)(2,1)S(1)}, bf16[512,512]{1,0:T(8,128)(2,1)S(1)}, u32[]{:S(2)}, u32[]{:S(2)}) collective-permute-start(bf16[512,512]{1,0:T(8,128)(2,1)S(1)} %shard_map.102.a), channel_id=1, source_target_pairs={{0,1},{1,0},{2,3},{3,2},{4,5},{5,4},{6,7},{7,6},{8,9},{9,8},{10,11... | collective-permute-start | bytes 1572872 | tf_op jit(solution)/shard_map/ppermute | solution.py:339
  52.2 0.8 copy-start.16
  53.0 20.5 %all-to-all-start = ((bf16[4,640,128]{2,1,0:T(8,128)(2,1)}), bf16[4,640,128]{2,1,0:T(8,128)(2,1)}, u32[]{:S(2)}, u32[]{:S(2)}) async-start(bf16[4,640,128]{2,1,0:T(8,128)(2,1)} %get-tuple-element.43), calls=%async_computation | async-start | bytes 1310720 | tf_op jit(solution)/shard_map/all_to_all | solution.py:318
  57.9 2.2 %copy-start.2 = (bf16[4,128,4096]{2,1,0:T(8,128)(2,1)S(1)}, bf16[4,128,4096]{2,1,0:T(8,128)(2,1)}, u32[]{:S(2)}) copy-start(bf16[4,128,4096]{2,1,0:T(8,128)(2,1)} %param.10) | copy-start | bytes 12582916
  63.7 21.3 %collective-permute-start.7 = (bf16[256,512]{1,0:T(8,128)(2,1)S(1)}, bf16[256,512]{1,0:T(8,128)(2,1)}, u32[]{:S(2)}, u32[]{:S(2)}) collective-permute-start(bf16[256,512]{1,0:T(8,128)(2,1)S(1)} %get-tuple-element.30), channel_id=1, source_target_pairs={{0,2},{2,4},{4,6},{6,0},{1,3},{3,5},{5,7},{7,1},{8,10},{10,12},{12... | collective-permute-start | bytes 786440 | tf_op jit(solution)/shard_map/ppermute | solution.py:345
  68.8 47.3 %collective-permute-start.9 = (bf16[256,512]{1,0:T(8,128)(2,1)}, bf16[256,512]{1,0:T(8,128)(2,1)S(1)}, u32[]{:S(2)}, u32[]{:S(2)}) collective-permute-start(bf16[256,512]{1,0:T(8,128)(2,1)} %get-tuple-element.31), channel_id=1, source_target_pairs={{0,2},{2,4},{4,6},{6,0},{1,3},{3,5},{5,7},{7,1},{8,10},{10,12},{12... | collective-permute-start | bytes 786440 | tf_op jit(solution)/shard_map/ppermute | solution.py:348
  70.0 46.8 %collective-permute-start.10 = (bf16[256,512]{1,0:T(8,128)(2,1)}, bf16[256,512]{1,0:T(8,128)(2,1)}, u32[]{:S(2)}, u32[]{:S(2)}) collective-permute-start(bf16[256,512]{1,0:T(8,128)(2,1)} %get-tuple-element.32), channel_id=1, source_target_pairs={{0,6},{2,0},{4,2},{6,4},{1,7},{3,1},{5,3},{7,5},{8,14},{10,8},{12,... | collective-permute-start | bytes 786440 | tf_op jit(solution)/shard_map/ppermute | solution.py:349
  70.8 25.5 %collective-permute-start.11 = (bf16[256,512]{1,0:T(8,128)(2,1)}, bf16[256,512]{1,0:T(8,128)(2,1)}, u32[]{:S(2)}, u32[]{:S(2)}) collective-permute-start(bf16[256,512]{1,0:T(8,128)(2,1)} %get-tuple-element.34), channel_id=1, source_target_pairs={{0,6},{2,0},{4,2},{6,4},{1,7},{3,1},{5,3},{7,5},{8,14},{10,8},{12,... | collective-permute-start | bytes 786440 | tf_op jit(solution)/shard_map/ppermute | solution.py:346
  74.7 9.6 %collective-permute-start.18 = (bf16[3,128,128]{2,1,0:T(8,128)(2,1)S(1)}, bf16[3,128,128]{2,1,0:T(8,128)(2,1)S(1)}, u32[]{:S(2)}, u32[]{:S(2)}) collective-permute-start(bf16[3,128,128]{2,1,0:T(8,128)(2,1)S(1)} %convert_element_type.83), channel_id=1, source_target_pairs={{0,32},{32,0},{64,96},{96,64},{128,160},{160,128},{192,224},{224,1... | collective-permute-start | bytes 294920 | tf_op jit(solution)/shard_map/ppermute | solution.py:326
  78.7 2.2 %copy-start.3 = (bf16[4,128,4096]{2,1,0:T(8,128)(2,1)S(1)}, bf16[4,128,4096]{2,1,0:T(8,128)(2,1)}, u32[]{:S(2)}) copy-start(bf16[4,128,4096]{2,1,0:T(8,128)(2,1)} %param.10) | copy-start | bytes 12582916
  84.3 13.7 %copy-start.8 = (f32[512,512]{1,0:T(8,128)}, f32[512,512]{1,0:T(8,128)S(1)}, u32[]{:S(2)}) copy-start(f32[512,512]{1,0:T(8,128)S(1)} %get-tuple-element.28.own) | copy-start | bytes 3145732
  84.4 5.4 %collective-permute-start.19 = (bf16[2,128,128]{2,1,0:T(8,128)(2,1)S(1)}, bf16[2,128,128]{2,1,0:T(8,128)(2,1)S(1)}, u32[]{:S(2)}, u32[]{:S(2)}) collective-permute-start(bf16[2,128,128]{2,1,0:T(8,128)(2,1)S(1)} %get-tuple-element.49), channel_id=1, source_target_pairs={{0,64},{32,96},{64,0},{96,32},{128,192},{160,224},{192,128},{224,1... | collective-permute-start | bytes 196616 | tf_op jit(solution)/shard_map/ppermute | solution.py:326
  86.7 30.1 %collective-permute-start.8 = (bf16[256,512]{1,0:T(8,128)(2,1)}, bf16[256,512]{1,0:T(8,128)(2,1)}, u32[]{:S(2)}, u32[]{:S(2)}) collective-permute-start(bf16[256,512]{1,0:T(8,128)(2,1)} %add_convert_fusion.1), channel_id=1, source_target_pairs={{0,2},{2,4},{4,6},{6,0},{1,3},{3,5},{5,7},{7,1},{8,10},{10,12},{12... | collective-permute-start | bytes 786440 | tf_op jit(solution)/shard_map/ppermute | solution.py:355
  89.8 15.8 %copy-start.15 = (bf16[512,4,128]{2,1,0:T(4,128)(2,1)S(1)}, bf16[512,4,128]{2,1,0:T(4,128)(2,1)}, u32[]{:S(2)}) copy-start(bf16[512,4,128]{2,1,0:T(4,128)(2,1)} %q_ref.5) | copy-start | bytes 1572868
  89.8 10.2 %collective-permute-start.20 = (bf16[1,128,128]{2,1,0:T(8,128)(2,1)S(1)}, bf16[1,128,128]{2,1,0:T(8,128)(2,1)S(1)}, u32[]{:S(2)}, u32[]{:S(2)}) collective-permute-start(bf16[1,128,128]{2,1,0:T(8,128)(2,1)S(1)} %fusion.7), channel_id=1, source_target_pairs={{0,128},{32,160},{64,192},{96,224},{128,0},{160,32},{192,64},{224,... | collective-permute-start | bytes 98312 | tf_op jit(solution)/shard_map/ppermute | solution.py:326
  98.1 18.7 %collective-permute-start.12 = (bf16[256,512]{1,0:T(8,128)(2,1)}, bf16[256,512]{1,0:T(8,128)(2,1)}, u32[]{:S(2)}, u32[]{:S(2)}) collective-permute-start(bf16[256,512]{1,0:T(8,128)(2,1)} %add_convert_fusion), channel_id=1, source_target_pairs={{0,6},{2,0},{4,2},{6,4},{1,7},{3,1},{5,3},{7,5},{8,14},{10,8},{12,... | collective-permute-start | bytes 786440 | tf_op jit(solution)/shard_map/ppermute | solution.py:356
  100.8 19.1 %all-to-all-start.1 = ((bf16[4,128,128]{2,1,0:T(8,128)(2,1)}), bf16[4,128,128]{2,1,0:T(8,128)(2,1)}, u32[]{:S(2)}, u32[]{:S(2)}) async-start(bf16[4,128,128]{2,1,0:T(8,128)(2,1)} %pad_maximum_fusion), calls=%async_computation.1 | async-start | bytes 262144 | tf_op jit(solution)/shard_map/all_to_all | solution.py:330
  105.6 1.0 copy-start.17
  106.7 0.9 copy-start.21
  107.6 5.8 %copy-start.22 = (f32[15,4,512]{2,1,0:T(4,128)S(1)}, f32[15,4,512]{2,1,0:T(4,128)}, u32[]{:S(2)}) copy-start(f32[15,4,512]{2,1,0:T(4,128)} %lw_ref.5) | copy-start | bytes 368644
  112.4 1.0 copy-start.6
  113.4 3.4 %copy-start.9 = (f32[512,512]{1,0:T(8,128)S(1)}, f32[512,512]{1,0:T(8,128)}, u32[]{:S(2)}) copy-start(f32[512,512]{1,0:T(8,128)} %copy-done.8) | copy-start | bytes 3145732
  116.1 0.7 copy-start.18
  116.8 1.0 copy-start.19
  117.7 2.2 %copy-start.7 = (f32[512,512]{1,0:T(8,128)S(1)}, f32[512,512]{1,0:T(8,128)}, u32[]{:S(2)}) copy-start(f32[512,512]{1,0:T(8,128)} %copy-done.6) | copy-start | bytes 3145732

commit v2 on v1

--- a/solution.py
+++ b/solution.py
@@ -13,6 +13,7 @@
 BLK = 128
 NEAR = 10
 FAR = 5
+NX = 4
 HD = 128
 C = [2.0 ** (-max(l - 1, 0) / 2) / math.sqrt(HD) for l in range(NEAR + FAR)]
 
@@ -120,27 +121,39 @@
                 dv_ref[pl.ds(0, n), lanes] += dot(at, g_i, NN)
 
 
-def left_stack(m_ref, r_refs, h):
+def bit_of(axis, bit):
+    return lax.rem(lax.div(lax.axis_index(axis), 1 << bit), 2)
+
+
+def tree_bits():
+    return [bit_of("y", 0), bit_of("y", 1), bit_of("z", 0), bit_of("z", 1), bit_of("z", 2)]
+
+
+def left_stack(r_refs, h):
     return jnp.concatenate(
-        [(r[h].astype(F32) * m_ref[j]).astype(BF16) for j, r in enumerate(r_refs)], axis=0
-    )
-
-
-def attend_kernel(m_ref, lo_ref, wq_ref, r0, r1, r2, r3, r4, att_ref):
+        [
+            (r[h].astype(F32) * b.astype(F32)).astype(BF16)
+            for b, r in zip(tree_bits(), r_refs, strict=True)
+        ],
+        axis=0,
+    )
+
+
+def attend_kernel(lo_ref, wq_ref, r0, r1, r2, r3, r4, att_ref):
     for h in range(wq_ref.shape[0]):
         lanes = slice(h * HD, (h + 1) * HD)
-        states = left_stack(m_ref, (r0, r1, r2, r3, r4), h)
+        states = left_stack((r0, r1, r2, r3, r4), h)
         att_ref[:, lanes] = (lo_ref[:, lanes] + dot(wq_ref[h], states, TN)).astype(BF16)
 
 
-def dq_kernel(m_ref, q_ref, g_ref, lw_ref, dql_ref, ng_ref, r0, r1, r2, r3, r4, dq_ref, gl_ref):
+def dq_kernel(q_ref, g_ref, lw_ref, dql_ref, ng_ref, r0, r1, r2, r3, r4, dq_ref, gl_ref):
     _, heads, _ = q_ref.shape
     q_all = flat(q_ref)
     outs = []
     gl_ref[pl.ds(0, NEAR)] = ng_ref[...]
     for h in range(heads):
         lanes = slice(h * HD, (h + 1) * HD)
-        states = left_stack(m_ref, (r0, r1, r2, r3, r4), h)
+        states = left_stack((r0, r1, r2, r3, r4), h)
         read = dot(states, g_ref[:, lanes], NT)
         qt = q_all[:, lanes].astype(F32).T
         total = jnp.zeros(qt.shape, F32)
@@ -155,16 +168,62 @@
     dq_ref[...] = jnp.concatenate(outs, axis=1).reshape(q_ref.shape)
 
 
-def state_kernel(own_ref, rec_ref, wq_ref, g_ref, ws_ref):
-    for h in range(wq_ref.shape[0]):
-        lanes = slice(h * HD, (h + 1) * HD)
-        g = (own_ref[:, lanes] + rec_ref[:, lanes].astype(F32)).astype(BF16)
-        g_ref[:, lanes] = g
-        ws_ref[h] = dot(wq_ref[h], g, NN).astype(BF16)
-
-
-def final_kernel(dkl_ref, dvl_ref, k_ref, v_ref, r_ref, dk_ref, dv_ref):
+def swapped(m):
+    b0, b1 = bit_of("y", 0), bit_of("y", 1)
+    low = 1 - b0 if m & 1 else b0
+    high = 1 - b1 if m & 2 else b1
+    return high * 2 + low
+
+
+def state_kernel(own_ref, rec_ref, wq_ref, g_ref, *ws_refs):
+    g_ref[...] = (own_ref[...] + rec_ref[...].astype(F32)).astype(BF16)
+    for m, ws_ref in enumerate(ws_refs):
+        h = swapped(m)
+        g = g_ref[:, pl.ds(pl.multiple_of(h * HD, HD), HD)]
+        ws_ref[...] = dot(wq_ref[h], g, NN).astype(BF16).reshape(FAR, HD, HD)
+
+
+def rsum_kernel(w0, w1, w2, w3, near_ref, held_ref, send_ref):
+    w = (w0, w1, w2, w3)
+    b0, b1 = bit_of("y", 0), bit_of("y", 1)
+    low = [(1 - b0 if n & 1 else b0).astype(F32) for n in range(4)]
+    high = [(1 - b1 if n & 2 else b1).astype(F32) for n in range(4)]
+    first = [w[n][0].astype(F32) * low[n] for n in range(4)]
+    second = [w[n][1].astype(F32) * high[n] for n in range(4)]
+    for m in range(4):
+        near_ref[m] = first[m ^ 1] + second[m ^ 2] + second[m ^ 3]
+    for j in range(2, FAR):
+        total = sum(w[n][j].astype(F32) for n in range(4))
+        held_ref[j - 2] = total
+        send_ref[j - 2] = total.astype(BF16)
+
+
+def tree0_kernel(held_ref, got_ref, acc_ref, next_ref, send_ref):
+    off = (1 - bit_of("z", 0)).astype(F32)
+    acc_ref[...] = got_ref[0].astype(F32) * off
+    for j in range(2):
+        total = held_ref[j + 1] + got_ref[j + 1].astype(F32)
+        next_ref[j] = total
+        send_ref[j] = total.astype(BF16)
+
+
+def tree1_kernel(acc_in, held_ref, got_ref, acc_ref, send_ref):
+    off = (1 - bit_of("z", 1)).astype(F32)
+    acc_ref[...] = acc_in[...] + got_ref[0].astype(F32) * off
+    send_ref[0] = (held_ref[1] + got_ref[1].astype(F32)).astype(BF16)
+
+
+def tree2_kernel(acc_in, near_ref, got_ref, *out_refs):
+    off = (1 - bit_of("z", 2)).astype(F32)
+    acc = acc_in[...] + got_ref[0].astype(F32) * off
+    for m, ref in enumerate(out_refs):
+        ref[...] = (near_ref[m] + acc).astype(BF16)
+
+
+def final_kernel(dkl_ref, dvl_ref, k_ref, v_ref, r0, r1, r2, r3, dk_ref, dv_ref, r_ref):
     k_all, v_all = flat(k_ref), flat(v_ref)
+    for m, r in enumerate((r0, r1, r2, r3)):
+        r_ref[swapped(m)] = r[...]
     dks, dvs = [], []
     for h in range(r_ref.shape[0]):
         lanes = slice(h * HD, (h + 1) * HD)
@@ -175,73 +234,77 @@
     dv_ref[...] = jnp.concatenate(dvs, axis=1).reshape(k_ref.shape)
 
 
-def wcol(ref, idx_ref, n, seg):
-    return ref[:, pl.ds(pl.multiple_of(idx_ref[n] * seg, seg), seg)]
-
-
-def mix12_kernel(idx_ref, go, gl, gr, w_ref, p_ref, own_ref, par_ref):
+def wcol(ref, n, seg):
+    steps = (0, NX - 1, 1, 2)[n]
+    at = lax.rem(lax.axis_index("x") + steps, NX) * 2 + lax.axis_index("c")
+    return ref[:, pl.ds(pl.multiple_of(at * seg, seg), seg)]
+
+
+def mix12_kernel(go, gl, gr, w_ref, p_ref, own_ref, par_ref):
     seg = go.shape[1]
     for ref, out in ((p_ref, par_ref), (w_ref, own_ref)):
         out[...] = (
-            dot(go[...], wcol(ref, idx_ref, 0, seg), NT)
-            + dot(gl[...], wcol(ref, idx_ref, 1, seg), NT)
-            + dot(gr[...], wcol(ref, idx_ref, 2, seg), NT)
+            dot(go[...], wcol(ref, 0, seg), NT)
+            + dot(gl[...], wcol(ref, 1, seg), NT)
+            + dot(gr[...], wcol(ref, 2, seg), NT)
         )
 
 
-def mix3_kernel(idx_ref, top, bot, acc, w_ref, out_ref):
+def mix3_kernel(top, bot, acc, w_ref, out_ref):
     half, seg = top.shape
-    w = wcol(w_ref, idx_ref, 3, seg)
+    w = wcol(w_ref, 3, seg)
     for base, part in ((0, top), (half, bot)):
         rows = pl.ds(base, half)
         out_ref[rows, :] = (acc[rows, :] + dot(part[...], w, NT)).astype(out_ref.dtype)
 
 
-def out_rows(idx_ref, a, ap, w_ref, p_ref, n, rows, seg):
-    return dot(a[rows, :], wcol(w_ref, idx_ref, n, seg), NN) + dot(
-        ap[rows, :], wcol(p_ref, idx_ref, n, seg), NN
-    )
-
-
-def out_far_kernel(idx_ref, a, ap, w_ref, p_ref, top_ref, bot_ref):
+def out_rows(a, ap, w_ref, p_ref, n, rows, seg):
+    return dot(a[rows, :], wcol(w_ref, n, seg), NN) + dot(
+        ap[rows, :], wcol(p_ref, n, seg), NN
+    )
+
+
+def out_far_kernel(a, ap, w_ref, p_ref, top_ref, bot_ref):
     half, seg = top_ref.shape
     for ref, base in ((top_ref, 0), (bot_ref, half)):
-        ref[...] = out_rows(idx_ref, a, ap, w_ref, p_ref, 3, pl.ds(base, half), seg).astype(BF16)
-
-
-def out_first_kernel(idx_ref, a, ap, w_ref, p_ref, r_bot, l_top):
+        ref[...] = out_rows(a, ap, w_ref, p_ref, 3, pl.ds(base, half), seg).astype(BF16)
+
+
+def out_rest_kernel(a, ap, w_ref, p_ref, r_bot, l_top, r_top, l_bot, own):
     half, seg = r_bot.shape
-    r_bot[...] = out_rows(idx_ref, a, ap, w_ref, p_ref, 2, pl.ds(half, half), seg).astype(BF16)
-    l_top[...] = out_rows(idx_ref, a, ap, w_ref, p_ref, 1, pl.ds(0, half), seg).astype(BF16)
-
-
-def out_rest_kernel(idx_ref, a, ap, w_ref, p_ref, r_top, l_bot, own):
-    half, seg = r_top.shape
-    r_top[...] = out_rows(idx_ref, a, ap, w_ref, p_ref, 2, pl.ds(0, half), seg)
-    l_bot[...] = out_rows(idx_ref, a, ap, w_ref, p_ref, 1, pl.ds(half, half), seg)
-    own[...] = out_rows(idx_ref, a, ap, w_ref, p_ref, 0, pl.ds(0, 2 * half), seg)
-
-
-def sum_kernel(own, lt, lb, rt, rb, out_ref):
-    half = lt.shape[0]
-    for base, a, b in ((0, lt, rt), (half, lb, rb)):
+    top, bot = pl.ds(0, half), pl.ds(half, half)
+    r_bot[...] = out_rows(a, ap, w_ref, p_ref, 2, bot, seg).astype(BF16)
+    l_top[...] = out_rows(a, ap, w_ref, p_ref, 1, top, seg).astype(BF16)
+    r_top[...] = out_rows(a, ap, w_ref, p_ref, 2, top, seg)
+    l_bot[...] = out_rows(a, ap, w_ref, p_ref, 1, bot, seg)
+    own[...] = out_rows(a, ap, w_ref, p_ref, 0, pl.ds(0, 2 * half), seg)
+
+
+def join_kernel(r_top, l_bot, via_l, via_r, r_out, l_out):
+    r_out[...] = (r_top[...] + via_l[...].astype(F32)).astype(BF16)
+    l_out[...] = (l_bot[...] + via_r[...].astype(F32)).astype(BF16)
+
+
+def sum_kernel(own, l_top, l_bot, r_top, r_bot, out_ref):
+    half = l_top.shape[0]
+    for base, a, b in ((0, l_top, r_top), (half, l_bot, r_bot)):
         rows = pl.ds(base, half)
         out_ref[rows, :] = (own[rows, :] + a[...].astype(F32) + b[...].astype(F32)).astype(BF16)
 
 
-SMEM = pl.BlockSpec(memory_space=pltpu.SMEM)
 VMEM = pl.BlockSpec(memory_space=pltpu.VMEM)
 
 
-def kernel_call(body, outs, operands, flops, scalars=0, vmem=16):
+def kernel_call(body, outs, operands, flops, scratch=(), vmem=16):
     out_shape = [jax.ShapeDtypeStruct(s, d) for s, d in outs]
     nbytes = sum(math.prod(s) * jnp.dtype(d).itemsize for s, d in outs)
     nbytes += sum(o.size * o.dtype.itemsize for o in operands)
     return pl.pallas_call(
         body,
-        in_specs=[SMEM] * scalars + [VMEM] * (len(operands) - scalars),
+        in_specs=[VMEM] * len(operands),
         out_specs=[VMEM] * len(outs),
         out_shape=out_shape,
+        scratch_shapes=list(scratch),
         cost_estimate=pl.CostEstimate(
             flops=int(flops), transcendentals=0, bytes_accessed=int(nbytes)
         ),
@@ -255,7 +318,6 @@
     feat = out_weight.shape[2]
     levels = level_weight.shape[0]
     half = rows // 2
-    z, y, x, c = (lax.axis_index(n) for n in ("z", "y", "x", "c"))
     nx, ny, nz = (lax.axis_size(n) for n in ("x", "y", "z"))
     right = [(i, (i + 1) % nx) for i in range(nx)]
     left = [(i, (i - 1) % nx) for i in range(nx)]
@@ -277,9 +339,6 @@
         lefts.append(got)
         if not last:
             run = run + got.astype(F32)
-    bits = [y & 1, y >> 1 & 1, z & 1, z >> 1 & 1, z >> 2 & 1]
-    mask = jnp.stack(bits).astype(F32)
-
     block = 2 * rows * rows * width
     local_out, wq = kernel_call(
         fwd_kernel,
@@ -288,70 +347,75 @@
         2 * block,
     )
 
-    xs = jnp.stack([x, (x + nx - 1) % nx, (x + 1) % nx, (x + 2) % nx])
-    idx = (xs * 2 + c).astype(jnp.int32)
-
     far_top = lax.ppermute(from_l[:half], "x", right)
     far_bot = lax.ppermute(from_r[half:], "x", left)
     mm = 2 * rows * seg * width
     own12, par12 = kernel_call(
-        mix12_kernel,
-        [((rows, width), F32)] * 2,
-        (idx, grad_out, from_l, from_r, w2, w_par),
-        6 * mm,
-        scalars=1,
+        mix12_kernel, [((rows, width), F32)] * 2, (grad_out, from_l, from_r, w2, w_par), 6 * mm
     )
     (mix_send,) = kernel_call(
-        mix3_kernel, [((rows, width), BF16)], (idx, far_top, far_bot, par12, w_par), mm, scalars=1
+        mix3_kernel, [((rows, width), BF16)], (far_top, far_bot, par12, w_par), mm
     )
     mix_got = lax.ppermute(mix_send, "c", swap)
-    (mix_own,) = kernel_call(
-        mix3_kernel, [((rows, width), F32)], (idx, far_top, far_bot, own12, w2), mm, scalars=1
-    )
-    g2, ws = kernel_call(
+    (mix_own,) = kernel_call(mix3_kernel, [((rows, width), F32)], (far_top, far_bot, own12, w2), mm)
+    square = (hd, hd)
+    g2, *ws = kernel_call(
         state_kernel,
-        [((rows, width), BF16), ((heads, FAR * hd, hd), BF16)],
+        [((rows, width), BF16)] + [((FAR, *square), BF16)] * ny,
         (mix_own, mix_got, wq),
         2 * rows * hd * hd * FAR * heads,
     )
 
-    got = lax.all_to_all(ws, "y", split_axis=0, concat_axis=0, tiled=True)
-    got = got.reshape(ny, FAR, hd, hd).astype(F32)
-    pairs = got[2, 1] + got[3, 1]
-    near = [got[1, 0] + pairs, pairs, got[3, 0], jnp.zeros_like(pairs)]
-    held = got[:, 2:].sum(axis=0)
-    acc = jnp.zeros_like(pairs)
-    for bit in range(3):
-        route = [(i, i ^ (1 << bit)) for i in range(nz)]
-        other = lax.ppermute(held.astype(BF16), "z", route).astype(F32)
-        acc = acc + jnp.where(z >> bit & 1, 0.0, other[0])
-        held = held[1:] + other[1:]
-    back = jnp.stack([part + acc for part in near]).astype(BF16)
-    right_states = lax.all_to_all(back, "y", split_axis=0, concat_axis=0, tiled=True)
+    def across_y(parts):
+        arrived = [parts[0]]
+        for m in range(1, ny):
+            arrived.append(lax.ppermute(parts[m], "y", [(i, i ^ m) for i in range(ny)]))
+        return arrived
+
+    def across_z(bit, value):
+        return lax.ppermute(value, "z", [(i, i ^ (1 << bit)) for i in range(nz)])
+
+    tiny = 8 * hd * hd
+    near, held, send = kernel_call(
+        rsum_kernel,
+        [((ny, *square), F32), ((3, *square), F32), ((3, *square), BF16)],
+        across_y(ws),
+        tiny,
+    )
+    acc, held, send = kernel_call(
+        tree0_kernel,
+        [(square, F32), ((2, *square), F32), ((2, *square), BF16)],
+        (held, across_z(0, send)),
+        tiny,
+    )
+    acc, send = kernel_call(
+        tree1_kernel, [(square, F32), ((1, *square), BF16)], (acc, held, across_z(1, send)), tiny
+    )
+    back = kernel_call(tree2_kernel, [(square, BF16)] * ny, (acc, near, across_z(2, send)), tiny)
+    right_states = across_y(back)
 
     (attended,) = kernel_call(
         attend_kernel,
         [((rows, width), BF16)],
-        (mask, local_out, wq, *lefts),
+        (local_out, wq, *lefts),
         2 * rows * hd * hd * FAR * heads,
-        scalars=1,
     )
     att_par = lax.ppermute(attended, "c", swap)
 
     piece = ((half, seg), BF16)
     piece32 = ((half, seg), F32)
-    operands = (idx, attended, att_par, w2, w_par)
-    opp_top, opp_bot = kernel_call(out_far_kernel, [piece] * 2, operands, 2 * mm, scalars=1)
+    operands = (attended, att_par, w2, w_par)
+    opp_top, opp_bot = kernel_call(out_far_kernel, [piece] * 2, operands, 2 * mm)
     via_l = lax.ppermute(opp_top, "x", right)
     via_r = lax.ppermute(opp_bot, "x", left)
-    r_bot, l_top = kernel_call(out_first_kernel, [piece] * 2, operands, 2 * mm, scalars=1)
+    r_bot, l_top, r_top, l_bot, out_own = kernel_call(
+        out_rest_kernel, [piece] * 2 + [piece32] * 2 + [((rows, seg), F32)], operands, 6 * mm
+    )
     in_l_bot = lax.ppermute(r_bot, "x", right)
     in_r_top = lax.ppermute(l_top, "x", left)
-    r_top, l_bot, out_own = kernel_call(
-        out_rest_kernel, [piece32, piece32, ((rows, seg), F32)], operands, 4 * mm, scalars=1
-    )
-    r_top = (r_top + via_l.astype(F32)).astype(BF16)
-    l_bot = (l_bot + via_r.astype(F32)).astype(BF16)
+    r_top, l_bot = kernel_call(
+        join_kernel, [piece] * 2, (r_top, l_bot, via_l, via_r), rows * seg * 2
+    )
     in_l_top = lax.ppermute(r_top, "x", right)
     in_r_bot = lax.ppermute(l_bot, "x", left)
     (mixed_out,) = kernel_call(
@@ -370,15 +434,15 @@
     grad_queries, grad_levels = kernel_call(
         dq_kernel,
         [((rows, heads, hd), BF16), ((levels, heads, rows), F32)],
-        (mask, queries, g2, level_weight, dq_local, near_grad, *lefts),
+        (queries, g2, level_weight, dq_local, near_grad, *lefts),
         2 * rows * hd * hd * FAR * heads,
-        scalars=1,
     )
     grad_keys, grad_values = kernel_call(
         final_kernel,
         [((rows, heads, hd), BF16)] * 2,
-        (dk_local, dv_local, key_matrix, value_matrix, right_states),
+        (dk_local, dv_local, key_matrix, value_matrix, *right_states),
         4 * rows * hd * hd * heads,
+        scratch=[pltpu.VMEM((heads, hd, hd), BF16)],
     )
     return mixed_out, grad_queries, grad_keys, grad_values, grad_levels
 

time: 123 us -> 94.6 us (0.77)
  the two profiles are of different devices: /device:TPU:10 before, /device:TPU:6 now
where the time goes in v2:
time: 94.6 us; the launch traced here: 94.5 us
  starting transfers between devices  45.5 us (48%)
  waiting for transfers between devices  26.2 us (28%)
  Pallas kernels  19.1 us (20%)
  matrix products  1.71 us (2%)
  between operations  0.95 us (1%)
    pallas_call x17, Pallas kernels, kernel_call(): pl.pallas_call(body, in_specs=[VMEM] * len(operands), out_specs=[VMEM] *...  19.1 us
    ppermute x5, starting transfers between devices, body(): got = lax.ppermute(run.astype(BF16), axis, route)  18.7 us
    ppermute x3, waiting for transfers between devices, across_z(): return lax.ppermute(value, 'z', [(i, i ^ 1 << bit) for i in range(nz)])  11.8 us
    ppermute x6, starting transfers between devices, across_y(): arrived.append(lax.ppermute(parts[m], 'y', [(i, i ^ m) for i in range(ny)]))  10.2 us
    ppermute x5, waiting for transfers between devices, body(): got = lax.ppermute(run.astype(BF16), axis, route)  10.2 us
    ppermute x3, starting transfers between devices, across_z(): return lax.ppermute(value, 'z', [(i, i ^ 1 << bit) for i in range(nz)])  4.29 us
    ppermute x1, starting transfers between devices, body(): in_l_bot = lax.ppermute(r_bot, 'x', right)  3.31 us
    ppermute x6, waiting for transfers between devices, across_y(): arrived.append(lax.ppermute(parts[m], 'y', [(i, i ^ m) for i in range(ny)]))  2.63 us
  transfers between devices with their start and end apart: 27, of which 9 were waited for; matrix products, arithmetic and copies ran while one was open for 2% of the time, Pallas kernels for 19%

profile of v2, /device:TPU:6, one launch (start us, length us, event | category | flops | bytes accessed | tf_op | source)
XLA Modules:
  0.0 94.5 jit_solution(17320696597183915803)
XLA Ops:
  0.8 1.7 %fusion.6 = (bf16[4,128,128]{2,1,0:T(8,128)(2,1)S(1)}, f32[4,128,128]{2,1,0:T(8,128)S(1)}) fusion(bf16[512,4,128]{2,1,0:T(4,128)(2,1)} %v_ref.5, bf16[512,4,128]{2,1,0:T(4,128)(2,1)} %k_ref.5), kind=kOutput, calls=%fused_computation.10 | convolution fusion | flops 67174400 | bytes 1441792 | tf_op jit(solution)/shard_map/gpl,gpq->plq/dot_general | solution.py:332
  2.5 1.7 %collective-permute-start = (bf16[4,128,128]{2,1,0:T(8,128)(2,1)S(1)}, bf16[4,128,128]{2,1,0:T(8,128)(2,1)S(1)}, u32[]{:S(2)}, u32[]{:S(2)}) collective-permute-start(bf16[4,128,128]{2,1,0:T(8,128)(2,1)S(1)} %get-tuple-element.81), channel_id=1, source_target_pairs={{0,8},{8,0},{16,24},{24,16},{1,9},{9,1},{17,25},{25,17},{2,10},{10... | collective-permute-start | bytes 393224 | tf_op jit(solution)/shard_map/ppermute | solution.py:338
  4.1 4.5 %collective-permute-done.r0 = bf16[4,128,128]{2,1,0:T(8,128)(2,1)S(1)} collective-permute-done((bf16[4,128,128]{2,1,0:T(8,128)(2,1)S(1)}, bf16[4,128,128]{2,1,0:T(8,128)(2,1)S(1)}, u32[]{:S(2)}, u32[]{:S(2)}) %collective-permute-start) | collective-permute-done | bytes 131104 | tf_op jit(solution)/shard_map/ppermute | solution.py:338
  8.7 3.3 %collective-permute-start.1 = (bf16[4,128,128]{2,1,0:T(8,128)(2,1)S(1)}, bf16[4,128,128]{2,1,0:T(8,128)(2,1)S(1)}, u32[]{:S(2)}, u32[]{:S(2)}) collective-permute-start(bf16[4,128,128]{2,1,0:T(8,128)(2,1)S(1)} %fusion.3), channel_id=1, source_target_pairs={{0,16},{8,24},{16,0},{24,8},{1,17},{9,25},{17,1},{25,9},{2,18},{10... | collective-permute-start | bytes 393224 | tf_op jit(solution)/shard_map/ppermute | solution.py:338
  12.0 0.5 collective-permute-start.13
  12.5 1.5 %collective-permute-start.15 = (bf16[512,512]{1,0:T(8,128)(2,1)}, bf16[512,512]{1,0:T(8,128)(2,1)S(1)}, u32[]{:S(2)}, u32[]{:S(2)}) collective-permute-start(bf16[512,512]{1,0:T(8,128)(2,1)} %go.1), channel_id=1, source_target_pairs={{0,6},{2,0},{4,2},{6,4},{1,7},{3,1},{5,3},{7,5},{8,14},{10,8},{12,... | collective-permute-start | bytes 1572872 | tf_op jit(solution)/shard_map/ppermute | solution.py:329
  14.0 1.5 %collective-permute-done.1.r1 = bf16[4,128,128]{2,1,0:T(8,128)(2,1)S(1)} collective-permute-done((bf16[4,128,128]{2,1,0:T(8,128)(2,1)S(1)}, bf16[4,128,128]{2,1,0:T(8,128)(2,1)S(1)}, u32[]{:S(2)}, u32[]{:S(2)}) %collective-permute-start.1) | collective-permute-done | bytes 131104 | tf_op jit(solution)/shard_map/ppermute | solution.py:338
  15.6 2.0 %collective-permute-start.2 = (bf16[4,128,128]{2,1,0:T(8,128)(2,1)S(1)}, bf16[4,128,128]{2,1,0:T(8,128)(2,1)S(1)}, u32[]{:S(2)}, u32[]{:S(2)}) collective-permute-start(bf16[4,128,128]{2,1,0:T(8,128)(2,1)S(1)} %fusion.5), channel_id=1, source_target_pairs={{0,32},{32,0},{64,96},{96,64},{128,160},{160,128},{192,224},{224,1... | collective-permute-start | bytes 393224 | tf_op jit(solution)/shard_map/ppermute | solution.py:338
  17.6 3.0 %collective-permute-done.2.r2 = bf16[4,128,128]{2,1,0:T(8,128)(2,1)S(1)} collective-permute-done((bf16[4,128,128]{2,1,0:T(8,128)(2,1)S(1)}, bf16[4,128,128]{2,1,0:T(8,128)(2,1)S(1)}, u32[]{:S(2)}, u32[]{:S(2)}) %collective-permute-start.2) | collective-permute-done | bytes 131104 | tf_op jit(solution)/shard_map/ppermute | solution.py:338
  20.7 3.4 %collective-permute-start.3 = (bf16[4,128,128]{2,1,0:T(8,128)(2,1)S(1)}, bf16[4,128,128]{2,1,0:T(8,128)(2,1)S(1)}, u32[]{:S(2)}, u32[]{:S(2)}) collective-permute-start(bf16[4,128,128]{2,1,0:T(8,128)(2,1)S(1)} %fusion.4), channel_id=1, source_target_pairs={{0,64},{32,96},{64,0},{96,32},{128,192},{160,224},{192,128},{224,1... | collective-permute-start | bytes 393224 | tf_op jit(solution)/shard_map/ppermute | solution.py:338
  24.1 1.5 %collective-permute-done.13.gl = bf16[512,512]{1,0:T(8,128)(2,1)S(1)} collective-permute-done((bf16[512,512]{1,0:T(8,128)(2,1)}, bf16[512,512]{1,0:T(8,128)(2,1)S(1)}, u32[]{:S(2)}, u32[]{:S(2)}) %collective-permute-start.13) | collective-permute-done | bytes 524320 | tf_op jit(solution)/shard_map/ppermute | solution.py:328
  25.6 1.8 %collective-permute-start.14 = (bf16[256,512]{1,0:T(8,128)(2,1)S(1)}, bf16[256,512]{1,0:T(8,128)(2,1)S(1)}, u32[]{:S(2)}, u32[]{:S(2)}) collective-permute-start(bf16[256,512]{1,0:T(8,128)(2,1)S(1)} %slice.8), channel_id=1, source_target_pairs={{0,2},{2,4},{4,6},{6,0},{1,3},{3,5},{5,7},{7,1},{8,10},{10,12},{12... | collective-permute-start | bytes 786440 | tf_op jit(solution)/shard_map/ppermute | solution.py:350
  27.4 0.4 collective-permute-start.16
  27.8 1.1 %collective-permute-done.3.r3 = bf16[4,128,128]{2,1,0:T(8,128)(2,1)S(1)} collective-permute-done((bf16[4,128,128]{2,1,0:T(8,128)(2,1)S(1)}, bf16[4,128,128]{2,1,0:T(8,128)(2,1)S(1)}, u32[]{:S(2)}, u32[]{:S(2)}) %collective-permute-start.3) | collective-permute-done | bytes 131104 | tf_op jit(solution)/shard_map/ppermute | solution.py:338
  29.0 8.3 %collective-permute-start.4 = (bf16[4,128,128]{2,1,0:T(8,128)(2,1)S(1)}, bf16[4,128,128]{2,1,0:T(8,128)(2,1)S(1)}, u32[]{:S(2)}, u32[]{:S(2)}) collective-permute-start(bf16[4,128,128]{2,1,0:T(8,128)(2,1)S(1)} %add_convert_fusion), channel_id=1, source_target_pairs={{0,128},{32,160},{64,192},{96,224},{1,129},{33,161},{65,193},{97,2... | collective-permute-start | bytes 393224 | tf_op jit(solution)/shard_map/ppermute | solution.py:338
  37.3 1.8 %shard_map.107 = (f32[512,512]{1,0:T(8,128)S(1)}, f32[512,512]{1,0:T(8,128)S(1)}) custom-call(bf16[512,512]{1,0:T(8,128)(2,1)S(1)} %copy-done.3, bf16[512,512]{1,0:T(8,128)(2,1)S(1)} %collective-permute-done.13.gl, bf16[512,512]{1,0:T(8,128)(2,1)S(1)} %collective-permute-done.15.gr, bf16[512,4096]{1,0:T(8,128)(2,1)S(1)} %bitcast.2, ...), custom_call_target="tpu_custom_call" | custom-call | flops 1610612736 | bytes 12058624 | tf_op jit(solution)/shard_map/pallas_call | solution.py:302
  39.3 0.5 shard_map.109
  39.9 0.4 copy-done.1
  40.2 0.2 copy-done.2
  40.4 0.2 copy-done.4
  40.6 2.3 %shard_map.101 = (f32[512,512]{1,0:T(8,128)S(1)}, bf16[4,640,512]{2,1,0:T(8,128)(2,1)S(1)}) custom-call(bf16[512,4,128]{2,1,0:T(4,128)(2,1)S(1)} %copy-done.4, bf16[512,4,128]{2,1,0:T(4,128)(2,1)S(1)} %copy-done.1, bf16[512,4,128]{2,1,0:T(4,128)(2,1)S(1)} %copy-done.2, f32[15,4,512]{2,1,0:T(4,128)S(1)} %copy-done.5), custom_call_target="tpu_custom_call" | custom-call | flops 536870912 | bytes 5365760 | tf_op jit(solution)/shard_map/pallas_call | solution.py:302
  42.9 0.9 shard_map.102.a
  43.8 0.3 collective-permute-start.5
  44.0 0.5 shard_map.108.own_ref
  44.5 0.9 shard_map.110
  45.5 1.7 %collective-permute-start.18 = (bf16[5,128,128]{2,1,0:T(8,128)(2,1)S(1)}, bf16[5,128,128]{2,1,0:T(8,128)(2,1)S(1)}, u32[]{:S(2)}, u32[]{:S(2)}) collective-permute-start(bf16[5,128,128]{2,1,0:T(8,128)(2,1)S(1)} %get-tuple-element.63), channel_id=1, source_target_pairs={{0,8},{8,0},{16,24},{24,16},{1,9},{9,1},{17,25},{25,17},{2,10},{10... | collective-permute-start | bytes 491528 | tf_op jit(solution)/shard_map/ppermute | solution.py:372
  47.2 2.9 %collective-permute-start.19 = (bf16[5,128,128]{2,1,0:T(8,128)(2,1)S(1)}, bf16[5,128,128]{2,1,0:T(8,128)(2,1)S(1)}, u32[]{:S(2)}, u32[]{:S(2)}) collective-permute-start(bf16[5,128,128]{2,1,0:T(8,128)(2,1)S(1)} %get-tuple-element.64), channel_id=1, source_target_pairs={{0,16},{8,24},{16,0},{24,8},{1,17},{9,25},{17,1},{25,9},{2,18},{10... | collective-permute-start | bytes 491528 | tf_op jit(solution)/shard_map/ppermute | solution.py:372
  50.1 0.7 shard_map.104
  50.8 0.8 collective-permute-start.7
  51.5 1.3 %collective-permute-start.8 = (bf16[256,512]{1,0:T(8,128)(2,1)S(1)}, bf16[256,512]{1,0:T(8,128)(2,1)S(1)}, u32[]{:S(2)}, u32[]{:S(2)}) collective-permute-start(bf16[256,512]{1,0:T(8,128)(2,1)S(1)} %get-tuple-element.49), channel_id=1, source_target_pairs={{0,6},{2,0},{4,2},{6,4},{1,7},{3,1},{5,3},{7,5},{8,14},{10,8},{12,... | collective-permute-start | bytes 786440 | tf_op jit(solution)/shard_map/ppermute | solution.py:410
  52.9 0.8 collective-permute-start.20
  53.7 1.8 %shard_map.103 = (bf16[256,512]{1,0:T(8,128)(2,1)S(1)}, bf16[256,512]{1,0:T(8,128)(2,1)S(1)}, f32[256,512]{1,0:T(8,128)S(1)}, f32[256,512]{1,0:T(8,128)S(1)}, f32[512,512]{1,0:T(8,128)S(1)}) custom-call(bf16[512,512]{1,0:T(8,128)(2,1)S(1)} %shard_map.102.a, bf16[512,512]{1,0:T(8,128)(2,1)S(1)} %collective-permute-done.5.ap, bf16[512,4096]{1,0:T(8,128)(2,1)S(1)} %bitcast.5, ...), custom_call_target="tpu_custom_call" | custom-call | flops 1610612736 | bytes 12058624 | tf_op jit(solution)/shard_map/pallas_call | solution.py:302
  55.5 3.3 %collective-permute-start.10 = (bf16[256,512]{1,0:T(8,128)(2,1)S(1)}, bf16[256,512]{1,0:T(8,128)(2,1)S(1)}, u32[]{:S(2)}, u32[]{:S(2)}) collective-permute-start(bf16[256,512]{1,0:T(8,128)(2,1)S(1)} %get-tuple-element.51), channel_id=1, source_target_pairs={{0,2},{2,4},{4,6},{6,0},{1,3},{3,5},{5,7},{7,1},{8,10},{10,12},{12... | collective-permute-start | bytes 786440 | tf_op jit(solution)/shard_map/ppermute | solution.py:414
  58.8 0.2 collective-permute-start.11
  59.0 2.6 %collective-permute-done.20.w3 = bf16[5,128,128]{2,1,0:T(8,128)(2,1)S(1)} collective-permute-done((bf16[5,128,128]{2,1,0:T(8,128)(2,1)S(1)}, bf16[5,128,128]{2,1,0:T(8,128)(2,1)S(1)}, u32[]{:S(2)}, u32[]{:S(2)}) %collective-permute-start.20) | collective-permute-done | bytes 163872 | tf_op jit(solution)/shard_map/ppermute | solution.py:372
  62.0 1.7 %collective-permute-start.9 = (bf16[256,512]{1,0:T(8,128)(2,1)S(1)}, bf16[256,512]{1,0:T(8,128)(2,1)S(1)}, u32[]{:S(2)}, u32[]{:S(2)}) collective-permute-start(bf16[256,512]{1,0:T(8,128)(2,1)S(1)} %get-tuple-element.50), channel_id=1, source_target_pairs={{0,2},{2,4},{4,6},{6,0},{1,3},{3,5},{5,7},{7,1},{8,10},{10,12},{12... | collective-permute-start | bytes 786440 | tf_op jit(solution)/shard_map/ppermute | solution.py:419
  63.7 0.4 collective-permute-start.12
  64.1 2.5 %collective-permute-done.21.got_ref = bf16[3,128,128]{2,1,0:T(8,128)(2,1)S(1)} collective-permute-done((bf16[3,128,128]{2,1,0:T(8,128)(2,1)S(1)}, bf16[3,128,128]{2,1,0:T(8,128)(2,1)S(1)}, u32[]{:S(2)}, u32[]{:S(2)}) %collective-permute-start.21) | collective-permute-done | bytes 98336 | tf_op jit(solution)/shard_map/ppermute | solution.py:376
  66.6 0.8 collective-permute-start.22
  67.4 4.9 %collective-permute-done.22.got_ref = bf16[2,128,128]{2,1,0:T(8,128)(2,1)S(1)} collective-permute-done((bf16[2,128,128]{2,1,0:T(8,128)(2,1)S(1)}, bf16[2,128,128]{2,1,0:T(8,128)(2,1)S(1)}, u32[]{:S(2)}, u32[]{:S(2)}) %collective-permute-start.22) | collective-permute-done | bytes 65568 | tf_op jit(solution)/shard_map/ppermute | solution.py:376
  72.3 3.4 %collective-permute-start.23 = (bf16[1,128,128]{2,1,0:T(8,128)(2,1)S(1)}, bf16[1,128,128]{2,1,0:T(8,128)(2,1)S(1)}, u32[]{:S(2)}, u32[]{:S(2)}) collective-permute-start(bf16[1,128,128]{2,1,0:T(8,128)(2,1)S(1)} %get-tuple-element.73), channel_id=1, source_target_pairs={{0,128},{32,160},{64,192},{96,224},{128,0},{160,32},{192,64},{224,... | collective-permute-start | bytes 98312 | tf_op jit(solution)/shard_map/ppermute | solution.py:376
  75.7 4.5 %collective-permute-done.23.got_ref = bf16[1,128,128]{2,1,0:T(8,128)(2,1)S(1)} collective-permute-done((bf16[1,128,128]{2,1,0:T(8,128)(2,1)S(1)}, bf16[1,128,128]{2,1,0:T(8,128)(2,1)S(1)}, u32[]{:S(2)}, u32[]{:S(2)}) %collective-permute-start.23) | collective-permute-done | bytes 32800 | tf_op jit(solution)/shard_map/ppermute | solution.py:376
  80.3 1.9 %collective-permute-start.25 = (bf16[128,128]{1,0:T(8,128)(2,1)S(1)}, bf16[128,128]{1,0:T(8,128)(2,1)S(1)}, u32[]{:S(2)}, u32[]{:S(2)}) collective-permute-start(bf16[128,128]{1,0:T(8,128)(2,1)S(1)} %get-tuple-element.76), channel_id=1, source_target_pairs={{0,16},{8,24},{16,0},{24,8},{1,17},{9,25},{17,1},{25,9},{2,18},{10... | collective-permute-start | bytes 98312 | tf_op jit(solution)/shard_map/ppermute | solution.py:372
  82.2 2.8 %collective-permute-start.26 = (bf16[128,128]{1,0:T(8,128)(2,1)S(1)}, bf16[128,128]{1,0:T(8,128)(2,1)S(1)}, u32[]{:S(2)}, u32[]{:S(2)}) collective-permute-start(bf16[128,128]{1,0:T(8,128)(2,1)S(1)} %get-tuple-element.77), channel_id=1, source_target_pairs={{0,24},{8,16},{16,8},{24,0},{1,25},{9,17},{17,9},{25,1},{2,26},{10... | collective-permute-start | bytes 98312 | tf_op jit(solution)/shard_map/ppermute | solution.py:372
  85.0 4.8 %shard_map.111 = (f32[512,512]{1,0:T(8,128)S(1)}, f32[512,512]{1,0:T(8,128)S(1)}, f32[512,512]{1,0:T(8,128)S(1)}, f32[10,4,512]{2,1,0:T(4,128)S(1)}) custom-call(bf16[512,4,128]{2,1,0:T(4,128)(2,1)S(1)} %copy-done.4, bf16[512,4,128]{2,1,0:T(4,128)(2,1)S(1)} %copy-done.1, bf16[512,4,128]{2,1,0:T(4,128)(2,1)S(1)} %copy-done.2, ...), custom_call_target="tpu_custom_call" | custom-call | flops 1342177280 | bytes 5447680 | tf_op jit(solution)/shard_map/pallas_call | solution.py:302
  89.9 2.1 %shard_map.112 = (bf16[512,4,128]{2,1,0:T(4,128)(2,1)}, f32[15,4,512]{2,1,0:T(4,128)}) custom-call(bf16[512,4,128]{2,1,0:T(4,128)(2,1)S(1)} %copy-done.4, bf16[512,512]{1,0:T(8,128)(2,1)S(1)} %get-tuple-element.56.g_ref, f32[15,4,512]{2,1,0:T(4,128)S(1)} %copy-done.5, f32[512,512]{1,0:T(8,128)S(1)} %get-tuple-element.57.dql_ref, ...), custom_call_target="tpu_custom_call" | custom-call | flops 335544320 | bytes 3604480 | tf_op jit(solution)/shard_map/pallas_call | solution.py:302
  92.0 1.0 %shard_map.106 = bf16[512,512]{1,0:T(8,128)(2,1)} custom-call(f32[512,512]{1,0:T(8,128)S(1)} %get-tuple-element.45.own, bf16[256,512]{1,0:T(8,128)(2,1)S(1)} %collective-permute-done.9.l_top, bf16[256,512]{1,0:T(8,128)(2,1)S(1)} %collective-permute-done.10.l_bot, bf16[256,512]{1,0:T(8,128)(2,1)S(1)} %collective-permute-done.11.r_top, ...), custom_call_target="tpu_custom_call" | custom-call | flops 1048576 | bytes 2621440 | tf_op jit(solution)/shard_map/pallas_call | solution.py:302
  93.0 1.5 %shard_map.117 = (bf16[512,4,128]{2,1,0:T(4,128)(2,1)}, bf16[512,4,128]{2,1,0:T(4,128)(2,1)}) custom-call(f32[512,512]{1,0:T(8,128)S(1)} %get-tuple-element.60.dkl_ref, f32[512,512]{1,0:T(8,128)S(1)} %get-tuple-element.61.dvl_ref, bf16[512,4,128]{2,1,0:T(4,128)(2,1)S(1)} %copy-done.1, bf16[512,4,128]{2,1,0:T(4,128)(2,1)S(1)} %copy-done.2, ...), custom_call_target="tpu_custom_call" | custom-call | flops 134217728 | bytes 4325376 | tf_op jit(solution)/shard_map/pallas_call | solution.py:302
  (42 shorter events, 1.0 us)
Async XLA Ops:
  0.6 36.7 %copy-start = (bf16[4,128,4096]{2,1,0:T(8,128)(2,1)S(1)}, bf16[4,128,4096]{2,1,0:T(8,128)(2,1)}, u32[]{:S(2)}) copy-start(bf16[4,128,4096]{2,1,0:T(8,128)(2,1)} %param.10) | copy-start | bytes 12582916
  0.6 36.7 %copy-start.3 = (bf16[512,512]{1,0:T(8,128)(2,1)S(1)}, bf16[512,512]{1,0:T(8,128)(2,1)}, u32[]{:S(2)}) copy-start(bf16[512,512]{1,0:T(8,128)(2,1)} %go.1) | copy-start | bytes 1572868
  0.7 36.7 %collective-permute-start.6 = (bf16[512,4096]{1,0:T(8,128)(2,1)}, bf16[512,4096]{1,0:T(8,128)(2,1)S(1)}, u32[]{:S(2)}, u32[]{:S(2)}) collective-permute-start(bf16[512,4096]{1,0:T(8,128)(2,1)} %bitcast.1), channel_id=1, source_target_pairs={{0,1},{1,0},{2,3},{3,2},{4,5},{5,4},{6,7},{7,6},{8,9},{9,8},{10,11... | collective-permute-start | bytes 12582920 | tf_op jit(solution)/shard_map/ppermute | solution.py:330
  2.5 6.2 %collective-permute-start = (bf16[4,128,128]{2,1,0:T(8,128)(2,1)S(1)}, bf16[4,128,128]{2,1,0:T(8,128)(2,1)S(1)}, u32[]{:S(2)}, u32[]{:S(2)}) collective-permute-start(bf16[4,128,128]{2,1,0:T(8,128)(2,1)S(1)} %get-tuple-element.81), channel_id=1, source_target_pairs={{0,8},{8,0},{16,24},{24,16},{1,9},{9,1},{17,25},{25,17},{2,10},{10... | collective-permute-start | bytes 393224 | tf_op jit(solution)/shard_map/ppermute | solution.py:338
  8.7 6.9 %collective-permute-start.1 = (bf16[4,128,128]{2,1,0:T(8,128)(2,1)S(1)}, bf16[4,128,128]{2,1,0:T(8,128)(2,1)S(1)}, u32[]{:S(2)}, u32[]{:S(2)}) collective-permute-start(bf16[4,128,128]{2,1,0:T(8,128)(2,1)S(1)} %fusion.3), channel_id=1, source_target_pairs={{0,16},{8,24},{16,0},{24,8},{1,17},{9,25},{17,1},{25,9},{2,18},{10... | collective-permute-start | bytes 393224 | tf_op jit(solution)/shard_map/ppermute | solution.py:338
  12.0 13.6 %collective-permute-start.13 = (bf16[512,512]{1,0:T(8,128)(2,1)}, bf16[512,512]{1,0:T(8,128)(2,1)S(1)}, u32[]{:S(2)}, u32[]{:S(2)}) collective-permute-start(bf16[512,512]{1,0:T(8,128)(2,1)} %go.1), channel_id=1, source_target_pairs={{0,2},{2,4},{4,6},{6,0},{1,3},{3,5},{5,7},{7,1},{8,10},{10,12},{12... | collective-permute-start | bytes 1572872 | tf_op jit(solution)/shard_map/ppermute | solution.py:328
  12.5 14.9 %collective-permute-start.15 = (bf16[512,512]{1,0:T(8,128)(2,1)}, bf16[512,512]{1,0:T(8,128)(2,1)S(1)}, u32[]{:S(2)}, u32[]{:S(2)}) collective-permute-start(bf16[512,512]{1,0:T(8,128)(2,1)} %go.1), channel_id=1, source_target_pairs={{0,6},{2,0},{4,2},{6,4},{1,7},{3,1},{5,3},{7,5},{8,14},{10,8},{12,... | collective-permute-start | bytes 1572872 | tf_op jit(solution)/shard_map/ppermute | solution.py:329
  15.6 5.1 %collective-permute-start.2 = (bf16[4,128,128]{2,1,0:T(8,128)(2,1)S(1)}, bf16[4,128,128]{2,1,0:T(8,128)(2,1)S(1)}, u32[]{:S(2)}, u32[]{:S(2)}) collective-permute-start(bf16[4,128,128]{2,1,0:T(8,128)(2,1)S(1)} %fusion.5), channel_id=1, source_target_pairs={{0,32},{32,0},{64,96},{96,64},{128,160},{160,128},{192,224},{224,1... | collective-permute-start | bytes 393224 | tf_op jit(solution)/shard_map/ppermute | solution.py:338
  20.7 8.2 %collective-permute-start.3 = (bf16[4,128,128]{2,1,0:T(8,128)(2,1)S(1)}, bf16[4,128,128]{2,1,0:T(8,128)(2,1)S(1)}, u32[]{:S(2)}, u32[]{:S(2)}) collective-permute-start(bf16[4,128,128]{2,1,0:T(8,128)(2,1)S(1)} %fusion.4), channel_id=1, source_target_pairs={{0,64},{32,96},{64,0},{96,32},{128,192},{160,224},{192,128},{224,1... | collective-permute-start | bytes 393224 | tf_op jit(solution)/shard_map/ppermute | solution.py:338
  25.6 13.6 %collective-permute-start.14 = (bf16[256,512]{1,0:T(8,128)(2,1)S(1)}, bf16[256,512]{1,0:T(8,128)(2,1)S(1)}, u32[]{:S(2)}, u32[]{:S(2)}) collective-permute-start(bf16[256,512]{1,0:T(8,128)(2,1)S(1)} %slice.8), channel_id=1, source_target_pairs={{0,2},{2,4},{4,6},{6,0},{1,3},{3,5},{5,7},{7,1},{8,10},{10,12},{12... | collective-permute-start | bytes 786440 | tf_op jit(solution)/shard_map/ppermute | solution.py:350
  27.4 11.8 %collective-permute-start.16 = (bf16[256,512]{1,0:T(8,128)(2,1)S(1)}, bf16[256,512]{1,0:T(8,128)(2,1)S(1)}, u32[]{:S(2)}, u32[]{:S(2)}) collective-permute-start(bf16[256,512]{1,0:T(8,128)(2,1)S(1)} %slice.9), channel_id=1, source_target_pairs={{0,6},{2,0},{4,2},{6,4},{1,7},{3,1},{5,3},{7,5},{8,14},{10,8},{12,... | collective-permute-start | bytes 786440 | tf_op jit(solution)/shard_map/ppermute | solution.py:351
  29.0 13.9 %collective-permute-start.4 = (bf16[4,128,128]{2,1,0:T(8,128)(2,1)S(1)}, bf16[4,128,128]{2,1,0:T(8,128)(2,1)S(1)}, u32[]{:S(2)}, u32[]{:S(2)}) collective-permute-start(bf16[4,128,128]{2,1,0:T(8,128)(2,1)S(1)} %add_convert_fusion), channel_id=1, source_target_pairs={{0,128},{32,160},{64,192},{96,224},{1,129},{33,161},{65,193},{97,2... | collective-permute-start | bytes 393224 | tf_op jit(solution)/shard_map/ppermute | solution.py:338
  39.2 1.0 %copy-start.1 = (bf16[512,4,128]{2,1,0:T(4,128)(2,1)S(1)}, bf16[512,4,128]{2,1,0:T(4,128)(2,1)}, u32[]{:S(2)}) copy-start(bf16[512,4,128]{2,1,0:T(4,128)(2,1)} %k_ref.5) | copy-start | bytes 1572868
  39.2 1.2 %copy-start.2 = (bf16[512,4,128]{2,1,0:T(4,128)(2,1)S(1)}, bf16[512,4,128]{2,1,0:T(4,128)(2,1)}, u32[]{:S(2)}) copy-start(bf16[512,4,128]{2,1,0:T(4,128)(2,1)} %v_ref.5) | copy-start | bytes 1572868
  39.2 1.3 %copy-start.4 = (bf16[512,4,128]{2,1,0:T(4,128)(2,1)S(1)}, bf16[512,4,128]{2,1,0:T(4,128)(2,1)}, u32[]{:S(2)}) copy-start(bf16[512,4,128]{2,1,0:T(4,128)(2,1)} %q_ref.5) | copy-start | bytes 1572868
  39.2 1.3 %copy-start.5 = (f32[15,4,512]{2,1,0:T(4,128)S(1)}, f32[15,4,512]{2,1,0:T(4,128)}, u32[]{:S(2)}) copy-start(f32[15,4,512]{2,1,0:T(4,128)} %lw_ref.5) | copy-start | bytes 368644
  39.7 4.8 %collective-permute-start.17 = (bf16[512,512]{1,0:T(8,128)(2,1)S(1)}, bf16[512,512]{1,0:T(8,128)(2,1)S(1)}, u32[]{:S(2)}, u32[]{:S(2)}) collective-permute-start(bf16[512,512]{1,0:T(8,128)(2,1)S(1)} %shard_map.109), channel_id=1, source_target_pairs={{0,1},{1,0},{2,3},{3,2},{4,5},{5,4},{6,7},{7,6},{8,9},{9,8},{10,11... | collective-permute-start | bytes 1572872 | tf_op jit(solution)/shard_map/ppermute | solution.py:359
  43.8 6.3 %collective-permute-start.5 = (bf16[512,512]{1,0:T(8,128)(2,1)S(1)}, bf16[512,512]{1,0:T(8,128)(2,1)S(1)}, u32[]{:S(2)}, u32[]{:S(2)}) collective-permute-start(bf16[512,512]{1,0:T(8,128)(2,1)S(1)} %shard_map.102.a), channel_id=1, source_target_pairs={{0,1},{1,0},{2,3},{3,2},{4,5},{5,4},{6,7},{7,6},{8,9},{9,8},{10,11... | collective-permute-start | bytes 1572872 | tf_op jit(solution)/shard_map/ppermute | solution.py:403
  45.5 10.0 %collective-permute-start.18 = (bf16[5,128,128]{2,1,0:T(8,128)(2,1)S(1)}, bf16[5,128,128]{2,1,0:T(8,128)(2,1)S(1)}, u32[]{:S(2)}, u32[]{:S(2)}) collective-permute-start(bf16[5,128,128]{2,1,0:T(8,128)(2,1)S(1)} %get-tuple-element.63), channel_id=1, source_target_pairs={{0,8},{8,0},{16,24},{24,16},{1,9},{9,1},{17,25},{25,17},{2,10},{10... | collective-permute-start | bytes 491528 | tf_op jit(solution)/shard_map/ppermute | solution.py:372
  47.2 11.7 %collective-permute-start.19 = (bf16[5,128,128]{2,1,0:T(8,128)(2,1)S(1)}, bf16[5,128,128]{2,1,0:T(8,128)(2,1)S(1)}, u32[]{:S(2)}, u32[]{:S(2)}) collective-permute-start(bf16[5,128,128]{2,1,0:T(8,128)(2,1)S(1)} %get-tuple-element.64), channel_id=1, source_target_pairs={{0,16},{8,24},{16,0},{24,8},{1,17},{9,25},{17,1},{25,9},{2,18},{10... | collective-permute-start | bytes 491528 | tf_op jit(solution)/shard_map/ppermute | solution.py:372
  50.8 11.1 %collective-permute-start.7 = (bf16[256,512]{1,0:T(8,128)(2,1)S(1)}, bf16[256,512]{1,0:T(8,128)(2,1)S(1)}, u32[]{:S(2)}, u32[]{:S(2)}) collective-permute-start(bf16[256,512]{1,0:T(8,128)(2,1)S(1)} %get-tuple-element.48), channel_id=1, source_target_pairs={{0,2},{2,4},{4,6},{6,0},{1,3},{3,5},{5,7},{7,1},{8,10},{10,12},{12... | collective-permute-start | bytes 786440 | tf_op jit(solution)/shard_map/ppermute | solution.py:409
  51.5 10.3 %collective-permute-start.8 = (bf16[256,512]{1,0:T(8,128)(2,1)S(1)}, bf16[256,512]{1,0:T(8,128)(2,1)S(1)}, u32[]{:S(2)}, u32[]{:S(2)}) collective-permute-start(bf16[256,512]{1,0:T(8,128)(2,1)S(1)} %get-tuple-element.49), channel_id=1, source_target_pairs={{0,6},{2,0},{4,2},{6,4},{1,7},{3,1},{5,3},{7,5},{8,14},{10,8},{12,... | collective-permute-start | bytes 786440 | tf_op jit(solution)/shard_map/ppermute | solution.py:410
  52.9 8.8 %collective-permute-start.20 = (bf16[5,128,128]{2,1,0:T(8,128)(2,1)S(1)}, bf16[5,128,128]{2,1,0:T(8,128)(2,1)S(1)}, u32[]{:S(2)}, u32[]{:S(2)}) collective-permute-start(bf16[5,128,128]{2,1,0:T(8,128)(2,1)S(1)} %get-tuple-element.65), channel_id=1, source_target_pairs={{0,24},{8,16},{16,8},{24,0},{1,25},{9,17},{17,9},{25,1},{2,26},{10... | collective-permute-start | bytes 491528 | tf_op jit(solution)/shard_map/ppermute | solution.py:372
  55.5 24.8 %collective-permute-start.10 = (bf16[256,512]{1,0:T(8,128)(2,1)S(1)}, bf16[256,512]{1,0:T(8,128)(2,1)S(1)}, u32[]{:S(2)}, u32[]{:S(2)}) collective-permute-start(bf16[256,512]{1,0:T(8,128)(2,1)S(1)} %get-tuple-element.51), channel_id=1, source_target_pairs={{0,2},{2,4},{4,6},{6,0},{1,3},{3,5},{5,7},{7,1},{8,10},{10,12},{12... | collective-permute-start | bytes 786440 | tf_op jit(solution)/shard_map/ppermute | solution.py:414
  58.8 23.4 %collective-permute-start.11 = (bf16[256,512]{1,0:T(8,128)(2,1)S(1)}, bf16[256,512]{1,0:T(8,128)(2,1)S(1)}, u32[]{:S(2)}, u32[]{:S(2)}) collective-permute-start(bf16[256,512]{1,0:T(8,128)(2,1)S(1)} %get-tuple-element.52), channel_id=1, source_target_pairs={{0,6},{2,0},{4,2},{6,4},{1,7},{3,1},{5,3},{7,5},{8,14},{10,8},{12,... | collective-permute-start | bytes 786440 | tf_op jit(solution)/shard_map/ppermute | solution.py:415
  61.8 4.8 %collective-permute-start.21 = (bf16[3,128,128]{2,1,0:T(8,128)(2,1)S(1)}, bf16[3,128,128]{2,1,0:T(8,128)(2,1)S(1)}, u32[]{:S(2)}, u32[]{:S(2)}) collective-permute-start(bf16[3,128,128]{2,1,0:T(8,128)(2,1)S(1)} %get-tuple-element.67), channel_id=1, source_target_pairs={{0,32},{32,0},{64,96},{96,64},{128,160},{160,128},{192,224},{224,1... | collective-permute-start | bytes 294920 | tf_op jit(solution)/shard_map/ppermute | solution.py:376
  62.0 30.0 %collective-permute-start.9 = (bf16[256,512]{1,0:T(8,128)(2,1)S(1)}, bf16[256,512]{1,0:T(8,128)(2,1)S(1)}, u32[]{:S(2)}, u32[]{:S(2)}) collective-permute-start(bf16[256,512]{1,0:T(8,128)(2,1)S(1)} %get-tuple-element.50), channel_id=1, source_target_pairs={{0,2},{2,4},{4,6},{6,0},{1,3},{3,5},{5,7},{7,1},{8,10},{10,12},{12... | collective-permute-start | bytes 786440 | tf_op jit(solution)/shard_map/ppermute | solution.py:419
  63.7 28.3 %collective-permute-start.12 = (bf16[256,512]{1,0:T(8,128)(2,1)S(1)}, bf16[256,512]{1,0:T(8,128)(2,1)S(1)}, u32[]{:S(2)}, u32[]{:S(2)}) collective-permute-start(bf16[256,512]{1,0:T(8,128)(2,1)S(1)} %get-tuple-element.53), channel_id=1, source_target_pairs={{0,6},{2,0},{4,2},{6,4},{1,7},{3,1},{5,3},{7,5},{8,14},{10,8},{12,... | collective-permute-start | bytes 786440 | tf_op jit(solution)/shard_map/ppermute | solution.py:420
  66.6 5.7 %collective-permute-start.22 = (bf16[2,128,128]{2,1,0:T(8,128)(2,1)S(1)}, bf16[2,128,128]{2,1,0:T(8,128)(2,1)S(1)}, u32[]{:S(2)}, u32[]{:S(2)}) collective-permute-start(bf16[2,128,128]{2,1,0:T(8,128)(2,1)S(1)} %get-tuple-element.70), channel_id=1, source_target_pairs={{0,64},{32,96},{64,0},{96,32},{128,192},{160,224},{192,128},{224,1... | collective-permute-start | bytes 196616 | tf_op jit(solution)/shard_map/ppermute | solution.py:376
  72.3 7.9 %collective-permute-start.23 = (bf16[1,128,128]{2,1,0:T(8,128)(2,1)S(1)}, bf16[1,128,128]{2,1,0:T(8,128)(2,1)S(1)}, u32[]{:S(2)}, u32[]{:S(2)}) collective-permute-start(bf16[1,128,128]{2,1,0:T(8,128)(2,1)S(1)} %get-tuple-element.73), channel_id=1, source_target_pairs={{0,128},{32,160},{64,192},{96,224},{128,0},{160,32},{192,64},{224,... | collective-permute-start | bytes 98312 | tf_op jit(solution)/shard_map/ppermute | solution.py:376
  80.2 12.8 %collective-permute-start.24 = (bf16[128,128]{1,0:T(8,128)(2,1)S(1)}, bf16[128,128]{1,0:T(8,128)(2,1)S(1)}, u32[]{:S(2)}, u32[]{:S(2)}) collective-permute-start(bf16[128,128]{1,0:T(8,128)(2,1)S(1)} %get-tuple-element.75), channel_id=1, source_target_pairs={{0,8},{8,0},{16,24},{24,16},{1,9},{9,1},{17,25},{25,17},{2,10},{10... | collective-permute-start | bytes 98312 | tf_op jit(solution)/shard_map/ppermute | solution.py:372
  80.3 12.6 %collective-permute-start.25 = (bf16[128,128]{1,0:T(8,128)(2,1)S(1)}, bf16[128,128]{1,0:T(8,128)(2,1)S(1)}, u32[]{:S(2)}, u32[]{:S(2)}) collective-permute-start(bf16[128,128]{1,0:T(8,128)(2,1)S(1)} %get-tuple-element.76), channel_id=1, source_target_pairs={{0,16},{8,24},{16,0},{24,8},{1,17},{9,25},{17,1},{25,9},{2,18},{10... | collective-permute-start | bytes 98312 | tf_op jit(solution)/shard_map/ppermute | solution.py:372
  82.2 10.7 %collective-permute-start.26 = (bf16[128,128]{1,0:T(8,128)(2,1)S(1)}, bf16[128,128]{1,0:T(8,128)(2,1)S(1)}, u32[]{:S(2)}, u32[]{:S(2)}) collective-permute-start(bf16[128,128]{1,0:T(8,128)(2,1)S(1)} %get-tuple-element.77), channel_id=1, source_target_pairs={{0,24},{8,16},{16,8},{24,0},{1,25},{9,17},{17,9},{25,1},{2,26},{10... | collective-permute-start | bytes 98312 | tf_op jit(solution)/shard_map/ppermute | solution.py:372

commit v3 on v2

--- a/solution.py
+++ b/solution.py
@@ -1,3 +1,4 @@
+import functools
 import math
 
 import jax
@@ -53,6 +54,18 @@
 def flat(ref):
     rows, heads, hd = ref.shape
     return ref[...].reshape(rows, heads * hd)
+
+
+def stage_kernel(*refs):
+    n = (len(refs) - 1) // 2
+    moves = [
+        pltpu.make_async_copy(src, dst, refs[-1].at[i])
+        for i, (src, dst) in enumerate(zip(refs[:n], refs[n : 2 * n], strict=True))
+    ]
+    for move in moves:
+        move.start()
+    for move in moves:
+        move.wait()
 
 
 def fwd_kernel(q_ref, k_ref, v_ref, lw_ref, lo_ref, wq_ref):
@@ -77,14 +90,16 @@
             wq_ref[h, pl.ds(j * HD, HD), :] = (qt * row).astype(BF16)
 
 
-def bwd_kernel(q_ref, k_ref, v_ref, g_ref, lw_ref, dq_ref, dk_ref, dv_ref, ng_ref):
+def bwd_kernel(first, q_ref, k_ref, v_ref, g_ref, lw_ref, dq_ref, dk_ref, dv_ref, ng_ref):
     level = diag_level()
-    rows, heads, _ = q_ref.shape
+    rows = q_ref.shape[0]
     blocks = rows // BLK
     q_all, k_all, v_all = flat(q_ref), flat(k_ref), flat(v_ref)
-    for h in range(heads):
-        lanes = slice(h * HD, (h + 1) * HD)
-        q, k, v, g = q_all[:, lanes], k_all[:, lanes], v_all[:, lanes], g_ref[:, lanes]
+    for n_head in range(dq_ref.shape[1] // HD):
+        h = first + n_head
+        held = slice(h * HD, (h + 1) * HD)
+        lanes = slice(n_head * HD, (n_head + 1) * HD)
+        q, k, v, g = q_all[:, held], k_all[:, held], v_all[:, held], g_ref[:, held]
         for i in reversed(range(blocks)):
             n = (i + 1) * BLK
             q_i, g_i = q[i * BLK : n], g[i * BLK : n]
@@ -111,7 +126,7 @@
             gt = jnp.concatenate(gts, axis=0)
             for l in range(NEAR):
                 value = jnp.zeros((1, BLK), F32) if sums[l] is None else sums[l] * C[l]
-                ng_ref[l, pl.ds(h, 1), pl.ds(i * BLK, BLK)] = value
+                ng_ref[n_head, pl.ds(l, 1), pl.ds(i * BLK, BLK)] = value
             dq_ref[pl.ds(i * BLK, BLK), lanes] = dot(gt, k[:n], TN)
             if i == blocks - 1:
                 dk_ref[:, lanes] = dot(gt, q_i, NN)
@@ -146,11 +161,10 @@
         att_ref[:, lanes] = (lo_ref[:, lanes] + dot(wq_ref[h], states, TN)).astype(BF16)
 
 
-def dq_kernel(q_ref, g_ref, lw_ref, dql_ref, ng_ref, r0, r1, r2, r3, r4, dq_ref, gl_ref):
+def dq_kernel(q_ref, g_ref, lw_ref, dqa, dqb, nga, ngb, r0, r1, r2, r3, r4, dq_ref, gl_ref):
     _, heads, _ = q_ref.shape
     q_all = flat(q_ref)
     outs = []
-    gl_ref[pl.ds(0, NEAR)] = ng_ref[...]
     for h in range(heads):
         lanes = slice(h * HD, (h + 1) * HD)
         states = left_stack((r0, r1, r2, r3, r4), h)
@@ -164,7 +178,10 @@
             gl_ref[NEAR + j, pl.ds(h, 1), :] = (
                 jnp.sum(part * qt, axis=0, keepdims=True) * C[NEAR + j]
             )
-        outs.append((dql_ref[:, lanes] + total.T).astype(BF16))
+        local, near, at = (dqa, nga, h) if h < heads // 2 else (dqb, ngb, h - heads // 2)
+        for l in range(NEAR):
+            gl_ref[l, pl.ds(h, 1), :] = near[at, pl.ds(l, 1), :]
+        outs.append((local[:, at * HD : (at + 1) * HD] + total.T).astype(BF16))
     dq_ref[...] = jnp.concatenate(outs, axis=1).reshape(q_ref.shape)
 
 
@@ -220,7 +237,7 @@
         ref[...] = (near_ref[m] + acc).astype(BF16)
 
 
-def final_kernel(dkl_ref, dvl_ref, k_ref, v_ref, r0, r1, r2, r3, dk_ref, dv_ref, r_ref):
+def final_kernel(dka, dva, dkb, dvb, k_ref, v_ref, r0, r1, r2, r3, dk_ref, dv_ref, r_ref):
     k_all, v_all = flat(k_ref), flat(v_ref)
     for m, r in enumerate((r0, r1, r2, r3)):
         r_ref[swapped(m)] = r[...]
@@ -228,8 +245,11 @@
     for h in range(r_ref.shape[0]):
         lanes = slice(h * HD, (h + 1) * HD)
         r = r_ref[h]
-        dks.append((dkl_ref[:, lanes] + dot(v_all[:, lanes], r, NT)).astype(BF16))
-        dvs.append((dvl_ref[:, lanes] + dot(k_all[:, lanes], r, NN)).astype(BF16))
+        half = r_ref.shape[0] // 2
+        dkl, dvl, at = (dka, dva, h) if h < half else (dkb, dvb, h - half)
+        part = slice(at * HD, (at + 1) * HD)
+        dks.append((dkl[:, part] + dot(v_all[:, lanes], r, NT)).astype(BF16))
+        dvs.append((dvl[:, part] + dot(k_all[:, lanes], r, NN)).astype(BF16))
     dk_ref[...] = jnp.concatenate(dks, axis=1).reshape(k_ref.shape)
     dv_ref[...] = jnp.concatenate(dvs, axis=1).reshape(k_ref.shape)
 
@@ -293,15 +313,16 @@
 
 
 VMEM = pl.BlockSpec(memory_space=pltpu.VMEM)
-
-
-def kernel_call(body, outs, operands, flops, scratch=(), vmem=16):
+HBM = pl.BlockSpec(memory_space=pltpu.HBM)
+
+
+def kernel_call(body, outs, operands, flops, scratch=(), space=VMEM, vmem=16):
     out_shape = [jax.ShapeDtypeStruct(s, d) for s, d in outs]
     nbytes = sum(math.prod(s) * jnp.dtype(d).itemsize for s, d in outs)
     nbytes += sum(o.size * o.dtype.itemsize for o in operands)
     return pl.pallas_call(
         body,
-        in_specs=[VMEM] * len(operands),
+        in_specs=[space] * len(operands),
         out_specs=[VMEM] * len(outs),
         out_shape=out_shape,
         scratch_shapes=list(scratch),
@@ -330,15 +351,24 @@
     w_par = lax.ppermute(w2, "c", swap)
 
     run = jnp.einsum("gpl,gpq->plq", key_matrix, value_matrix, preferred_element_type=F32)
+    inputs = [
+        pltpu.with_memory_space_constraint(i, pltpu.HBM)
+        for i in (queries, key_matrix, value_matrix, level_weight)
+    ]
+    queries, key_matrix, value_matrix, level_weight = kernel_call(
+        stage_kernel,
+        [(i.shape, i.dtype) for i in inputs],
+        inputs,
+        0,
+        scratch=[pltpu.SemaphoreType.DMA((4,))],
+        space=HBM,
+    )
     lefts = []
-    for step, (axis, bit) in enumerate((("y", 0), ("y", 1), ("z", 0), ("z", 1), ("z", 2))):
-        n = lax.axis_size(axis)
-        last = step == 4
-        route = [(i, i ^ (1 << bit)) for i in range(n) if not (last and i >> bit & 1)]
+    for axis, mask in (("y", 1), ("y", 3), ("z", 1), ("z", 2), ("z", 6)):
+        route = [(i, i ^ mask) for i in range(lax.axis_size(axis))]
         got = lax.ppermute(run.astype(BF16), axis, route)
         lefts.append(got)
-        if not last:
-            run = run + got.astype(F32)
+        run = run + got.astype(F32)
     block = 2 * rows * rows * width
     local_out, wq = kernel_call(
         fwd_kernel,
@@ -373,7 +403,7 @@
         return arrived
 
     def across_z(bit, value):
-        return lax.ppermute(value, "z", [(i, i ^ (1 << bit)) for i in range(nz)])
+        return lax.ppermute(value, "z", [(i, i ^ (1, 2, 6)[bit]) for i in range(nz)])
 
     tiny = 8 * hd * hd
     near, held, send = kernel_call(
@@ -425,22 +455,27 @@
         rows * seg * 4,
     )
 
-    dq_local, dk_local, dv_local, near_grad = kernel_call(
-        bwd_kernel,
-        [((rows, width), F32)] * 3 + [((NEAR, heads, rows), F32)],
-        (queries, key_matrix, value_matrix, g2, level_weight),
-        5 * block,
-    )
+    def backward(first):
+        two = heads // 2
+        return kernel_call(
+            functools.partial(bwd_kernel, first),
+            [((rows, two * hd), F32)] * 3 + [((two, NEAR, rows), F32)],
+            (queries, key_matrix, value_matrix, g2, level_weight),
+            2.5 * block,
+        )
+
+    dq_a, dk_a, dv_a, near_a = backward(0)
+    dq_b, dk_b, dv_b, near_b = backward(heads // 2)
     grad_queries, grad_levels = kernel_call(
         dq_kernel,
         [((rows, heads, hd), BF16), ((levels, heads, rows), F32)],
-        (queries, g2, level_weight, dq_local, near_grad, *lefts),
+        (queries, g2, level_weight, dq_a, dq_b, near_a, near_b, *lefts),
         2 * rows * hd * hd * FAR * heads,
     )
     grad_keys, grad_values = kernel_call(
         final_kernel,
         [((rows, heads, hd), BF16)] * 2,
-        (dk_local, dv_local, key_matrix, value_matrix, *right_states),
+        (dk_a, dv_a, dk_b, dv_b, key_matrix, value_matrix, *right_states),
         4 * rows * hd * hd * heads,
         scratch=[pltpu.VMEM((heads, hd, hd), BF16)],
     )

time: 94.6 us -> 92.5 us (0.978)
  the two profiles are of different devices: /device:TPU:6 before, /device:TPU:32 now
where the time goes in v3:
time: 92.5 us; the launch traced here: 92.4 us
  starting transfers between devices  44.6 us (48%)
  waiting for transfers between devices  24.3 us (26%)
  Pallas kernels  20.7 us (22%)
  matrix products  1.55 us (2%)
    pallas_call x19, Pallas kernels, kernel_call(): pl.pallas_call(body, in_specs=[space] * len(operands), out_specs=[VMEM] *...  20.7 us
    ppermute x5, starting transfers between devices, body(): got = lax.ppermute(run.astype(BF16), axis, route)  15.9 us
    ppermute x5, waiting for transfers between devices, body(): got = lax.ppermute(run.astype(BF16), axis, route)  11.3 us
    ppermute x6, starting transfers between devices, across_y(): arrived.append(lax.ppermute(parts[m], 'y', [(i, i ^ m) for i in range(ny)]))  9.56 us
    ppermute x6, waiting for transfers between devices, across_y(): arrived.append(lax.ppermute(parts[m], 'y', [(i, i ^ m) for i in range(ny)]))  6.93 us
    ppermute x3, waiting for transfers between devices, across_z(): lax.ppermute(value, 'z', [(i, i ^ (1, 2, 6)[bit]) for i in range(nz)])  6.04 us
    ppermute x3, starting transfers between devices, across_z(): lax.ppermute(value, 'z', [(i, i ^ (1, 2, 6)[bit]) for i in range(nz)])  4.68 us
    ppermute x1, starting transfers between devices, body(): from_r = lax.ppermute(grad_out, 'x', left)  3.23 us
  transfers between devices with their start and end apart: 27, of which 9 were waited for; matrix products, arithmetic and copies ran while one was open for 2% of the time, Pallas kernels for 21%

profile of v3, /device:TPU:32, one launch (start us, length us, event | category | flops | bytes accessed | tf_op | source)
XLA Modules:
  0.0 92.4 jit_solution(14804641444058262261)
XLA Ops:
  0.6 0.1 collective-permute-start.6
  0.7 1.6 %fusion.6 = (bf16[4,128,128]{2,1,0:T(8,128)(2,1)S(1)}, f32[4,128,128]{2,1,0:T(8,128)S(1)}) fusion(bf16[512,4,128]{2,1,0:T(4,128)(2,1)} %refs_2_.1, bf16[512,4,128]{2,1,0:T(4,128)(2,1)} %refs_1_.1), kind=kOutput, calls=%fused_computation.10 | convolution fusion | flops 67174400 | bytes 1441792 | tf_op jit(solution)/shard_map/gpl,gpq->plq/dot_general | solution.py:353
  2.3 1.7 %collective-permute-start = (bf16[4,128,128]{2,1,0:T(8,128)(2,1)S(1)}, bf16[4,128,128]{2,1,0:T(8,128)(2,1)S(1)}, u32[]{:S(2)}, u32[]{:S(2)}) collective-permute-start(bf16[4,128,128]{2,1,0:T(8,128)(2,1)S(1)} %get-tuple-element.97), channel_id=1, source_target_pairs={{0,8},{8,0},{16,24},{24,16},{1,9},{9,1},{17,25},{25,17},{2,10},{10... | collective-permute-start | bytes 393224 | tf_op jit(solution)/shard_map/ppermute | solution.py:369
  4.0 4.3 %collective-permute-done.r0 = bf16[4,128,128]{2,1,0:T(8,128)(2,1)S(1)} collective-permute-done((bf16[4,128,128]{2,1,0:T(8,128)(2,1)S(1)}, bf16[4,128,128]{2,1,0:T(8,128)(2,1)S(1)}, u32[]{:S(2)}, u32[]{:S(2)}) %collective-permute-start) | collective-permute-done | bytes 131104 | tf_op jit(solution)/shard_map/ppermute | solution.py:369
  8.3 3.1 %collective-permute-start.1 = (bf16[4,128,128]{2,1,0:T(8,128)(2,1)S(1)}, bf16[4,128,128]{2,1,0:T(8,128)(2,1)S(1)}, u32[]{:S(2)}, u32[]{:S(2)}) collective-permute-start(bf16[4,128,128]{2,1,0:T(8,128)(2,1)S(1)} %fusion.3), channel_id=1, source_target_pairs={{0,24},{8,16},{16,8},{24,0},{1,25},{9,17},{17,9},{25,1},{2,26},{10... | collective-permute-start | bytes 393224 | tf_op jit(solution)/shard_map/ppermute | solution.py:369
  11.4 3.3 %collective-permute-done.1.r1 = bf16[4,128,128]{2,1,0:T(8,128)(2,1)S(1)} collective-permute-done((bf16[4,128,128]{2,1,0:T(8,128)(2,1)S(1)}, bf16[4,128,128]{2,1,0:T(8,128)(2,1)S(1)}, u32[]{:S(2)}, u32[]{:S(2)}) %collective-permute-start.1) | collective-permute-done | bytes 131104 | tf_op jit(solution)/shard_map/ppermute | solution.py:369
  14.8 1.8 %collective-permute-start.2 = (bf16[4,128,128]{2,1,0:T(8,128)(2,1)S(1)}, bf16[4,128,128]{2,1,0:T(8,128)(2,1)S(1)}, u32[]{:S(2)}, u32[]{:S(2)}) collective-permute-start(bf16[4,128,128]{2,1,0:T(8,128)(2,1)S(1)} %fusion.5), channel_id=1, source_target_pairs={{0,32},{32,0},{64,96},{96,64},{128,160},{160,128},{192,224},{224,1... | collective-permute-start | bytes 393224 | tf_op jit(solution)/shard_map/ppermute | solution.py:369
  16.6 3.2 %collective-permute-start.15 = (bf16[512,512]{1,0:T(8,128)(2,1)}, bf16[512,512]{1,0:T(8,128)(2,1)S(1)}, u32[]{:S(2)}, u32[]{:S(2)}) collective-permute-start(bf16[512,512]{1,0:T(8,128)(2,1)} %go.1), channel_id=1, source_target_pairs={{0,6},{2,0},{4,2},{6,4},{1,7},{3,1},{5,3},{7,5},{8,14},{10,8},{12,... | collective-permute-start | bytes 1572872 | tf_op jit(solution)/shard_map/ppermute | solution.py:350
  19.9 3.3 %collective-permute-start.3 = (bf16[4,128,128]{2,1,0:T(8,128)(2,1)S(1)}, bf16[4,128,128]{2,1,0:T(8,128)(2,1)S(1)}, u32[]{:S(2)}, u32[]{:S(2)}) collective-permute-start(bf16[4,128,128]{2,1,0:T(8,128)(2,1)S(1)} %fusion.4), channel_id=1, source_target_pairs={{0,64},{32,96},{64,0},{96,32},{128,192},{160,224},{192,128},{224,1... | collective-permute-start | bytes 393224 | tf_op jit(solution)/shard_map/ppermute | solution.py:369
  23.2 3.6 %collective-permute-done.3.r3 = bf16[4,128,128]{2,1,0:T(8,128)(2,1)S(1)} collective-permute-done((bf16[4,128,128]{2,1,0:T(8,128)(2,1)S(1)}, bf16[4,128,128]{2,1,0:T(8,128)(2,1)S(1)}, u32[]{:S(2)}, u32[]{:S(2)}) %collective-permute-start.3) | collective-permute-done | bytes 131104 | tf_op jit(solution)/shard_map/ppermute | solution.py:369
  26.9 6.0 %collective-permute-start.4 = (bf16[4,128,128]{2,1,0:T(8,128)(2,1)S(1)}, bf16[4,128,128]{2,1,0:T(8,128)(2,1)S(1)}, u32[]{:S(2)}, u32[]{:S(2)}) collective-permute-start(bf16[4,128,128]{2,1,0:T(8,128)(2,1)S(1)} %add_convert_fusion), channel_id=1, source_target_pairs={{0,192},{32,224},{64,128},{96,160},{128,64},{160,96},{192,0},{224,... | collective-permute-start | bytes 393224 | tf_op jit(solution)/shard_map/ppermute | solution.py:369
  32.9 1.5 %collective-permute-start.14 = (bf16[256,512]{1,0:T(8,128)(2,1)S(1)}, bf16[256,512]{1,0:T(8,128)(2,1)S(1)}, u32[]{:S(2)}, u32[]{:S(2)}) collective-permute-start(bf16[256,512]{1,0:T(8,128)(2,1)S(1)} %slice.8), channel_id=1, source_target_pairs={{0,2},{2,4},{4,6},{6,0},{1,3},{3,5},{5,7},{7,1},{8,10},{10,12},{12... | collective-permute-start | bytes 786440 | tf_op jit(solution)/shard_map/ppermute | solution.py:380
  34.5 1.9 %collective-permute-start.16 = (bf16[256,512]{1,0:T(8,128)(2,1)S(1)}, bf16[256,512]{1,0:T(8,128)(2,1)S(1)}, u32[]{:S(2)}, u32[]{:S(2)}) collective-permute-start(bf16[256,512]{1,0:T(8,128)(2,1)S(1)} %slice.9), channel_id=1, source_target_pairs={{0,6},{2,0},{4,2},{6,4},{1,7},{3,1},{5,3},{7,5},{8,14},{10,8},{12,... | collective-permute-start | bytes 786440 | tf_op jit(solution)/shard_map/ppermute | solution.py:381
  36.4 1.4 %shard_map.101 = (bf16[512,4,128]{2,1,0:T(4,128)(2,1)S(1)}, bf16[512,4,128]{2,1,0:T(4,128)(2,1)S(1)}, bf16[512,4,128]{2,1,0:T(4,128)(2,1)S(1)}, f32[15,4,512]{2,1,0:T(4,128)S(1)}) custom-call(bf16[512,4,128]{2,1,0:T(4,128)(2,1)} %refs_0_.1, bf16[512,4,128]{2,1,0:T(4,128)(2,1)} %refs_1_.1, bf16[512,4,128]{2,1,0:T(4,128)(2,1)} %refs_2_.1, f32[15,4,512]{2,1,0:T(4,128)} %refs_3_.1), custom_call_target="tpu_custom_call" | custom-call | bytes 3391488 | tf_op jit(solution)/shard_map/pallas_call | solution.py:323
  37.8 2.3 %shard_map.102 = (f32[512,512]{1,0:T(8,128)S(1)}, bf16[4,640,512]{2,1,0:T(8,128)(2,1)S(1)}) custom-call(bf16[512,4,128]{2,1,0:T(4,128)(2,1)S(1)} %get-tuple-element.51.q_ref, bf16[512,4,128]{2,1,0:T(4,128)(2,1)S(1)} %get-tuple-element.52.k_ref, bf16[512,4,128]{2,1,0:T(4,128)(2,1)S(1)} %get-tuple-element.53.v_ref, f32[15,4,512]{2,1,0:T(4,128)S(1)} %get-tuple-element.54.lw_ref), custom_call_target="tpu_custom_call" | custom-call | flops 536870912 | bytes 5365760 | tf_op jit(solution)/shard_map/pallas_call | solution.py:323
  40.1 0.9 shard_map.103.a
  41.0 0.3 collective-permute-start.5
  41.3 1.8 %shard_map.108 = (f32[512,512]{1,0:T(8,128)S(1)}, f32[512,512]{1,0:T(8,128)S(1)}) custom-call(bf16[512,512]{1,0:T(8,128)(2,1)S(1)} %copy-done.1, bf16[512,512]{1,0:T(8,128)(2,1)S(1)} %collective-permute-done.13.gl, bf16[512,512]{1,0:T(8,128)(2,1)S(1)} %collective-permute-done.15.gr, bf16[512,4096]{1,0:T(8,128)(2,1)S(1)} %bitcast.2, ...), custom_call_target="tpu_custom_call" | custom-call | flops 1610612736 | bytes 12058624 | tf_op jit(solution)/shard_map/pallas_call | solution.py:323
  43.2 0.5 shard_map.110
  43.7 0.6 collective-permute-start.17
  44.2 0.7 shard_map.105
  44.9 0.6 collective-permute-start.7
  45.5 2.7 %collective-permute-start.8 = (bf16[256,512]{1,0:T(8,128)(2,1)S(1)}, bf16[256,512]{1,0:T(8,128)(2,1)S(1)}, u32[]{:S(2)}, u32[]{:S(2)}) collective-permute-start(bf16[256,512]{1,0:T(8,128)(2,1)S(1)} %get-tuple-element.61), channel_id=1, source_target_pairs={{0,6},{2,0},{4,2},{6,4},{1,7},{3,1},{5,3},{7,5},{8,14},{10,8},{12,... | collective-permute-start | bytes 786440 | tf_op jit(solution)/shard_map/ppermute | solution.py:440
  48.2 0.5 shard_map.109.own_ref
  48.7 0.9 %shard_map.111 = (bf16[512,512]{1,0:T(8,128)(2,1)S(1)}, bf16[5,128,128]{2,1,0:T(8,128)(2,1)S(1)}, bf16[5,128,128]{2,1,0:T(8,128)(2,1)S(1)}, bf16[5,128,128]{2,1,0:T(8,128)(2,1)S(1)}, bf16[5,128,128]{2,1,0:T(8,128)(2,1)S(1)}) custom-call(f32[512,512]{1,0:T(8,128)S(1)} %shard_map.109.own_ref, bf16[512,512]{1,0:T(8,128)(2,1)S(1)} %collective-permute-done.17.rec_ref, ...), custom_call_target="tpu_custom_call" | custom-call | flops 335544320 | bytes 5373952 | tf_op jit(solution)/shard_map/pallas_call | solution.py:323
  49.7 0.3 collective-permute-start.18
  50.0 4.1 %collective-permute-start.19 = (bf16[5,128,128]{2,1,0:T(8,128)(2,1)S(1)}, bf16[5,128,128]{2,1,0:T(8,128)(2,1)S(1)}, u32[]{:S(2)}, u32[]{:S(2)}) collective-permute-start(bf16[5,128,128]{2,1,0:T(8,128)(2,1)S(1)} %get-tuple-element.80), channel_id=1, source_target_pairs={{0,16},{8,24},{16,0},{24,8},{1,17},{9,25},{17,1},{25,9},{2,18},{10... | collective-permute-start | bytes 491528 | tf_op jit(solution)/shard_map/ppermute | solution.py:402
  54.1 0.4 collective-permute-start.20
  54.5 1.8 %shard_map.104 = (bf16[256,512]{1,0:T(8,128)(2,1)S(1)}, bf16[256,512]{1,0:T(8,128)(2,1)S(1)}, f32[256,512]{1,0:T(8,128)S(1)}, f32[256,512]{1,0:T(8,128)S(1)}, f32[512,512]{1,0:T(8,128)S(1)}) custom-call(bf16[512,512]{1,0:T(8,128)(2,1)S(1)} %shard_map.103.a, bf16[512,512]{1,0:T(8,128)(2,1)S(1)} %collective-permute-done.5.ap, bf16[512,4096]{1,0:T(8,128)(2,1)S(1)} %bitcast.5, ...), custom_call_target="tpu_custom_call" | custom-call | flops 1610612736 | bytes 12058624 | tf_op jit(solution)/shard_map/pallas_call | solution.py:323
  56.2 0.6 collective-permute-done.18.w1
  56.8 4.4 %collective-permute-done.19.w2 = bf16[5,128,128]{2,1,0:T(8,128)(2,1)S(1)} collective-permute-done((bf16[5,128,128]{2,1,0:T(8,128)(2,1)S(1)}, bf16[5,128,128]{2,1,0:T(8,128)(2,1)S(1)}, u32[]{:S(2)}, u32[]{:S(2)}) %collective-permute-start.19) | collective-permute-done | bytes 163872 | tf_op jit(solution)/shard_map/ppermute | solution.py:402
  61.2 0.3 collective-permute-start.11
  61.6 1.9 %collective-permute-done.20.w3 = bf16[5,128,128]{2,1,0:T(8,128)(2,1)S(1)} collective-permute-done((bf16[5,128,128]{2,1,0:T(8,128)(2,1)S(1)}, bf16[5,128,128]{2,1,0:T(8,128)(2,1)S(1)}, u32[]{:S(2)}, u32[]{:S(2)}) %collective-permute-start.20) | collective-permute-done | bytes 163872 | tf_op jit(solution)/shard_map/ppermute | solution.py:402
  63.5 0.1 shard_map.115
  63.7 0.1 shard_map.106
  63.9 3.2 %collective-permute-start.12 = (bf16[256,512]{1,0:T(8,128)(2,1)S(1)}, bf16[256,512]{1,0:T(8,128)(2,1)S(1)}, u32[]{:S(2)}, u32[]{:S(2)}) collective-permute-start(bf16[256,512]{1,0:T(8,128)(2,1)S(1)} %get-tuple-element.65), channel_id=1, source_target_pairs={{0,6},{2,0},{4,2},{6,4},{1,7},{3,1},{5,3},{7,5},{8,14},{10,8},{12,... | collective-permute-start | bytes 786440 | tf_op jit(solution)/shard_map/ppermute | solution.py:450
  67.2 1.2 %collective-permute-done.21.got_ref = bf16[3,128,128]{2,1,0:T(8,128)(2,1)S(1)} collective-permute-done((bf16[3,128,128]{2,1,0:T(8,128)(2,1)S(1)}, bf16[3,128,128]{2,1,0:T(8,128)(2,1)S(1)}, u32[]{:S(2)}, u32[]{:S(2)}) %collective-permute-start.21) | collective-permute-done | bytes 98336 | tf_op jit(solution)/shard_map/ppermute | solution.py:406
  68.3 1.7 %collective-permute-start.22 = (bf16[2,128,128]{2,1,0:T(8,128)(2,1)S(1)}, bf16[2,128,128]{2,1,0:T(8,128)(2,1)S(1)}, u32[]{:S(2)}, u32[]{:S(2)}) collective-permute-start(bf16[2,128,128]{2,1,0:T(8,128)(2,1)S(1)} %get-tuple-element.86), channel_id=1, source_target_pairs={{0,64},{32,96},{64,0},{96,32},{128,192},{160,224},{192,128},{224,1... | collective-permute-start | bytes 196616 | tf_op jit(solution)/shard_map/ppermute | solution.py:406
  70.0 3.9 %collective-permute-done.22.got_ref = bf16[2,128,128]{2,1,0:T(8,128)(2,1)S(1)} collective-permute-done((bf16[2,128,128]{2,1,0:T(8,128)(2,1)S(1)}, bf16[2,128,128]{2,1,0:T(8,128)(2,1)S(1)}, u32[]{:S(2)}, u32[]{:S(2)}) %collective-permute-start.22) | collective-permute-done | bytes 65568 | tf_op jit(solution)/shard_map/ppermute | solution.py:406
  73.9 2.9 %collective-permute-start.23 = (bf16[1,128,128]{2,1,0:T(8,128)(2,1)S(1)}, bf16[1,128,128]{2,1,0:T(8,128)(2,1)S(1)}, u32[]{:S(2)}, u32[]{:S(2)}) collective-permute-start(bf16[1,128,128]{2,1,0:T(8,128)(2,1)S(1)} %get-tuple-element.89), channel_id=1, source_target_pairs={{0,192},{32,224},{64,128},{96,160},{128,64},{160,96},{192,0},{224,... | collective-permute-start | bytes 98312 | tf_op jit(solution)/shard_map/ppermute | solution.py:406
  76.8 2.5 %shard_map.112 = (f32[512,256]{1,0:T(8,128)S(1)}, f32[512,256]{1,0:T(8,128)S(1)}, f32[512,256]{1,0:T(8,128)S(1)}, f32[2,10,512]{2,1,0:T(8,128)S(1)}) custom-call(bf16[512,4,128]{2,1,0:T(4,128)(2,1)S(1)} %get-tuple-element.51.q_ref, bf16[512,4,128]{2,1,0:T(4,128)(2,1)S(1)} %get-tuple-element.52.k_ref, bf16[512,4,128]{2,1,0:T(4,128)(2,1)S(1)} %get-tuple-element.53.v_ref, ...), custom_call_target="tpu_custom_call" | custom-call | flops 671088640 | bytes 3833856 | tf_op jit(solution)/shard_map/pallas_call | solution.py:323
  79.4 1.0 %collective-permute-done.23.got_ref = bf16[1,128,128]{2,1,0:T(8,128)(2,1)S(1)} collective-permute-done((bf16[1,128,128]{2,1,0:T(8,128)(2,1)S(1)}, bf16[1,128,128]{2,1,0:T(8,128)(2,1)S(1)}, u32[]{:S(2)}, u32[]{:S(2)}) %collective-permute-start.23) | collective-permute-done | bytes 32800 | tf_op jit(solution)/shard_map/ppermute | solution.py:406
  80.5 1.8 %collective-permute-start.25 = (bf16[128,128]{1,0:T(8,128)(2,1)S(1)}, bf16[128,128]{1,0:T(8,128)(2,1)S(1)}, u32[]{:S(2)}, u32[]{:S(2)}) collective-permute-start(bf16[128,128]{1,0:T(8,128)(2,1)S(1)} %get-tuple-element.92), channel_id=1, source_target_pairs={{0,16},{8,24},{16,0},{24,8},{1,17},{9,25},{17,1},{25,9},{2,18},{10... | collective-permute-start | bytes 98312 | tf_op jit(solution)/shard_map/ppermute | solution.py:402
  82.4 2.9 %collective-permute-start.26 = (bf16[128,128]{1,0:T(8,128)(2,1)S(1)}, bf16[128,128]{1,0:T(8,128)(2,1)S(1)}, u32[]{:S(2)}, u32[]{:S(2)}) collective-permute-start(bf16[128,128]{1,0:T(8,128)(2,1)S(1)} %get-tuple-element.93), channel_id=1, source_target_pairs={{0,24},{8,16},{16,8},{24,0},{1,25},{9,17},{17,9},{25,1},{2,26},{10... | collective-permute-start | bytes 98312 | tf_op jit(solution)/shard_map/ppermute | solution.py:402
  85.2 2.5 %shard_map.113 = (f32[512,256]{1,0:T(8,128)S(1)}, f32[512,256]{1,0:T(8,128)S(1)}, f32[512,256]{1,0:T(8,128)S(1)}, f32[2,10,512]{2,1,0:T(8,128)S(1)}) custom-call(bf16[512,4,128]{2,1,0:T(4,128)(2,1)S(1)} %get-tuple-element.51.q_ref, bf16[512,4,128]{2,1,0:T(4,128)(2,1)S(1)} %get-tuple-element.52.k_ref, bf16[512,4,128]{2,1,0:T(4,128)(2,1)S(1)} %get-tuple-element.53.v_ref, ...), custom_call_target="tpu_custom_call" | custom-call | flops 671088640 | bytes 3833856 | tf_op jit(solution)/shard_map/pallas_call | solution.py:323
  87.8 2.2 %shard_map.114 = (bf16[512,4,128]{2,1,0:T(4,128)(2,1)}, f32[15,4,512]{2,1,0:T(4,128)}) custom-call(bf16[512,4,128]{2,1,0:T(4,128)(2,1)S(1)} %get-tuple-element.51.q_ref, bf16[512,512]{1,0:T(8,128)(2,1)S(1)} %get-tuple-element.68.g_ref, f32[15,4,512]{2,1,0:T(4,128)S(1)} %get-tuple-element.54.lw_ref, f32[512,256]{1,0:T(8,128)S(1)} %get-tuple-element.69.dqa, ...), custom_call_target="tpu_custom_call" | custom-call | flops 335544320 | bytes 3604480 | tf_op jit(solution)/shard_map/pallas_call | solution.py:323
  90.0 1.0 %shard_map.107 = bf16[512,512]{1,0:T(8,128)(2,1)} custom-call(f32[512,512]{1,0:T(8,128)S(1)} %get-tuple-element.57.own, bf16[256,512]{1,0:T(8,128)(2,1)S(1)} %collective-permute-done.9.l_top, bf16[256,512]{1,0:T(8,128)(2,1)S(1)} %collective-permute-done.10.l_bot, bf16[256,512]{1,0:T(8,128)(2,1)S(1)} %collective-permute-done.11.r_top, ...), custom_call_target="tpu_custom_call" | custom-call | flops 1048576 | bytes 2621440 | tf_op jit(solution)/shard_map/pallas_call | solution.py:323
  90.9 1.4 %shard_map.119 = (bf16[512,4,128]{2,1,0:T(4,128)(2,1)}, bf16[512,4,128]{2,1,0:T(4,128)(2,1)}) custom-call(f32[512,256]{1,0:T(8,128)S(1)} %get-tuple-element.74.dka, f32[512,256]{1,0:T(8,128)S(1)} %get-tuple-element.75.dva, f32[512,256]{1,0:T(8,128)S(1)} %get-tuple-element.76.dkb, f32[512,256]{1,0:T(8,128)S(1)} %get-tuple-element.77.dvb, ...), custom_call_target="tpu_custom_call" | custom-call | flops 134217728 | bytes 4325376 | tf_op jit(solution)/shard_map/pallas_call | solution.py:323
  (36 shorter events, 0.7 us)
Async XLA Ops:
  0.6 40.6 %collective-permute-start.6 = (bf16[512,4096]{1,0:T(8,128)(2,1)}, bf16[512,4096]{1,0:T(8,128)(2,1)S(1)}, u32[]{:S(2)}, u32[]{:S(2)}) collective-permute-start(bf16[512,4096]{1,0:T(8,128)(2,1)} %bitcast.1), channel_id=1, source_target_pairs={{0,1},{1,0},{2,3},{3,2},{4,5},{5,4},{6,7},{7,6},{8,9},{9,8},{10,11... | collective-permute-start | bytes 12582920 | tf_op jit(solution)/shard_map/ppermute | solution.py:351
  2.3 6.0 %collective-permute-start = (bf16[4,128,128]{2,1,0:T(8,128)(2,1)S(1)}, bf16[4,128,128]{2,1,0:T(8,128)(2,1)S(1)}, u32[]{:S(2)}, u32[]{:S(2)}) collective-permute-start(bf16[4,128,128]{2,1,0:T(8,128)(2,1)S(1)} %get-tuple-element.97), channel_id=1, source_target_pairs={{0,8},{8,0},{16,24},{24,16},{1,9},{9,1},{17,25},{25,17},{2,10},{10... | collective-permute-start | bytes 393224 | tf_op jit(solution)/shard_map/ppermute | solution.py:369
  8.3 6.4 %collective-permute-start.1 = (bf16[4,128,128]{2,1,0:T(8,128)(2,1)S(1)}, bf16[4,128,128]{2,1,0:T(8,128)(2,1)S(1)}, u32[]{:S(2)}, u32[]{:S(2)}) collective-permute-start(bf16[4,128,128]{2,1,0:T(8,128)(2,1)S(1)} %fusion.3), channel_id=1, source_target_pairs={{0,24},{8,16},{16,8},{24,0},{1,25},{9,17},{17,9},{25,1},{2,26},{10... | collective-permute-start | bytes 393224 | tf_op jit(solution)/shard_map/ppermute | solution.py:369
  14.8 5.1 %collective-permute-start.2 = (bf16[4,128,128]{2,1,0:T(8,128)(2,1)S(1)}, bf16[4,128,128]{2,1,0:T(8,128)(2,1)S(1)}, u32[]{:S(2)}, u32[]{:S(2)}) collective-permute-start(bf16[4,128,128]{2,1,0:T(8,128)(2,1)S(1)} %fusion.5), channel_id=1, source_target_pairs={{0,32},{32,0},{64,96},{96,64},{128,160},{160,128},{192,224},{224,1... | collective-permute-start | bytes 393224 | tf_op jit(solution)/shard_map/ppermute | solution.py:369
  16.6 16.3 %collective-permute-start.13 = (bf16[512,512]{1,0:T(8,128)(2,1)}, bf16[512,512]{1,0:T(8,128)(2,1)S(1)}, u32[]{:S(2)}, u32[]{:S(2)}) collective-permute-start(bf16[512,512]{1,0:T(8,128)(2,1)} %go.1), channel_id=1, source_target_pairs={{0,2},{2,4},{4,6},{6,0},{1,3},{3,5},{5,7},{7,1},{8,10},{10,12},{12... | collective-permute-start | bytes 1572872 | tf_op jit(solution)/shard_map/ppermute | solution.py:349
  16.6 17.8 %collective-permute-start.15 = (bf16[512,512]{1,0:T(8,128)(2,1)}, bf16[512,512]{1,0:T(8,128)(2,1)S(1)}, u32[]{:S(2)}, u32[]{:S(2)}) collective-permute-start(bf16[512,512]{1,0:T(8,128)(2,1)} %go.1), channel_id=1, source_target_pairs={{0,6},{2,0},{4,2},{6,4},{1,7},{3,1},{5,3},{7,5},{8,14},{10,8},{12,... | collective-permute-start | bytes 1572872 | tf_op jit(solution)/shard_map/ppermute | solution.py:350
  19.9 7.0 %collective-permute-start.3 = (bf16[4,128,128]{2,1,0:T(8,128)(2,1)S(1)}, bf16[4,128,128]{2,1,0:T(8,128)(2,1)S(1)}, u32[]{:S(2)}, u32[]{:S(2)}) collective-permute-start(bf16[4,128,128]{2,1,0:T(8,128)(2,1)S(1)} %fusion.4), channel_id=1, source_target_pairs={{0,64},{32,96},{64,0},{96,32},{128,192},{160,224},{192,128},{224,1... | collective-permute-start | bytes 393224 | tf_op jit(solution)/shard_map/ppermute | solution.py:369
  26.9 13.2 %collective-permute-start.4 = (bf16[4,128,128]{2,1,0:T(8,128)(2,1)S(1)}, bf16[4,128,128]{2,1,0:T(8,128)(2,1)S(1)}, u32[]{:S(2)}, u32[]{:S(2)}) collective-permute-start(bf16[4,128,128]{2,1,0:T(8,128)(2,1)S(1)} %add_convert_fusion), channel_id=1, source_target_pairs={{0,192},{32,224},{64,128},{96,160},{128,64},{160,96},{192,0},{224,... | collective-permute-start | bytes 393224 | tf_op jit(solution)/shard_map/ppermute | solution.py:369
  32.9 10.2 %collective-permute-start.14 = (bf16[256,512]{1,0:T(8,128)(2,1)S(1)}, bf16[256,512]{1,0:T(8,128)(2,1)S(1)}, u32[]{:S(2)}, u32[]{:S(2)}) collective-permute-start(bf16[256,512]{1,0:T(8,128)(2,1)S(1)} %slice.8), channel_id=1, source_target_pairs={{0,2},{2,4},{4,6},{6,0},{1,3},{3,5},{5,7},{7,1},{8,10},{10,12},{12... | collective-permute-start | bytes 786440 | tf_op jit(solution)/shard_map/ppermute | solution.py:380
  34.4 6.9 %copy-start = (bf16[4,128,4096]{2,1,0:T(8,128)(2,1)S(1)}, bf16[4,128,4096]{2,1,0:T(8,128)(2,1)}, u32[]{:S(2)}) copy-start(bf16[4,128,4096]{2,1,0:T(8,128)(2,1)} %param.10) | copy-start | bytes 12582916
  34.4 6.9 %copy-start.1 = (bf16[512,512]{1,0:T(8,128)(2,1)S(1)}, bf16[512,512]{1,0:T(8,128)(2,1)}, u32[]{:S(2)}) copy-start(bf16[512,512]{1,0:T(8,128)(2,1)} %go.1) | copy-start | bytes 1572868
  34.5 8.7 %collective-permute-start.16 = (bf16[256,512]{1,0:T(8,128)(2,1)S(1)}, bf16[256,512]{1,0:T(8,128)(2,1)S(1)}, u32[]{:S(2)}, u32[]{:S(2)}) collective-permute-start(bf16[256,512]{1,0:T(8,128)(2,1)S(1)} %slice.9), channel_id=1, source_target_pairs={{0,6},{2,0},{4,2},{6,4},{1,7},{3,1},{5,3},{7,5},{8,14},{10,8},{12,... | collective-permute-start | bytes 786440 | tf_op jit(solution)/shard_map/ppermute | solution.py:381
  41.0 3.2 %collective-permute-start.5 = (bf16[512,512]{1,0:T(8,128)(2,1)S(1)}, bf16[512,512]{1,0:T(8,128)(2,1)S(1)}, u32[]{:S(2)}, u32[]{:S(2)}) collective-permute-start(bf16[512,512]{1,0:T(8,128)(2,1)S(1)} %shard_map.103.a), channel_id=1, source_target_pairs={{0,1},{1,0},{2,3},{3,2},{4,5},{5,4},{6,7},{7,6},{8,9},{9,8},{10,11... | collective-permute-start | bytes 1572872 | tf_op jit(solution)/shard_map/ppermute | solution.py:433
  43.7 5.1 %collective-permute-start.17 = (bf16[512,512]{1,0:T(8,128)(2,1)S(1)}, bf16[512,512]{1,0:T(8,128)(2,1)S(1)}, u32[]{:S(2)}, u32[]{:S(2)}) collective-permute-start(bf16[512,512]{1,0:T(8,128)(2,1)S(1)} %shard_map.110), channel_id=1, source_target_pairs={{0,1},{1,0},{2,3},{3,2},{4,5},{5,4},{6,7},{7,6},{8,9},{9,8},{10,11... | collective-permute-start | bytes 1572872 | tf_op jit(solution)/shard_map/ppermute | solution.py:389
  44.9 18.8 %collective-permute-start.7 = (bf16[256,512]{1,0:T(8,128)(2,1)S(1)}, bf16[256,512]{1,0:T(8,128)(2,1)S(1)}, u32[]{:S(2)}, u32[]{:S(2)}) collective-permute-start(bf16[256,512]{1,0:T(8,128)(2,1)S(1)} %get-tuple-element.60), channel_id=1, source_target_pairs={{0,2},{2,4},{4,6},{6,0},{1,3},{3,5},{5,7},{7,1},{8,10},{10,12},{12... | collective-permute-start | bytes 786440 | tf_op jit(solution)/shard_map/ppermute | solution.py:439
  45.5 18.2 %collective-permute-start.8 = (bf16[256,512]{1,0:T(8,128)(2,1)S(1)}, bf16[256,512]{1,0:T(8,128)(2,1)S(1)}, u32[]{:S(2)}, u32[]{:S(2)}) collective-permute-start(bf16[256,512]{1,0:T(8,128)(2,1)S(1)} %get-tuple-element.61), channel_id=1, source_target_pairs={{0,6},{2,0},{4,2},{6,4},{1,7},{3,1},{5,3},{7,5},{8,14},{10,8},{12,... | collective-permute-start | bytes 786440 | tf_op jit(solution)/shard_map/ppermute | solution.py:440
  49.7 7.2 %collective-permute-start.18 = (bf16[5,128,128]{2,1,0:T(8,128)(2,1)S(1)}, bf16[5,128,128]{2,1,0:T(8,128)(2,1)S(1)}, u32[]{:S(2)}, u32[]{:S(2)}) collective-permute-start(bf16[5,128,128]{2,1,0:T(8,128)(2,1)S(1)} %get-tuple-element.79), channel_id=1, source_target_pairs={{0,8},{8,0},{16,24},{24,16},{1,9},{9,1},{17,25},{25,17},{2,10},{10... | collective-permute-start | bytes 491528 | tf_op jit(solution)/shard_map/ppermute | solution.py:402
  50.0 11.3 %collective-permute-start.19 = (bf16[5,128,128]{2,1,0:T(8,128)(2,1)S(1)}, bf16[5,128,128]{2,1,0:T(8,128)(2,1)S(1)}, u32[]{:S(2)}, u32[]{:S(2)}) collective-permute-start(bf16[5,128,128]{2,1,0:T(8,128)(2,1)S(1)} %get-tuple-element.80), channel_id=1, source_target_pairs={{0,16},{8,24},{16,0},{24,8},{1,17},{9,25},{17,1},{25,9},{2,18},{10... | collective-permute-start | bytes 491528 | tf_op jit(solution)/shard_map/ppermute | solution.py:402
  54.1 9.4 %collective-permute-start.20 = (bf16[5,128,128]{2,1,0:T(8,128)(2,1)S(1)}, bf16[5,128,128]{2,1,0:T(8,128)(2,1)S(1)}, u32[]{:S(2)}, u32[]{:S(2)}) collective-permute-start(bf16[5,128,128]{2,1,0:T(8,128)(2,1)S(1)} %get-tuple-element.81), channel_id=1, source_target_pairs={{0,24},{8,16},{16,8},{24,0},{1,25},{9,17},{17,9},{25,1},{2,26},{10... | collective-permute-start | bytes 491528 | tf_op jit(solution)/shard_map/ppermute | solution.py:402
  56.8 23.7 %collective-permute-start.10 = (bf16[256,512]{1,0:T(8,128)(2,1)S(1)}, bf16[256,512]{1,0:T(8,128)(2,1)S(1)}, u32[]{:S(2)}, u32[]{:S(2)}) collective-permute-start(bf16[256,512]{1,0:T(8,128)(2,1)S(1)} %get-tuple-element.63), channel_id=1, source_target_pairs={{0,2},{2,4},{4,6},{6,0},{1,3},{3,5},{5,7},{7,1},{8,10},{10,12},{12... | collective-permute-start | bytes 786440 | tf_op jit(solution)/shard_map/ppermute | solution.py:444
  61.2 21.1 %collective-permute-start.11 = (bf16[256,512]{1,0:T(8,128)(2,1)S(1)}, bf16[256,512]{1,0:T(8,128)(2,1)S(1)}, u32[]{:S(2)}, u32[]{:S(2)}) collective-permute-start(bf16[256,512]{1,0:T(8,128)(2,1)S(1)} %get-tuple-element.64), channel_id=1, source_target_pairs={{0,6},{2,0},{4,2},{6,4},{1,7},{3,1},{5,3},{7,5},{8,14},{10,8},{12,... | collective-permute-start | bytes 786440 | tf_op jit(solution)/shard_map/ppermute | solution.py:445
  63.6 4.7 %collective-permute-start.21 = (bf16[3,128,128]{2,1,0:T(8,128)(2,1)S(1)}, bf16[3,128,128]{2,1,0:T(8,128)(2,1)S(1)}, u32[]{:S(2)}, u32[]{:S(2)}) collective-permute-start(bf16[3,128,128]{2,1,0:T(8,128)(2,1)S(1)} %get-tuple-element.83), channel_id=1, source_target_pairs={{0,32},{32,0},{64,96},{96,64},{128,160},{160,128},{192,224},{224,1... | collective-permute-start | bytes 294920 | tf_op jit(solution)/shard_map/ppermute | solution.py:406
  63.8 26.1 %collective-permute-start.9 = (bf16[256,512]{1,0:T(8,128)(2,1)S(1)}, bf16[256,512]{1,0:T(8,128)(2,1)S(1)}, u32[]{:S(2)}, u32[]{:S(2)}) collective-permute-start(bf16[256,512]{1,0:T(8,128)(2,1)S(1)} %get-tuple-element.62), channel_id=1, source_target_pairs={{0,2},{2,4},{4,6},{6,0},{1,3},{3,5},{5,7},{7,1},{8,10},{10,12},{12... | collective-permute-start | bytes 786440 | tf_op jit(solution)/shard_map/ppermute | solution.py:449
  63.9 26.0 %collective-permute-start.12 = (bf16[256,512]{1,0:T(8,128)(2,1)S(1)}, bf16[256,512]{1,0:T(8,128)(2,1)S(1)}, u32[]{:S(2)}, u32[]{:S(2)}) collective-permute-start(bf16[256,512]{1,0:T(8,128)(2,1)S(1)} %get-tuple-element.65), channel_id=1, source_target_pairs={{0,6},{2,0},{4,2},{6,4},{1,7},{3,1},{5,3},{7,5},{8,14},{10,8},{12,... | collective-permute-start | bytes 786440 | tf_op jit(solution)/shard_map/ppermute | solution.py:450
  68.3 5.6 %collective-permute-start.22 = (bf16[2,128,128]{2,1,0:T(8,128)(2,1)S(1)}, bf16[2,128,128]{2,1,0:T(8,128)(2,1)S(1)}, u32[]{:S(2)}, u32[]{:S(2)}) collective-permute-start(bf16[2,128,128]{2,1,0:T(8,128)(2,1)S(1)} %get-tuple-element.86), channel_id=1, source_target_pairs={{0,64},{32,96},{64,0},{96,32},{128,192},{160,224},{192,128},{224,1... | collective-permute-start | bytes 196616 | tf_op jit(solution)/shard_map/ppermute | solution.py:406
  73.9 6.5 %collective-permute-start.23 = (bf16[1,128,128]{2,1,0:T(8,128)(2,1)S(1)}, bf16[1,128,128]{2,1,0:T(8,128)(2,1)S(1)}, u32[]{:S(2)}, u32[]{:S(2)}) collective-permute-start(bf16[1,128,128]{2,1,0:T(8,128)(2,1)S(1)} %get-tuple-element.89), channel_id=1, source_target_pairs={{0,192},{32,224},{64,128},{96,160},{128,64},{160,96},{192,0},{224,... | collective-permute-start | bytes 98312 | tf_op jit(solution)/shard_map/ppermute | solution.py:406
  80.4 10.5 %collective-permute-start.24 = (bf16[128,128]{1,0:T(8,128)(2,1)S(1)}, bf16[128,128]{1,0:T(8,128)(2,1)S(1)}, u32[]{:S(2)}, u32[]{:S(2)}) collective-permute-start(bf16[128,128]{1,0:T(8,128)(2,1)S(1)} %get-tuple-element.91), channel_id=1, source_target_pairs={{0,8},{8,0},{16,24},{24,16},{1,9},{9,1},{17,25},{25,17},{2,10},{10... | collective-permute-start | bytes 98312 | tf_op jit(solution)/shard_map/ppermute | solution.py:402
  80.5 10.4 %collective-permute-start.25 = (bf16[128,128]{1,0:T(8,128)(2,1)S(1)}, bf16[128,128]{1,0:T(8,128)(2,1)S(1)}, u32[]{:S(2)}, u32[]{:S(2)}) collective-permute-start(bf16[128,128]{1,0:T(8,128)(2,1)S(1)} %get-tuple-element.92), channel_id=1, source_target_pairs={{0,16},{8,24},{16,0},{24,8},{1,17},{9,25},{17,1},{25,9},{2,18},{10... | collective-permute-start | bytes 98312 | tf_op jit(solution)/shard_map/ppermute | solution.py:402
  82.4 8.6 %collective-permute-start.26 = (bf16[128,128]{1,0:T(8,128)(2,1)S(1)}, bf16[128,128]{1,0:T(8,128)(2,1)S(1)}, u32[]{:S(2)}, u32[]{:S(2)}) collective-permute-start(bf16[128,128]{1,0:T(8,128)(2,1)S(1)} %get-tuple-element.93), channel_id=1, source_target_pairs={{0,24},{8,16},{16,8},{24,0},{1,25},{9,17},{17,9},{25,1},{2,26},{10... | collective-permute-start | bytes 98312 | tf_op jit(solution)/shard_map/ppermute | solution.py:402
